TPU v7x, 256 devices: a whole 4x4x8 slice. The times are simulated.
256 devices in a mesh: occ: 64 (over x_hi, y, z), off: 4 (over x_lo, core).
Axes of the slice: x: 4 (x_hi: 2, x_lo: 2; x = x_hi * 2 + x_lo), y: 4, z: 8, core: 2. Of those that a mesh axis runs over, the one named last changes fastest.
Arguments:
- factors: bfloat16 [64, 768, 2048], P('occ'), may hold values from -0.8984375 to 0.8984375
- occ_level: int32 [64], replicated, may hold values from 0 to 255
- vir_level: int32 [768], replicated, may hold values from 0 to 255
- occupied_energy_levels: float32 [256], replicated, may hold values from -2 to -0.5
- vir_table: float32 [256], replicated, may hold values from 0.5 to 4
- virtual_coefficient_matrix: bfloat16 [768, 1024], replicated, may hold values from -0.21875 to 0.21875
Outputs:
- density_ao: float32 [64, 2048, 1024], P(None, ('occ', 'off'))
Inputs may be any that keep to these rules, and one draw needn't show every extreme that they name: `occ_level`: indices into occupied_energy_levels. `vir_level`: indices into vir_table.
All inputs are finite; a program needn't handle non-finite values.
Results may differ from a plain program's by a relative error of at most 0.0032.
Values may be sent and summed in bfloat16 or wider, within the bound.
No kernel may reach another device: no remote copies, remote signals or barrier semaphores. Data moves between devices by JAX's collectives and lax.ppermute only.
A program may use at most 64 MiB of HBM per device.

v0:
```python
import jax
import jax.numpy as jnp
from jax import lax
from jax.sharding import PartitionSpec as P

PAIR_STEPS = 2


def passed_along(value, axis, by):
    length = lax.axis_size(axis)
    return lax.ppermute(value, axis, [(i, (i + by) % length) for i in range(length)])


def lookup(level, table):
    hits = level[:, None] == jnp.arange(table.shape[0], dtype=jnp.int32)[None, :]
    return jnp.sum(jnp.where(hits, table[None, :], jnp.float32(0.0)), axis=1)


def body(
    factors, occ_level, vir_level, occupied_energy_levels, vir_table, virtual_coefficient_matrix
):
    off_count = lax.axis_size("off")
    off_index = lax.axis_index("off")
    occ_count = lax.axis_size("occ")
    occ_index = lax.axis_index("occ")
    vir_energy = lookup(vir_level, vir_table)
    occ_energy = lookup(occ_level, occupied_energy_levels)
    own_energy = lax.dynamic_index_in_dim(occ_energy, occ_index, 0, keepdims=False)
    own = factors[0]
    carried = factors
    moved = factors
    for stride in range(1, off_count):
        moved = passed_along(moved, "occ", 1)
        carried = jnp.where(off_index == stride, moved, carried)
    gamma = jnp.zeros((own.shape[1], own.shape[0]), jnp.float32)
    for step_index in range(PAIR_STEPS):
        offset = off_index + off_count * step_index
        pair_companion = (occ_index - offset) % occ_count
        other_energy = lax.dynamic_index_in_dim(occ_energy, pair_companion, 0, keepdims=False)
        other = carried[0]
        if step_index < PAIR_STEPS - 1:
            carried = passed_along(carried, "occ", off_count)
        integral = lax.dot_general(
            own, other, (((1,), (1,)), ((), ())), preferred_element_type=jnp.float32
        )
        denom = vir_energy[:, None] + vir_energy[None, :] - own_energy - other_energy
        amp = integral / denom
        pair_weight = (2.0 * amp - amp.T).astype(jnp.bfloat16)
        gamma = gamma + lax.dot_general(
            other, pair_weight, (((0,), (1,)), ((), ())), preferred_element_type=jnp.float32
        )
    naux_rows = gamma.shape[0]
    per_device = naux_rows // (occ_count * off_count)
    blocks = gamma.reshape(occ_count, off_count, per_device, gamma.shape[1])
    total = lax.psum(blocks, "off")
    mine = lax.dynamic_slice_in_dim(total, off_index, 1, 1)
    lower_gamma_part = mine.reshape(occ_count, per_device, gamma.shape[1]).astype(jnp.bfloat16)
    finished_flag = jnp.einsum(
        "sbd,dw->sbw",
        lower_gamma_part,
        virtual_coefficient_matrix,
        preferred_element_type=jnp.float32,
    )
    moved_back = lax.all_to_all(finished_flag[None], "occ", split_axis=1, concat_axis=0, tiled=True)
    return moved_back.reshape(moved_back.shape[0], per_device, virtual_coefficient_matrix.shape[1])


def solution(mesh):
    in_specs = (P("occ", None, None), P(), P(), P(), P(), P())
    out_specs = P(None, ("occ", "off"), None)
    return jax.shard_map(body, mesh=mesh, in_specs=in_specs, out_specs=out_specs, check_vma=False)
```

profile of v0, /device:TPU:56, one launch (start us, length us, event | category | flops | bytes accessed | tf_op | source)
XLA Modules:
  0.0 574.3 jit_solution(9931685049981466083)
XLA Ops:
  0.0 0.0 copy-start
  0.0 1.9 collective-permute-start
  1.9 68.1 %collective-permute-done = bf16[1,768,2048]{2,1,0:T(8,128)(2,1)S(1)} collective-permute-done((bf16[1,768,2048]{2,1,0:T(8,128)(2,1)}, bf16[1,768,2048]{2,1,0:T(8,128)(2,1)S(1)}, u32[]{:S(2)}, u32[]{:S(2)}) %collective-permute-start) | collective-permute-done | bytes 3145760 | tf_op jit(solution)/shard_map/ppermute | solution.py:11
  70.1 1.6 copy-done.1
  71.7 1.9 collective-permute-start.1
  73.6 70.1 %collective-permute-done.1 = bf16[1,768,2048]{2,1,0:T(8,128)(2,1)} collective-permute-done((bf16[1,768,2048]{2,1,0:T(8,128)(2,1)S(1)}, bf16[1,768,2048]{2,1,0:T(8,128)(2,1)}, u32[]{:S(2)}, u32[]{:S(2)}) %collective-permute-start.1) | collective-permute-done | bytes 3145760 | tf_op jit(solution)/shard_map/ppermute | solution.py:11
  143.7 0.0 collective-permute-start.2
  143.7 0.0 copy-start.5
  143.7 70.8 %collective-permute-done.2 = bf16[1,768,2048]{2,1,0:T(8,128)(2,1)} collective-permute-done((bf16[1,768,2048]{2,1,0:T(8,128)(2,1)}, bf16[1,768,2048]{2,1,0:T(8,128)(2,1)}, u32[]{:S(2)}, u32[]{:S(2)}) %collective-permute-start.2) | collective-permute-done | bytes 3145760 | tf_op jit(solution)/shard_map/ppermute | solution.py:11
  214.5 4.1 select_select_fusion
  218.6 2.6 collective-permute-start.3
  221.3 0.0 copy-done.6
  221.3 0.0 copy-done.7
  221.3 0.2 select_reduce_fusion.1
  221.5 0.7 fusion.33
  222.1 0.0 copy-done.4
  222.1 0.0 copy-done.5
  222.1 0.3 select_reduce_fusion
  222.4 6.9 %fusion.5 = f32[768,768]{1,0:T(8,128)} fusion(bf16[1,768,2048]{2,1,0:T(8,128)(2,1)} %param.6, bf16[1,768,2048]{2,1,0:T(8,128)(2,1)} %select_select_fusion), kind=kOutput, calls=%fused_computation.6 | convolution fusion | flops 2415919104 | bytes 8650752 | tf_op jit(solution)/shard_map/dot_general | solution.py:43
  229.3 3.1 copy.14
  232.5 126.0 %collective-permute-done.3 = bf16[1,768,2048]{2,1,0:T(8,128)(2,1)} collective-permute-done((bf16[1,768,2048]{2,1,0:T(8,128)(2,1)}, bf16[1,768,2048]{2,1,0:T(8,128)(2,1)}, u32[]{:S(2)}, u32[]{:S(2)}) %collective-permute-start.3) | collective-permute-done | bytes 3145760 | tf_op jit(solution)/shard_map/ppermute | solution.py:11
  358.4 7.0 %fusion.2 = f32[768,768]{1,0:T(8,128)} fusion(bf16[1,768,2048]{2,1,0:T(8,128)(2,1)} %collective-permute-done.3, bf16[1,768,2048]{2,1,0:T(8,128)(2,1)} %param.6), kind=kOutput, calls=%fused_computation.3 | convolution fusion | flops 2415919104 | bytes 8650752 | tf_op jit(solution)/shard_map/dot_general | solution.py:43
  365.4 3.1 copy.15
  368.5 8.3 %fusion = f32[2048,768]{1,0:T(8,128)S(1)} fusion(bf16[1,768,2048]{2,1,0:T(8,128)(2,1)} %collective-permute-done.3, f32[768,768]{0,1:T(8,128)} %copy.15, f32[768,768]{1,0:T(8,128)} %fusion.2, f32[]{:T(128)} %bitcast.7, f32[]{:T(128)} %bitcast.3, f32[768]{0:T(1024)S(1)} %select_reduce_fusion), kind=kOutput, calls=%fused_computation.1 | convolution fusion | flops 2420637696 | bytes 14158856 | tf_op jit(solution)/shard_map/dot_general | solution.py:49
  376.8 0.0 copy-done.2
  376.8 0.0 copy-done.3
  376.8 6.7 %convolution_add_fusion = f32[2048,768]{1,0:T(8,128)S(1)} fusion(f32[2048,768]{1,0:T(8,128)S(1)} %fusion, bf16[1,768,2048]{2,1,0:T(8,128)(2,1)} %select_select_fusion, f32[768,768]{0,1:T(8,128)S(1)} %copy-done.3, f32[768,768]{1,0:T(8,128)S(1)} %copy-done.2, f32[]{:T(128)} %bitcast.4, f32[]{:T(128)} %bitcast.3, f32[768]{0:T(1024)S(1)} %select_reduce_fusion), kind=kOutput, calls=%fused_computation | convolution fusion | flops 2422210560 | bytes 20450312 | tf_op jit(solution)/shard_map/dot_general | solution.py:49
  383.5 3.2 copy.16
  386.7 111.8 %all-reduce.1 = bf16[64,4,8,768]{3,2,0,1:T(8,128)(2,1)} all-reduce(f32[64,4,8,768]{3,2,0,1:T(8,128)} %copy.16), channel_id=1, replica_groups=mesh['occ'=64,'off'=4] {'off'}, use_global_device_ids=true, to_apply=%region_2.3 | all-reduce | flops 1572864 | bytes 9437184 | tf_op jit(solution)/shard_map/psum | solution.py:55
  498.6 2.1 convolution_bitcast_fusion
  500.7 72.3 %all_to_all.4 = f32[1,64,8,1024]{3,2,0,1:T(8,128)S(1)} all-to-all(f32[1,64,8,1024]{3,2,0,1:T(8,128)S(1)} %convolution_bitcast_fusion), channel_id=1, replica_groups=mesh['occ'=64,'off'=4] {'occ'}, dimensions={1} | all-to-all | bytes 4194304 | tf_op jit(solution)/shard_map/all_to_all | solution.py:64
  572.9 1.3 copy.21
  (7 shorter events, 0.0 us)
Async XLA Ops:
  0.0 498.6 %copy-start = (bf16[768,1024]{1,0:T(8,128)(2,1)S(1)}, bf16[768,1024]{1,0:T(8,128)(2,1)}, u32[]{:S(2)}) copy-start(bf16[768,1024]{1,0:T(8,128)(2,1)} %param.11) | copy-start | bytes 4718596
  0.0 70.1 %collective-permute-start = (bf16[1,768,2048]{2,1,0:T(8,128)(2,1)}, bf16[1,768,2048]{2,1,0:T(8,128)(2,1)S(1)}, u32[]{:S(2)}, u32[]{:S(2)}) collective-permute-start(bf16[1,768,2048]{2,1,0:T(8,128)(2,1)} %param.6), channel_id=1, source_target_pairs={{0,4},{4,8},{8,12},{12,16},{16,20},{20,24},{24,28},{28,32},{32,36}... | collective-permute-start | bytes 9437192 | tf_op jit(solution)/shard_map/ppermute | solution.py:11
  70.1 1.6 copy-start.1
  71.7 72.0 %collective-permute-start.1 = (bf16[1,768,2048]{2,1,0:T(8,128)(2,1)S(1)}, bf16[1,768,2048]{2,1,0:T(8,128)(2,1)}, u32[]{:S(2)}, u32[]{:S(2)}) collective-permute-start(bf16[1,768,2048]{2,1,0:T(8,128)(2,1)S(1)} %collective-permute-done), channel_id=1, source_target_pairs={{0,4},{4,8},{8,12},{12,16},{16,20},{20,24},{24,28},{28,32},{32,36}... | collective-permute-start | bytes 9437192 | tf_op jit(solution)/shard_map/ppermute | solution.py:11
  143.7 70.8 %collective-permute-start.2 = (bf16[1,768,2048]{2,1,0:T(8,128)(2,1)}, bf16[1,768,2048]{2,1,0:T(8,128)(2,1)}, u32[]{:S(2)}, u32[]{:S(2)}) collective-permute-start(bf16[1,768,2048]{2,1,0:T(8,128)(2,1)} %collective-permute-done.1), channel_id=1, source_target_pairs={{0,4},{4,8},{8,12},{12,16},{16,20},{20,24},{24,28},{28,32},{32,36}... | collective-permute-start | bytes 9437192 | tf_op jit(solution)/shard_map/ppermute | solution.py:11
  143.7 77.6 %copy-start.6 = (f32[256]{0:T(256)S(1)}, f32[256]{0:T(256)}, u32[]{:S(2)}) copy-start(f32[256]{0:T(256)} %param.9) | copy-start | bytes 3076
  143.7 77.6 %copy-start.7 = (s32[64]{0:T(128)S(1)}, s32[64]{0:T(128)}, u32[]{:S(2)}) copy-start(s32[64]{0:T(128)} %param.7) | copy-start | bytes 772
  143.7 78.4 %copy-start.4 = (s32[768]{0:T(1024)S(1)}, s32[768]{0:T(1024)}, u32[]{:S(2)}) copy-start(s32[768]{0:T(1024)} %param.8) | copy-start | bytes 9220
  143.7 78.4 %copy-start.5 = (f32[256]{0:T(256)S(1)}, f32[256]{0:T(256)}, u32[]{:S(2)}) copy-start(f32[256]{0:T(256)} %param.10) | copy-start | bytes 3076
  218.6 139.8 %collective-permute-start.3 = (bf16[1,768,2048]{2,1,0:T(8,128)(2,1)}, bf16[1,768,2048]{2,1,0:T(8,128)(2,1)}, u32[]{:S(2)}, u32[]{:S(2)}) collective-permute-start(bf16[1,768,2048]{2,1,0:T(8,128)(2,1)} %select_select_fusion), channel_id=1, source_target_pairs={{0,16},{4,20},{8,24},{12,28},{16,32},{20,36},{24,40},{28,44},{32,4... | collective-permute-start | bytes 9437192 | tf_op jit(solution)/shard_map/ppermute | solution.py:11
  368.5 8.3 %copy-start.2 = (f32[768,768]{1,0:T(8,128)S(1)}, f32[768,768]{1,0:T(8,128)}, u32[]{:S(2)}) copy-start(f32[768,768]{1,0:T(8,128)} %fusion.5) | copy-start | bytes 7077892
  368.5 8.3 %copy-start.3 = (f32[768,768]{0,1:T(8,128)S(1)}, f32[768,768]{0,1:T(8,128)}, u32[]{:S(2)}) copy-start(f32[768,768]{0,1:T(8,128)} %copy.14) | copy-start | bytes 7077892
where the time goes:
time: 575 us; the launch traced here: 574 us
  waiting for transfers between devices  335 us (58%)
  blocking collectives  184 us (32%)
  matrix products  31 us (5%)
  local copies, waits for them, and re-layouts  13.1 us (2%)
  starting transfers between devices  6.48 us (1%)
    ppermute x4, waiting for transfers between devices, passed_along(): lax.ppermute(value, axis, [(i, (i + by) % length) for i in range(length)])  335 us
    psum x1, blocking collectives, body(): total = lax.psum(blocks, 'off')  112 us
    all_to_all x1, blocking collectives, body(): lax.all_to_all(finished_flag[None], 'occ', split_axis=1, concat_axis=0, t...  72.3 us
    dot_general x2, matrix products, body(): lax.dot_general(other, pair_weight, (((0,), (1,)), ((), ())), preferred_e...  15 us
    dot_general x2, matrix products, body(): lax.dot_general(own, other, (((1,), (1,)), ((), ())), preferred_element_t...  13.9 us
  transfers between devices with their start and end apart: 4, of which 4 were waited for; matrix products, arithmetic and copies ran while one was open for 2% of the time, Pallas kernels for 0%

commit v1 on v0

v1 whole, which is shorter than its diff:
```python
import jax
import jax.numpy as jnp
from jax import lax
from jax.sharding import PartitionSpec as P

BOTH = ("occ", "off")


def lookup(level, table):
    hits = level[:, None] == jnp.arange(table.shape[0], dtype=jnp.int32)[None, :]
    return jnp.sum(jnp.where(hits, table[None, :], jnp.float32(0.0)), axis=1)


def moves(n_occ, rule):
    pairs = []
    for i in range(n_occ):
        for chip in range(2):
            for core in range(2):
                shift, to = rule(core)
                pairs.append((i * 4 + chip * 2 + core, ((i + shift) % n_occ) * 4 + chip * 2 + to))
    return pairs


def swap(n_occ, mask):
    return [(i * 4 + o, i * 4 + (o ^ mask)) for i in range(n_occ) for o in range(4)]


def body(
    factors, occ_level, vir_level, occupied_energy_levels, vir_table, virtual_coefficient_matrix
):
    n_occ = lax.axis_size("occ")
    occ_index = lax.axis_index("occ")
    off_index = lax.axis_index("off")
    chip = off_index // 2
    core = off_index % 2
    own = factors[0]
    n_vir, n_aux = own.shape
    half = n_vir // 2
    quarter = n_vir // 4

    ev = lookup(vir_level, vir_table)
    eo = lookup(occ_level, occupied_energy_levels)
    eo_i = lax.dynamic_index_in_dim(eo, occ_index, 0, keepdims=False)

    def eo_at(k):
        return lax.dynamic_index_in_dim(eo, (occ_index - k) % n_occ, 0, keepdims=False)

    x0 = lax.dynamic_slice_in_dim(own, chip * half, half, 0)
    x1 = lax.ppermute(x0, BOTH, moves(n_occ, lambda r: (1, 1) if r == 0 else (7, 0)))
    x2 = lax.ppermute(x1, BOTH, moves(n_occ, lambda r: (1, 0) if r == 1 else (-1, 1)))
    x3 = lax.ppermute(x2, BOTH, moves(n_occ, lambda r: (1, 1) if r == 0 else (-1, 0)))
    x3q = lax.dynamic_slice_in_dim(x3, (1 - core) * quarter, quarter, 0)
    x4 = lax.ppermute(x3q, BOTH, moves(n_occ, lambda r: (1, 1) if r == 1 else (-1, 0)))

    def amp_t(x, k, first):
        integral = lax.dot_general(x, own, (((1,), (1,)), ((), ())), preferred_element_type=jnp.float32)
        eb = lax.dynamic_slice_in_dim(ev, first, x.shape[0], 0)
        return integral / (eb[:, None] + ev[None, :] - eo_i - eo_at(k))

    def add(total, x, w):
        term = lax.dot_general(x, w, (((0,), (0,)), ((), ())), preferred_element_type=jnp.float32)
        return term if total is None else total + term

    first = chip * half + (1 - core) * quarter
    xq = lax.dynamic_slice_in_dim(own, first, quarter, 0)
    total = add(None, xq, amp_t(xq, 0, first).astype(jnp.bfloat16))

    for x, k in ((x1, jnp.where(core == 1, 1, 7)), (x2, jnp.where(core == 1, 6, 2)), (x3, jnp.where(core == 1, 3, 5))):
        at = amp_t(x, k, chip * half)
        mine = lax.dynamic_slice_in_dim(at, chip * half, half, 1)
        theirs = lax.dynamic_slice_in_dim(at, (1 - chip) * half, half, 1)
        got = lax.ppermute(theirs, BOTH, swap(n_occ, 2))
        low = jnp.where(chip == 0, mine, got)
        high = jnp.where(chip == 0, got, mine)
        back = jnp.concatenate([low.T, high.T], axis=1)
        total = add(total, x, (2.0 * at - back).astype(jnp.bfloat16))

    at = amp_t(x4, 4, first)
    piece = chip * 2 + (1 - core)
    back = jnp.zeros_like(at)
    for mask in range(4):
        target = piece ^ mask
        part = lax.dynamic_slice_in_dim(at, target * quarter, quarter, 1)
        if mask:
            part = lax.ppermute(part, BOTH, swap(n_occ, mask))
        back = lax.dynamic_update_slice_in_dim(back, part.T, target * quarter, 1)
    total = add(total, x4, (2.0 * at - back).astype(jnp.bfloat16))

    rows = n_aux // (n_occ * 4)
    blocks = total.reshape(n_occ, 2, 2, rows, n_vir)
    keep = lax.dynamic_index_in_dim(blocks, core, 2, keepdims=False)
    send = lax.dynamic_index_in_dim(blocks, 1 - core, 2, keepdims=False)
    both = keep + lax.ppermute(send, BOTH, swap(n_occ, 1))
    keep = lax.dynamic_index_in_dim(both, chip, 1, keepdims=False)
    send = lax.dynamic_index_in_dim(both, 1 - chip, 1, keepdims=False)
    gamma = keep + lax.ppermute(send, BOTH, swap(n_occ, 2))
    low = gamma.astype(jnp.bfloat16)
    mine = lax.all_to_all(low, "occ", split_axis=0, concat_axis=0, tiled=True)
    return jnp.einsum("sbd,dw->sbw", mine, virtual_coefficient_matrix, preferred_element_type=jnp.float32)


def solution(mesh):
    in_specs = (P("occ", None, None), P(), P(), P(), P(), P())
    out_specs = P(None, ("occ", "off"), None)
    return jax.shard_map(body, mesh=mesh, in_specs=in_specs, out_specs=out_specs, check_vma=False)
```

time: 575 us -> 259 us (0.45)
  waiting for transfers between devices: 335 us -> 75.2 us
  blocking collectives: 184 us -> 33.1 us
  starting transfers between devices: 6.48 us -> 61.2 us
  matrix products: 31 us -> 50.6 us
  local copies, waits for them, and re-layouts: 13.1 us -> 27.7 us
    ppermute x4 -> x12, waiting for transfers between devices: 335 us -> 75.2 us  [the longest x1 35 us: body(): gamma = keep + lax.ppermute(send, BOTH, swap(n_occ, 2))]
    psum x1 -> x0, blocking collectives: 112 us -> none  [body(): total = lax.psum(blocks, 'off')]
    ppermute x4 -> x12, starting transfers between devices: 6.48 us -> 61.2 us  [the longest x1 35.3 us: body(): lax.ppermute(x3q, BOTH, moves(n_occ, lambda r: (1, 1) if r == 1 else (-1,...]
    all_to_all x1, blocking collectives: 72.3 us -> 33.1 us  [body(): mine = lax.all_to_all(low, 'occ', split_axis=0, concat_axis=0, tiled=True)]
    dot_general x5 -> x10, matrix products: 31 us -> 50.6 us  [the longest x5 30.5 us: add(): lax.dot_general(x, w, (((0,), (0,)), ((), ())), preferred_element_type=jn...]
    div x0 -> x3, local copies, waits for them, and re-layouts: none -> 8.06 us  [amp_t(): return integral / (eb[:, None] + ev[None, :] - eo_i - eo_at(k))]
    dynamic_slice x1 -> x9, local copies, waits for them, and re-layouts: 0.67 us -> 7.43 us  [the longest x3 3.99 us: body(): theirs = lax.dynamic_slice_in_dim(at, (1 - chip) * half, half, 1)]
    dot_general x2 -> x0, local copies, waits for them, and re-layouts: 6.19 us -> none  [body(): lax.dot_general(own, other, (((1,), (1,)), ((), ())), preferred_element_t...]
  transfers between devices with their start and end apart: 4 -> 12, of which waited for: 4 -> 8; matrix products, arithmetic and copies ran while one was open for 2% -> 21% of each run, Pallas kernels for 0% -> 0%
where the time goes in v1:
time: 259 us; the launch traced here: 257 us
  waiting for transfers between devices  75.2 us (29%)
  starting transfers between devices  61.2 us (24%)
  matrix products  50.6 us (20%)
  blocking collectives  33.1 us (13%)
  local copies, waits for them, and re-layouts  27.7 us (11%)
  other arithmetic  9.22 us (4%)
    ppermute x1, starting transfers between devices, body(): lax.ppermute(x3q, BOTH, moves(n_occ, lambda r: (1, 1) if r == 1 else (-1,...  35.3 us
    ppermute x1, waiting for transfers between devices, body(): gamma = keep + lax.ppermute(send, BOTH, swap(n_occ, 2))  35 us
    all_to_all x1, blocking collectives, body(): mine = lax.all_to_all(low, 'occ', split_axis=0, concat_axis=0, tiled=True)  33.1 us
    dot_general x5, matrix products, add(): lax.dot_general(x, w, (((0,), (0,)), ((), ())), preferred_element_type=jn...  30.5 us
    ppermute x1, waiting for transfers between devices, body(): lax.ppermute(x0, BOTH, moves(n_occ, lambda r: (1, 1) if r == 0 else (7, 0)))  19.5 us
    dot_general x4, matrix products, amp_t(): lax.dot_general(x, own, (((1,), (1,)), ((), ())), preferred_element_type=...  17.8 us
    ppermute x1, starting transfers between devices, body(): lax.ppermute(x1, BOTH, moves(n_occ, lambda r: (1, 0) if r == 1 else (-1,...  14.6 us
    ppermute x3, waiting for transfers between devices, body(): got = lax.ppermute(theirs, BOTH, swap(n_occ, 2))  11 us
  transfers between devices with their start and end apart: 12, of which 8 were waited for; matrix products, arithmetic and copies ran while one was open for 21% of the time, Pallas kernels for 0%

profile of v1, /device:TPU:56, one launch (start us, length us, event | category | flops | bytes accessed | tf_op | source)
XLA Modules:
  0.0 257.3 jit_solution(495908159786606518)
XLA Ops:
  0.0 1.9 copy-done
  3.5 19.5 %collective-permute-done = bf16[384,2048]{1,0:T(8,128)(2,1)} collective-permute-done((bf16[384,2048]{1,0:T(8,128)(2,1)S(1)}, bf16[384,2048]{1,0:T(8,128)(2,1)}, u32[]{:S(2)}, u32[]{:S(2)}) %collective-permute-start) | collective-permute-done | bytes 1572896 | tf_op jit(solution)/shard_map/ppermute | solution.py:49
  23.0 14.6 %collective-permute-start.2 = (bf16[384,2048]{1,0:T(8,128)(2,1)}, bf16[384,2048]{1,0:T(8,128)(2,1)}, u32[]{:S(2)}, u32[]{:S(2)}) collective-permute-start(bf16[384,2048]{1,0:T(8,128)(2,1)} %collective-permute-done), channel_id=1, source_target_pairs={{0,253},{1,4},{2,255},{3,6},{4,1},{5,8},{6,3},{7,10},{8,5},{9,12},... | collective-permute-start | bytes 4718600 | tf_op jit(solution)/shard_map/ppermute | solution.py:50
  39.0 5.7 %fusion.29 = f32[2048,768]{1,0:T(8,128)} fusion(bf16[1,768,2048]{2,1,0:T(8,128)(2,1)S(1)} %copy-done, s32[]{:T(128)S(6)} %select_n.150, f32[]{:T(128)} %bitcast.3, f32[]{:T(128)} %bitcast.2, f32[768]{0:T(1024)S(1)} %select_reduce_fusion, f32[192]{0:T(256)S(1)} %dynamic_slice.87), kind=kOutput, calls=%fused_computation.24 | convolution fusion | flops 1208696832 | bytes 11016200 | tf_op jit(solution)/shard_map/dot_general | solution.py:61
  44.7 5.1 %fusion.13 = f32[384,768]{1,0:T(8,128)} fusion(bf16[384,2048]{1,0:T(8,128)(2,1)} %collective-permute-done, bf16[1,768,2048]{2,1,0:T(8,128)(2,1)S(1)} %copy-done, f32[]{:T(128)} %bitcast.5, f32[]{:T(128)} %bitcast.2, f32[768]{0:T(1024)S(1)} %select_reduce_fusion, f32[384]{0:T(512)S(1)} %dynamic_slice.92), kind=kOutput, calls=%fused_computation.19 | convolution fusion | flops 1209139200 | bytes 5902856 | tf_op jit(solution)/shard_map/dot_general | solution.py:56
  49.8 2.7 %copy.23 = f32[384,768]{0,1:T(8,128)} copy(f32[384,768]{1,0:T(8,128)} %fusion.13) | data formatting | bytes 2359296 | tf_op jit(solution)/shard_map/div | solution.py:58
  53.6 1.6 collective-permute-start.1
  56.1 4.1 %fusion.16 = f32[384,768]{1,0:T(8,128)S(1)} fusion(bf16[384,2048]{1,0:T(8,128)(2,1)} %collective-permute-done.2, bf16[1,768,2048]{2,1,0:T(8,128)(2,1)S(1)} %copy-done, f32[]{:T(128)} %bitcast.8, f32[]{:T(128)} %bitcast.2, f32[768]{0:T(1024)S(1)} %select_reduce_fusion, f32[384]{0:T(512)S(1)} %dynamic_slice.92), kind=kOutput, calls=%fused_computation.20 | convolution fusion | flops 1209139200 | bytes 5902856 | tf_op jit(solution)/shard_map/dot_general | solution.py:56
  62.6 7.2 %collective-permute-done.1 = f32[384,384]{1,0:T(8,128)S(1)} collective-permute-done((f32[384,384]{1,0:T(8,128)S(1)}, f32[384,384]{1,0:T(8,128)S(1)}, u32[]{:S(2)}, u32[]{:S(2)}) %collective-permute-start.1) | collective-permute-done | bytes 589856 | tf_op jit(solution)/shard_map/ppermute | solution.py:72
  69.9 5.9 %fusion.44 = f32[2048,768]{1,0:T(8,128)} fusion(bf16[384,2048]{1,0:T(8,128)(2,1)} %collective-permute-done, f32[384,384]{0,1:T(8,128)S(1)} %get-tuple-element.8, f32[384,384]{0,1:T(8,128)S(1)} %get-tuple-element.7, f32[384,768]{0,1:T(8,128)S(1)} %copy-done.3), kind=kOutput, calls=%fused_computation.38 | convolution fusion | flops 1209139200 | bytes 10223616 | tf_op jit(solution)/shard_map/dot_general | solution.py:61
  75.9 2.7 %copy.24 = f32[384,768]{0,1:T(8,128)} copy(f32[384,768]{1,0:T(8,128)} %copy-done.5) | data formatting | bytes 2359296 | tf_op jit(solution)/shard_map/div | solution.py:58
  78.5 3.8 %collective-permute-done.3 = f32[384,384]{1,0:T(8,128)} collective-permute-done((f32[384,384]{1,0:T(8,128)}, f32[384,384]{1,0:T(8,128)}, u32[]{:S(2)}, u32[]{:S(2)}) %collective-permute-start.3) | collective-permute-done | bytes 589856 | tf_op jit(solution)/shard_map/ppermute | solution.py:72
  83.7 2.1 constant_dynamic-slice_fusion.3
  85.8 35.3 %collective-permute-start.6 = (bf16[192,2048]{1,0:T(8,128)(2,1)}, bf16[192,2048]{1,0:T(8,128)(2,1)}, u32[]{:S(2)}, u32[]{:S(2)}) collective-permute-start(bf16[192,2048]{1,0:T(8,128)(2,1)} %constant_dynamic-slice_fusion.3), channel_id=1, source_target_pairs={{0,252},{1,5},{2,254},{3,7},{4,0},{5,9},{6,2},{7,11},{8,4},{9,13},... | collective-permute-start | bytes 2359304 | tf_op jit(solution)/shard_map/ppermute | solution.py:53
  121.1 5.1 %fusion.19 = f32[384,768]{1,0:T(8,128)} fusion(bf16[384,2048]{1,0:T(8,128)(2,1)} %collective-permute-done.4, bf16[1,768,2048]{2,1,0:T(8,128)(2,1)S(1)} %copy-done, f32[]{:T(128)} %bitcast.11, f32[]{:T(128)} %bitcast.2, f32[768]{0:T(1024)S(1)} %select_reduce_fusion, f32[384]{0:T(512)S(1)} %dynamic_slice.92), kind=kOutput, calls=%fused_computation.21 | convolution fusion | flops 1209139200 | bytes 5902856 | tf_op jit(solution)/shard_map/dot_general | solution.py:56
  126.2 2.0 constant_dynamic-slice_fusion.4
  129.7 5.9 %fusion.42 = f32[2048,768]{1,0:T(8,128)} fusion(bf16[384,2048]{1,0:T(8,128)(2,1)} %collective-permute-done.2, f32[384,384]{0,1:T(8,128)S(1)} %get-tuple-element.10, f32[384,384]{0,1:T(8,128)S(1)} %get-tuple-element.9, f32[384,768]{0,1:T(8,128)S(1)} %copy-done.4), kind=kOutput, calls=%fused_computation.37 | convolution fusion | flops 1209139200 | bytes 10223616 | tf_op jit(solution)/shard_map/dot_general | solution.py:61
  135.6 2.7 %copy.25 = f32[384,768]{0,1:T(8,128)} copy(f32[384,768]{1,0:T(8,128)} %fusion.19) | data formatting | bytes 2359296 | tf_op jit(solution)/shard_map/div | solution.py:58
  138.3 3.4 %fusion.31 = f32[192,768]{1,0:T(8,128)S(1)} fusion(bf16[192,2048]{1,0:T(8,128)(2,1)} %collective-permute-done.6, bf16[1,768,2048]{2,1,0:T(8,128)(2,1)S(1)} %copy-done, f32[]{:T(128)} %bitcast.14, f32[]{:T(128)} %bitcast.2, f32[768]{0:T(1024)S(1)} %select_reduce_fusion, f32[192]{0:T(256)S(1)} %dynamic_slice.87), kind=kOutput, calls=%fused_computation.25 | convolution fusion | flops 604569600 | bytes 4525832 | tf_op jit(solution)/shard_map/dot_general | solution.py:56
  144.1 2.4 select_bitcast_fusion.1
  146.6 1.8 dynamic_update_slice.12
  149.5 2.4 collective-permute-done.8
  156.2 2.3 fusion.50
  159.2 10.5 %add_add_fusion = f32[2048,768]{1,0:T(8,128)} fusion(f32[2048,768]{1,0:T(8,128)S(1)} %fusion.50, f32[2048,768]{1,0:T(8,128)} %fusion.42, f32[2048,768]{1,0:T(8,128)} %fusion.29, f32[2048,768]{1,0:T(8,128)S(1)} %bitcast.82, bf16[384,2048]{1,0:T(8,128)(2,1)} %collective-permute-done.4, f32[384,384]{0,1:T(8,128)S(1)} %copy-done.10, f32[384,384]{0,1:T(8,128)S(1)} %copy-done.9, ...), kind=kOutput, calls=%fused_computation | convolution fusion | flops 1215430656 | bytes 35389440 | tf_op jit(solution)/shard_map/dot_general | solution.py:61
  169.7 2.1 dynamic-slice_bitcast_fusion
  172.9 5.4 %collective-permute-done.10 = f32[64,2,8,768]{3,2,1,0:T(8,128)} collective-permute-done((f32[64,2,8,768]{3,2,1,0:T(8,128)S(1)}, f32[64,2,8,768]{3,2,1,0:T(8,128)}, u32[]{:S(2)}, u32[]{:S(2)}) %collective-permute-start.10) | collective-permute-done | bytes 3145760 | tf_op jit(solution)/shard_map/ppermute | solution.py:93
  178.3 3.4 %bitcast_add_fusion = f32[64,2,8,768]{3,2,1,0:T(8,128)S(1)} fusion(f32[64,2,8,768]{3,2,1,0:T(8,128)} %collective-permute-done.10, f32[64,2,2,8,768]{4,3,2,1,0:T(8,128)} %bitcast.84, s32[]{:T(128)S(6)} %select_n.181), kind=kLoop, calls=%fused_computation.1 | loop fusion | flops 786432 | bytes 9437188 | tf_op jit(solution)/shard_map/add | solution.py:93
  183.0 2.3 collective-permute-start.11
  185.2 35.0 %collective-permute-done.11 = f32[64,8,768]{2,1,0:T(8,128)} collective-permute-done((f32[64,8,768]{2,1,0:T(8,128)}, f32[64,8,768]{2,1,0:T(8,128)}, u32[]{:S(2)}, u32[]{:S(2)}) %collective-permute-start.11) | collective-permute-done | bytes 1572896 | tf_op jit(solution)/shard_map/ppermute | solution.py:96
  220.3 1.6 fusion.12
  221.9 33.1 %all_to_all.5 = bf16[64,8,768]{2,1,0:T(8,128)(2,1)S(1)} all-to-all(bf16[64,8,768]{2,1,0:T(8,128)(2,1)S(1)} %fusion.12), channel_id=1, replica_groups=mesh['occ'=64,'off'=4] {'occ'}, dimensions={0} | all-to-all | bytes 1572864 | tf_op jit(solution)/shard_map/all_to_all | solution.py:98
  255.0 2.3 fusion.10
  (70 shorter events, 20.8 us)
Async XLA Ops:
  0.0 1.9 copy-start
  1.9 35.8 %copy-start.11 = (s32[768]{0:T(1024)S(1)}, s32[768]{0:T(1024)}, u32[]{:S(2)}) copy-start(s32[768]{0:T(1024)} %param.8) | copy-start | bytes 9220
  1.9 35.8 %copy-start.12 = (f32[256]{0:T(256)S(1)}, f32[256]{0:T(256)}, u32[]{:S(2)}) copy-start(f32[256]{0:T(256)} %param.10) | copy-start | bytes 3076
  1.9 36.2 %copy-start.13 = (f32[256]{0:T(256)S(1)}, f32[256]{0:T(256)}, u32[]{:S(2)}) copy-start(f32[256]{0:T(256)} %param.9) | copy-start | bytes 3076
  1.9 36.2 %copy-start.14 = (s32[64]{0:T(128)S(1)}, s32[64]{0:T(128)}, u32[]{:S(2)}) copy-start(s32[64]{0:T(128)} %param.7) | copy-start | bytes 772
  2.1 20.9 %collective-permute-start = (bf16[384,2048]{1,0:T(8,128)(2,1)S(1)}, bf16[384,2048]{1,0:T(8,128)(2,1)}, u32[]{:S(2)}, u32[]{:S(2)}) collective-permute-start(bf16[384,2048]{1,0:T(8,128)(2,1)S(1)} %dynamic-slice_bitcast_fusion.2), channel_id=1, source_target_pairs={{0,5},{1,28},{2,7},{3,30},{4,9},{5,32},{6,11},{7,34},{8,13},{9,36}... | collective-permute-start | bytes 4718600 | tf_op jit(solution)/shard_map/ppermute | solution.py:49
  23.0 33.0 %collective-permute-start.2 = (bf16[384,2048]{1,0:T(8,128)(2,1)}, bf16[384,2048]{1,0:T(8,128)(2,1)}, u32[]{:S(2)}, u32[]{:S(2)}) collective-permute-start(bf16[384,2048]{1,0:T(8,128)(2,1)} %collective-permute-done), channel_id=1, source_target_pairs={{0,253},{1,4},{2,255},{3,6},{4,1},{5,8},{6,3},{7,10},{8,5},{9,12},... | collective-permute-start | bytes 4718600 | tf_op jit(solution)/shard_map/ppermute | solution.py:50
  53.6 16.2 %collective-permute-start.1 = (f32[384,384]{1,0:T(8,128)S(1)}, f32[384,384]{1,0:T(8,128)S(1)}, u32[]{:S(2)}, u32[]{:S(2)}) collective-permute-start(f32[384,384]{1,0:T(8,128)S(1)} %constant_dynamic-slice_fusion.6), channel_id=1, source_target_pairs={{0,2},{1,3},{2,0},{3,1},{4,6},{5,7},{6,4},{7,5},{8,10},{9,11},{10,... | collective-permute-start | bytes 1769480 | tf_op jit(solution)/shard_map/ppermute | solution.py:72
  56.1 27.6 %collective-permute-start.4 = (bf16[384,2048]{1,0:T(8,128)(2,1)}, bf16[384,2048]{1,0:T(8,128)(2,1)}, u32[]{:S(2)}, u32[]{:S(2)}) collective-permute-start(bf16[384,2048]{1,0:T(8,128)(2,1)} %collective-permute-done.2), channel_id=1, source_target_pairs={{0,5},{1,252},{2,7},{3,254},{4,9},{5,0},{6,11},{7,2},{8,13},{9,4},... | collective-permute-start | bytes 4718600 | tf_op jit(solution)/shard_map/ppermute | solution.py:51
  56.1 13.8 %copy-start.6 = (f32[384,768]{1,0:T(8,128)S(1)}, f32[384,768]{1,0:T(8,128)}, u32[]{:S(2)}) copy-start(f32[384,768]{1,0:T(8,128)} %fusion.13) | copy-start | bytes 3538948
  60.2 9.7 %copy-start.5 = (f32[384,768]{1,0:T(8,128)}, f32[384,768]{1,0:T(8,128)S(1)}, u32[]{:S(2)}) copy-start(f32[384,768]{1,0:T(8,128)S(1)} %fusion.16) | copy-start | bytes 3538948
  60.2 9.7 %copy-start.3 = (f32[384,768]{0,1:T(8,128)S(1)}, f32[384,768]{0,1:T(8,128)}, u32[]{:S(2)}) copy-start(f32[384,768]{0,1:T(8,128)} %copy.23) | copy-start | bytes 3538948
  61.1 21.2 %collective-permute-start.3 = (f32[384,384]{1,0:T(8,128)}, f32[384,384]{1,0:T(8,128)}, u32[]{:S(2)}, u32[]{:S(2)}) collective-permute-start(f32[384,384]{1,0:T(8,128)} %constant_dynamic-slice_fusion.5), channel_id=1, source_target_pairs={{0,2},{1,3},{2,0},{3,1},{4,6},{5,7},{6,4},{7,5},{8,10},{9,11},{10,... | collective-permute-start | bytes 1769480 | tf_op jit(solution)/shard_map/ppermute | solution.py:72
  85.8 52.5 %collective-permute-start.6 = (bf16[192,2048]{1,0:T(8,128)(2,1)}, bf16[192,2048]{1,0:T(8,128)(2,1)}, u32[]{:S(2)}, u32[]{:S(2)}) collective-permute-start(bf16[192,2048]{1,0:T(8,128)(2,1)} %constant_dynamic-slice_fusion.3), channel_id=1, source_target_pairs={{0,252},{1,5},{2,254},{3,7},{4,0},{5,9},{6,2},{7,11},{8,4},{9,13},... | collective-permute-start | bytes 2359304 | tf_op jit(solution)/shard_map/ppermute | solution.py:53
  126.2 3.5 %copy-start.4 = (f32[384,768]{0,1:T(8,128)S(1)}, f32[384,768]{0,1:T(8,128)}, u32[]{:S(2)}) copy-start(f32[384,768]{0,1:T(8,128)} %copy.24) | copy-start | bytes 3538948
  128.2 15.8 %collective-permute-start.5 = (f32[384,384]{1,0:T(8,128)}, f32[384,384]{1,0:T(8,128)}, u32[]{:S(2)}, u32[]{:S(2)}) collective-permute-start(f32[384,384]{1,0:T(8,128)} %constant_dynamic-slice_fusion.4), channel_id=1, source_target_pairs={{0,2},{1,3},{2,0},{3,1},{4,6},{5,7},{6,4},{7,5},{8,10},{9,11},{10,... | collective-permute-start | bytes 1769480 | tf_op jit(solution)/shard_map/ppermute | solution.py:72
  141.8 4.6 %copy-start.7 = (f32[192,768]{1,0:T(8,128)}, f32[192,768]{1,0:T(8,128)S(1)}, u32[]{:S(2)}) copy-start(f32[192,768]{1,0:T(8,128)S(1)} %fusion.31) | copy-start | bytes 1769476
  142.1 7.3 %collective-permute-start.9 = (f32[192,192]{1,0:T(8,128)S(1)}, f32[192,192]{1,0:T(8,128)S(1)}, u32[]{:S(2)}, u32[]{:S(2)}) collective-permute-start(f32[192,192]{1,0:T(8,128)S(1)} %get-tuple-element.11), channel_id=1, source_target_pairs={{0,3},{1,2},{2,1},{3,0},{4,7},{5,6},{6,5},{7,4},{8,11},{9,10},{10,... | collective-permute-start | bytes 442376 | tf_op jit(solution)/shard_map/ppermute | solution.py:85
  142.2 9.7 %collective-permute-start.8 = (f32[192,192]{1,0:T(8,128)S(1)}, f32[192,192]{1,0:T(8,128)S(1)}, u32[]{:S(2)}, u32[]{:S(2)}) collective-permute-start(f32[192,192]{1,0:T(8,128)S(1)} %get-tuple-element.12), channel_id=1, source_target_pairs={{0,2},{1,3},{2,0},{3,1},{4,6},{5,7},{6,4},{7,5},{8,10},{9,11},{10,... | collective-permute-start | bytes 442376 | tf_op jit(solution)/shard_map/ppermute | solution.py:85
  142.9 9.1 %collective-permute-start.7 = (f32[192,192]{1,0:T(8,128)S(1)}, f32[192,192]{1,0:T(8,128)S(1)}, u32[]{:S(2)}, u32[]{:S(2)}) collective-permute-start(f32[192,192]{1,0:T(8,128)S(1)} %get-tuple-element.13), channel_id=1, source_target_pairs={{0,1},{1,0},{2,3},{3,2},{4,5},{5,4},{6,7},{7,6},{8,9},{9,8},{10,11... | collective-permute-start | bytes 442376 | tf_op jit(solution)/shard_map/ppermute | solution.py:85
  146.5 9.6 %copy-start.8 = (f32[192,768]{1,0:T(8,128)S(1)}, f32[192,768]{1,0:T(8,128)}, u32[]{:S(2)}) copy-start(f32[192,768]{1,0:T(8,128)} %copy-done.7) | copy-start | bytes 1769476
  154.9 3.6 %slice-start = ((s8[6291456]{0:T(1024)(128)(4,1)}), s8[2097152]{0:T(1024)(128)(4,1)S(1)}, s32[]{:S(2)}) async-start(s8[6291456]{0:T(1024)(128)(4,1)} %bitcast.81), calls=%async_computation.1 | async-start | bytes 4194304
  156.1 2.5 slice-start.1
  156.1 2.8 %copy-start.2 = (f32[384,768]{0,1:T(8,128)S(1)}, f32[384,768]{0,1:T(8,128)}, u32[]{:S(2)}) copy-start(f32[384,768]{0,1:T(8,128)} %copy.25) | copy-start | bytes 3538948
  156.1 2.9 %copy-start.9 = (f32[384,384]{0,1:T(8,128)S(1)}, f32[384,384]{0,1:T(8,128)}, u32[]{:S(2)}) copy-start(f32[384,384]{0,1:T(8,128)} %get-tuple-element.5) | copy-start | bytes 1769476
  156.2 3.1 %copy-start.10 = (f32[384,384]{0,1:T(8,128)S(1)}, f32[384,384]{0,1:T(8,128)}, u32[]{:S(2)}) copy-start(f32[384,384]{0,1:T(8,128)} %get-tuple-element.6) | copy-start | bytes 1769476
  171.8 6.5 %collective-permute-start.10 = (f32[64,2,8,768]{3,2,1,0:T(8,128)S(1)}, f32[64,2,8,768]{3,2,1,0:T(8,128)}, u32[]{:S(2)}, u32[]{:S(2)}) collective-permute-start(f32[64,2,8,768]{3,2,1,0:T(8,128)S(1)} %dynamic-slice_bitcast_fusion), channel_id=1, source_target_pairs={{0,1},{1,0},{2,3},{3,2},{4,5},{5,4},{6,7},{7,6},{8,9},{9,8},{10,11... | collective-permute-start | bytes 9437192 | tf_op jit(solution)/shard_map/ppermute | solution.py:93
  183.0 37.3 %collective-permute-start.11 = (f32[64,8,768]{2,1,0:T(8,128)}, f32[64,8,768]{2,1,0:T(8,128)}, u32[]{:S(2)}, u32[]{:S(2)}) collective-permute-start(f32[64,8,768]{2,1,0:T(8,128)} %dynamic-slice_bitcast_fusion.1), channel_id=1, source_target_pairs={{0,2},{1,3},{2,0},{3,1},{4,6},{5,7},{6,4},{7,5},{8,10},{9,11},{10,... | collective-permute-start | bytes 4718600 | tf_op jit(solution)/shard_map/ppermute | solution.py:96
  221.8 33.1 %copy-start.15 = (bf16[768,1024]{1,0:T(8,128)(2,1)S(1)}, bf16[768,1024]{1,0:T(8,128)(2,1)}, u32[]{:S(2)}) copy-start(bf16[768,1024]{1,0:T(8,128)(2,1)} %param.11) | copy-start | bytes 4718596
  221.8 35.4 %copy-start.1 = (bf16[1,768,2048]{2,1,0:T(8,128)(2,1)S(1)}, bf16[1,768,2048]{2,1,0:T(8,128)(2,1)}, u32[]{:S(2)}) copy-start(bf16[1,768,2048]{2,1,0:T(8,128)(2,1)} %param.6) | copy-start | bytes 9437188

commit v2 on v1

v2 whole, which is shorter than its diff:
```python
import functools

import jax
import jax.numpy as jnp
from jax import lax
from jax.experimental import pallas as pl
from jax.experimental.pallas import tpu as pltpu
from jax.sharding import PartitionSpec as P

BOTH = ("occ", "off")
F32 = jnp.float32
BF16 = jnp.bfloat16
RING = 8
TN = (((0,), (0,)), ((), ()))
NT = (((1,), (1,)), ((), ()))


def lookup(level, table):
    hits = level[:, None] == jnp.arange(table.shape[0], dtype=jnp.int32)[None, :]
    return jnp.sum(jnp.where(hits, table[None, :], jnp.float32(0.0)), axis=1)


def moves(n_occ, rule):
    pairs = []
    half = n_occ // 2
    for i in range(n_occ):
        for chip in range(2):
            for core in range(2):
                j, to = rule(i, core)
                j %= n_occ
                flip = (i // half) ^ (j // half)
                pairs.append((i * 4 + chip * 2 + core, j * 4 + (chip ^ flip) * 2 + to))
    return pairs


def swap(n_occ, mask):
    return [(i * 4 + o, i * 4 + (o ^ mask)) for i in range(n_occ) for o in range(4)]


def round1(i, core):
    if core == 0:
        return i + 1, 1
    return (i + RING, 0) if i % RING else (i, 0)


def round2(i, core):
    if core == 1:
        return i + 1, 0
    return i - i % RING + (i - 1) % RING, 1


def round3(i, core):
    return (i + 1, 1) if core == 0 else (i - 1, 0)


def round4(i, core):
    return (i + 1, 0) if core == 1 else (i - 1, 1)


def sds(shape, dtype):
    return jax.ShapeDtypeStruct(shape, dtype)


def cost(flops, nbytes):
    return pl.CostEstimate(flops=flops, bytes_accessed=nbytes, transcendentals=0)


def amp_kernel(sc, own, x, evc, evr, eo, s_out, w_out, acc, *, half, steps, slot):
    t = pl.program_id(0)
    prod = lax.dot_general(x[...], own[...], NT, preferred_element_type=F32)

    @pl.when(t == 0)
    def _():
        acc[...] = prod

    @pl.when(t > 0)
    def _():
        acc[...] += prod

    @pl.when(t == steps - 1)
    def _():
        h = sc[0]
        e = jnp.concatenate([evc[...]] * (half // 128), axis=1)

        def amp(first):
            cols = pl.ds(pl.multiple_of(first * half, half), half)
            return acc[:, cols] / (e + evr[:, cols] - eo[sc[3]] - eo[sc[4 + slot]])

        s_out[...] = amp(1 - h).astype(s_out.dtype)
        mine = amp(h)
        w_out[...] = (2.0 * mine - mine.T).astype(BF16)


def mix_kernel(sc, s, q, w, o, *, half):
    h = sc[0]
    o[:, pl.ds(pl.multiple_of(h * half, half), half)] = w[...]
    other = 2.0 * s[...].astype(F32) - q[...].astype(F32).T
    o[:, pl.ds(pl.multiple_of((1 - h) * half, half), half)] = other.astype(BF16)


def gamma_kernel(*refs, n, half):
    xs, ws, outs = refs[:n], refs[n : 2 * n], refs[2 * n :]
    res = lax.dot_general(xs[0][...], ws[0][...], TN, preferred_element_type=F32)
    for k in range(1, n):
        res += lax.dot_general(xs[k][...], ws[k][...], TN, preferred_element_type=F32)
    outs[0][...] = res[:, :half]
    outs[1][...] = res[:, half:]


def last_kernel(sc, *refs, n):
    xs, ws, early, keep, send = refs[:n], refs[n : 2 * n], refs[2 * n], refs[2 * n + 1], refs[2 * n + 2]
    res = early[...]
    for k in range(n):
        res += lax.dot_general(xs[k][...], ws[k][...], TN, preferred_element_type=F32)
    res = res.reshape(res.shape[0] // 32, 2, 2, 8, res.shape[1])
    a, b = res[:, :, 0], res[:, :, 1]
    first = sc[1] == 0
    keep[...] = jnp.where(first, a, b)
    send[...] = jnp.where(first, b, a)


def body(
    factors, occ_level, vir_level, occupied_energy_levels, vir_table, virtual_coefficient_matrix
):
    n_occ = lax.axis_size("occ")
    occ_index = lax.axis_index("occ")
    off_index = lax.axis_index("off")
    chip = off_index // 2
    core = off_index % 2
    own = factors[0]
    n_vir, n_aux = own.shape
    half = n_vir // 2
    h = chip ^ (occ_index // (n_occ // 2))
    partners = [(occ_index - jnp.where(core == 0, a, b)) % n_occ for a, b in ((0, 1), (2, 7), (6, 3), (4, 5))]
    sc = jnp.stack([h, core, chip, occ_index, *partners]).astype(jnp.int32)

    x0 = lax.dynamic_slice_in_dim(own, h * half, half, 0)
    x1 = lax.ppermute(x0, BOTH, moves(n_occ, round1))
    x2 = lax.ppermute(x1, BOTH, moves(n_occ, round2))

    ev = lookup(vir_level, vir_table)
    eo = lookup(occ_level, occupied_energy_levels)
    evr = ev[None, :]
    evc = jnp.broadcast_to(lax.dynamic_slice_in_dim(ev, h * half, half, 0)[:, None], (half, 128))

    steps = 2
    tile = n_aux // steps

    def amp(x, slot, s_dtype):
        return pl.pallas_call(
            functools.partial(amp_kernel, half=half, steps=steps, slot=slot),
            out_shape=(sds((half, half), s_dtype), sds((half, half), BF16)),
            grid_spec=pltpu.PrefetchScalarGridSpec(
                num_scalar_prefetch=1,
                grid=(steps,),
                in_specs=[
                    pl.BlockSpec((n_vir, tile), lambda t, s: (0, t)),
                    pl.BlockSpec((half, tile), lambda t, s: (0, t)),
                    pl.BlockSpec((half, 128), lambda t, s: (0, 0)),
                    pl.BlockSpec((1, n_vir), lambda t, s: (0, 0)),
                    pl.BlockSpec(memory_space=pltpu.SMEM),
                ],
                out_specs=[pl.BlockSpec((half, half), lambda t, s: (0, 0))] * 2,
                scratch_shapes=[pltpu.VMEM((half, n_vir), F32)],
            ),
            cost_estimate=cost(2 * n_vir * half * n_aux, 2 * n_aux * (n_vir + half)),
            name="amp",
        )(sc, own, x, evc, evr, eo)

    def mix(s, w):
        q = lax.ppermute(s, BOTH, swap(n_occ, 2))
        whole = pl.BlockSpec((half, half), lambda t, s: (0, 0))
        return pl.pallas_call(
            functools.partial(mix_kernel, half=half),
            out_shape=sds((half, n_vir), BF16),
            grid_spec=pltpu.PrefetchScalarGridSpec(
                num_scalar_prefetch=1,
                grid=(1,),
                in_specs=[whole] * 3,
                out_specs=pl.BlockSpec((half, n_vir), lambda t, s: (0, 0)),
            ),
            cost_estimate=cost(half * half * 4, half * half * 14),
            name="mix",
        )(sc, s, q, w)

    y1 = jnp.where(core == 0, x0, x1)
    s1, v1 = amp(y1, 0, F32)
    x2, s1 = lax.optimization_barrier((x2, s1))
    x3 = lax.ppermute(x2, BOTH, moves(n_occ, round3))
    s2, v2 = amp(x2, 1, F32)
    w1 = mix(s1, v1)
    x3, s2, w1 = lax.optimization_barrier((x3, s2, w1))
    x4 = lax.ppermute(x3, BOTH, moves(n_occ, round4))
    s3, v3 = amp(x3, 2, F32)
    w2 = mix(s2, v2)

    tiles = 4
    tile_p = n_aux // tiles
    early = pl.pallas_call(
        functools.partial(gamma_kernel, n=2, half=half),
        out_shape=(sds((n_aux, half), F32),) * 2,
        grid=(tiles,),
        in_specs=[pl.BlockSpec((half, tile_p), lambda t: (0, t))] * 2
        + [pl.BlockSpec((half, n_vir), lambda t: (0, 0))] * 2,
        out_specs=[pl.BlockSpec((tile_p, half), lambda t: (t, 0))] * 2,
        cost_estimate=cost(4 * n_aux * half * n_vir, 4 * n_aux * half + 4 * n_aux * n_vir),
        name="gamma",
    )(y1, x2, w1, w2)
    x4, s3, early = lax.optimization_barrier((x4, s3, early))
    s4, v4 = amp(x4, 3, BF16)
    w3 = mix(s3, v3)
    w4 = mix(s4, v4)

    groups = tile_p // 32

    def last(g, early):
        return pl.pallas_call(
            functools.partial(last_kernel, n=2),
            out_shape=(sds((n_occ, 2, 8, half), F32),) * 2,
            grid_spec=pltpu.PrefetchScalarGridSpec(
                num_scalar_prefetch=1,
                grid=(tiles,),
                in_specs=[pl.BlockSpec((half, tile_p), lambda t, s: (0, t))] * 2
                + [pl.BlockSpec((half, half), lambda t, s: (0, g))] * 2
                + [pl.BlockSpec((tile_p, half), lambda t, s: (t, 0))],
                out_specs=[pl.BlockSpec((groups, 2, 8, half), lambda t, s: (t, 0, 0, 0))] * 2,
            ),
            cost_estimate=cost(2 * n_aux * half * n_vir, 4 * n_aux * (n_vir + half)),
            name="last",
        )(sc, x3, x4, w3, w4, early)

    def part(keep, got, c):
        a = lax.dynamic_index_in_dim(keep, c, 1, keepdims=False)
        return a + lax.dynamic_index_in_dim(got, c, 1, keepdims=False)

    def finish(g, keep, got, far):
        low = (part(keep, got, chip) + far.astype(F32)).astype(BF16)
        mine = lax.all_to_all(low, "occ", split_axis=0, concat_axis=0, tiled=True)
        c = virtual_coefficient_matrix[g * half : (g + 1) * half]
        return jnp.einsum("sbd,dw->sbw", mine, c, preferred_element_type=F32)

    keep0, send0 = last(0, early[0])
    early1, send0 = lax.optimization_barrier((early[1], send0))
    got0 = lax.ppermute(send0, BOTH, swap(n_occ, 1))
    keep1, send1 = last(1, early1)
    away0 = part(keep0, got0, 1 - chip).astype(BF16)
    away0, send1 = lax.optimization_barrier((away0, send1))
    far0 = lax.ppermute(away0, BOTH, swap(n_occ, 2))
    got1 = lax.ppermute(send1, BOTH, swap(n_occ, 1))
    away1 = part(keep1, got1, 1 - chip)
    away1, far0 = lax.optimization_barrier((away1, far0))
    far1 = lax.ppermute(away1, BOTH, swap(n_occ, 2))
    return finish(0, keep0, got0, far0) + finish(1, keep1, got1, far1)


def solution(mesh):
    in_specs = (P("occ", None, None), P(), P(), P(), P(), P())
    out_specs = P(None, ("occ", "off"), None)
    return jax.shard_map(body, mesh=mesh, in_specs=in_specs, out_specs=out_specs, check_vma=False)
```

time: 259 us -> 205 us (0.79)
  Pallas kernels: 0 us -> 55.1 us
  matrix products: 50.6 us -> 5.01 us
  blocking collectives: 33.1 us -> 0 us
  local copies, waits for them, and re-layouts: 27.7 us -> 6.49 us
  starting transfers between devices: 61.2 us -> 42.4 us
  waiting for transfers between devices: 75.2 us -> 86.7 us
    pallas_call x0 -> x11, Pallas kernels: none -> 55.1 us  [the longest x4 21.5 us: amp(): pl.pallas_call(functools.partial(amp_kernel, half=half, steps=steps, slot...]
    dot_general x10 -> x2, matrix products: 50.6 us -> 5.01 us  [finish(): return jnp.einsum('sbd,dw->sbw', mine, c, preferred_element_type=F32)]
    ppermute x12, starting transfers between devices: 61.2 us -> 18.6 us  [the longest x4 5.61 us: mix(): q = lax.ppermute(s, BOTH, swap(n_occ, 2))]
    all_to_all x1 -> x0, blocking collectives: 33.1 us -> none  [body(): mine = lax.all_to_all(low, 'occ', split_axis=0, concat_axis=0, tiled=True)]
    all_to_all x0 -> x2, waiting for transfers between devices: none -> 24.5 us  [finish(): mine = lax.all_to_all(low, 'occ', split_axis=0, concat_axis=0, tiled=True)]
    all_to_all x0 -> x2, starting transfers between devices: none -> 23.8 us  [finish(): mine = lax.all_to_all(low, 'occ', split_axis=0, concat_axis=0, tiled=True)]
    ppermute x12, waiting for transfers between devices: 75.2 us -> 62.2 us  [the longest x4 25.7 us: mix(): q = lax.ppermute(s, BOTH, swap(n_occ, 2))]
    div x3 -> x0, local copies, waits for them, and re-layouts: 8.06 us -> none  [amp_t(): return integral / (eb[:, None] + ev[None, :] - eo_i - eo_at(k))]
  transfers between devices with their start and end apart: 12 -> 14, of which waited for: 8 -> 11; matrix products, arithmetic and copies ran while one was open for 21% -> 6% of each run, Pallas kernels for 0% -> 22%
where the time goes in v2:
time: 205 us; the launch traced here: 203 us
  waiting for transfers between devices  86.7 us (42%)
  Pallas kernels  55.1 us (27%)
  starting transfers between devices  42.4 us (21%)
  other arithmetic  7.5 us (4%)
  local copies, waits for them, and re-layouts  6.49 us (3%)
  matrix products  5.01 us (2%)
    ppermute x4, waiting for transfers between devices, mix(): q = lax.ppermute(s, BOTH, swap(n_occ, 2))  25.7 us
    all_to_all x2, waiting for transfers between devices, finish(): mine = lax.all_to_all(low, 'occ', split_axis=0, concat_axis=0, tiled=True)  24.5 us
    all_to_all x2, starting transfers between devices, finish(): mine = lax.all_to_all(low, 'occ', split_axis=0, concat_axis=0, tiled=True)  23.8 us
    pallas_call x4, Pallas kernels, amp(): pl.pallas_call(functools.partial(amp_kernel, half=half, steps=steps, slot...  21.5 us
    ppermute x1, waiting for transfers between devices, body(): x1 = lax.ppermute(x0, BOTH, moves(n_occ, round1))  18.6 us
    pallas_call x2, Pallas kernels, last(): pl.pallas_call(functools.partial(last_kernel, n=2), out_shape=(sds((n_occ...  14.5 us
    pallas_call x4, Pallas kernels, mix(): pl.pallas_call(functools.partial(mix_kernel, half=half), out_shape=sds((h...  11.9 us
    ppermute x1, waiting for transfers between devices, body(): x2 = lax.ppermute(x1, BOTH, moves(n_occ, round2))  7.97 us
  transfers between devices with their start and end apart: 14, of which 11 were waited for; matrix products, arithmetic and copies ran while one was open for 6% of the time, Pallas kernels for 22%

profile of v2, /device:TPU:56, one launch (start us, length us, event | category | flops | bytes accessed | tf_op | source)
XLA Modules:
  0.0 203.3 jit_solution(13893453302029923726)
XLA Ops:
  0.0 1.7 dynamic-slice_bitcast_fusion
  3.1 18.6 %collective-permute-done = bf16[384,2048]{1,0:T(8,128)(2,1)} collective-permute-done((bf16[384,2048]{1,0:T(8,128)(2,1)S(1)}, bf16[384,2048]{1,0:T(8,128)(2,1)}, u32[]{:S(2)}, u32[]{:S(2)}) %collective-permute-start) | collective-permute-done | bytes 1572896 | tf_op jit(solution)/shard_map/ppermute | solution.py:138
  21.7 4.1 %collective-permute-start.1 = (bf16[384,2048]{1,0:T(8,128)(2,1)}, bf16[384,2048]{1,0:T(8,128)(2,1)}, u32[]{:S(2)}, u32[]{:S(2)}) collective-permute-start(bf16[384,2048]{1,0:T(8,128)(2,1)} %collective-permute-done), channel_id=1, source_target_pairs={{0,29},{1,4},{2,31},{3,6},{4,1},{5,8},{6,3},{7,10},{8,5},{9,12},{1... | collective-permute-start | bytes 4718600 | tf_op jit(solution)/shard_map/ppermute | solution.py:139
  28.3 1.8 broadcast_select_fusion.x.refs_0_
  30.9 5.4 %amp.4 = (f32[384,384]{1,0:T(8,128)}, bf16[384,384]{1,0:T(8,128)(2,1)}) custom-call(s32[8]{0:T(128)} %stack.35.sc, bf16[768,2048]{1,0:T(8,128)(2,1)} %bitcast.47, bf16[384,2048]{1,0:T(8,128)(2,1)} %broadcast_select_fusion.x.refs_0_, f32[384,128]{1,0:T(8,128)} %broadcast_in_dim.41.evc, f32[1,768]{1,0:T(1,128)} %broadcast_in_dim.42.evr, f32[64]{0:T(128)} %select_reduce_fusion.1.eo), custom_call_target="tpu_custom_call" | custom-call | flops 1207959552 | bytes 4718592 | tf_op jit(solution)/shard_map/amp/pallas_call | solution.py:150
  36.3 8.0 %collective-permute-done.1.x.refs_1_ = bf16[384,2048]{1,0:T(8,128)(2,1)} collective-permute-done((bf16[384,2048]{1,0:T(8,128)(2,1)}, bf16[384,2048]{1,0:T(8,128)(2,1)}, u32[]{:S(2)}, u32[]{:S(2)}) %collective-permute-start.1) | collective-permute-done | bytes 1572896 | tf_op jit(solution)/shard_map/ppermute | solution.py:139
  45.8 5.4 %amp.5 = (f32[384,384]{1,0:T(8,128)}, bf16[384,384]{1,0:T(8,128)(2,1)}) custom-call(s32[8]{0:T(128)} %stack.35.sc, bf16[768,2048]{1,0:T(8,128)(2,1)} %bitcast.48, bf16[384,2048]{1,0:T(8,128)(2,1)} %collective-permute-done.1.x.refs_1_, f32[384,128]{1,0:T(8,128)} %broadcast_in_dim.41.evc, f32[1,768]{1,0:T(1,128)} %broadcast_in_dim.42.evr, ...), custom_call_target="tpu_custom_call" | custom-call | flops 1207959552 | bytes 4718592 | tf_op jit(solution)/shard_map/amp/pallas_call | solution.py:150
  51.2 8.6 %collective-permute-done.3.q = f32[384,384]{1,0:T(8,128)S(1)} collective-permute-done((f32[384,384]{1,0:T(8,128)}, f32[384,384]{1,0:T(8,128)S(1)}, u32[]{:S(2)}, u32[]{:S(2)}) %collective-permute-start.3) | collective-permute-done | bytes 589856 | tf_op jit(solution)/shard_map/ppermute | solution.py:171
  60.6 3.1 %mix.4.refs_2_ = bf16[384,768]{1,0:T(8,128)(2,1)} custom-call(s32[8]{0:T(128)} %stack.35.sc, f32[384,384]{1,0:T(8,128)} %get-tuple-element.37.s, f32[384,384]{1,0:T(8,128)} %copy-done.7, bf16[384,384]{1,0:T(8,128)(2,1)} %get-tuple-element.38.w), custom_call_target="tpu_custom_call" | custom-call | flops 589824 | bytes 2064384 | tf_op jit(solution)/shard_map/mix/pallas_call | solution.py:173
  64.3 3.9 %collective-permute-start.4 = (bf16[384,2048]{1,0:T(8,128)(2,1)S(1)}, bf16[384,2048]{1,0:T(8,128)(2,1)S(1)}, u32[]{:S(2)}, u32[]{:S(2)}) collective-permute-start(bf16[384,2048]{1,0:T(8,128)(2,1)S(1)} %collective-permute-done.2.x.refs_0_), channel_id=1, source_target_pairs={{0,255},{1,4},{2,253},{3,6},{4,1},{5,8},{6,3},{7,10},{8,5},{9,12},... | collective-permute-start | bytes 4718600 | tf_op jit(solution)/shard_map/ppermute | solution.py:193
  69.7 5.4 %amp.6 = (f32[384,384]{1,0:T(8,128)}, bf16[384,384]{1,0:T(8,128)(2,1)}) custom-call(s32[8]{0:T(128)} %stack.35.sc, bf16[768,2048]{1,0:T(8,128)(2,1)} %bitcast.49, bf16[384,2048]{1,0:T(8,128)(2,1)} %copy-done.1, f32[384,128]{1,0:T(8,128)} %broadcast_in_dim.41.evc, f32[1,768]{1,0:T(1,128)} %broadcast_in_dim.42.evr, f32[64]{0:T(128)} %select_reduce_fusion.1.eo), custom_call_target="tpu_custom_call" | custom-call | flops 1207959552 | bytes 4718592 | tf_op jit(solution)/shard_map/amp/pallas_call | solution.py:150
  75.0 6.3 %collective-permute-done.5.q = f32[384,384]{1,0:T(8,128)} collective-permute-done((f32[384,384]{1,0:T(8,128)}, f32[384,384]{1,0:T(8,128)}, u32[]{:S(2)}, u32[]{:S(2)}) %collective-permute-start.5) | collective-permute-done | bytes 589856 | tf_op jit(solution)/shard_map/ppermute | solution.py:171
  81.4 3.0 %mix.5.refs_3_ = bf16[384,768]{1,0:T(8,128)(2,1)} custom-call(s32[8]{0:T(128)} %stack.35.sc, f32[384,384]{1,0:T(8,128)} %get-tuple-element.42.s, f32[384,384]{1,0:T(8,128)} %collective-permute-done.5.q, bf16[384,384]{1,0:T(8,128)(2,1)} %get-tuple-element.43.w), custom_call_target="tpu_custom_call" | custom-call | flops 589824 | bytes 2064384 | tf_op jit(solution)/shard_map/mix/pallas_call | solution.py:173
  84.4 7.2 %gamma.1 = (f32[2048,384]{1,0:T(8,128)}, f32[2048,384]{1,0:T(8,128)}) custom-call(bf16[384,2048]{1,0:T(8,128)(2,1)} %broadcast_select_fusion.x.refs_0_, bf16[384,2048]{1,0:T(8,128)(2,1)} %collective-permute-done.1.x.refs_1_, bf16[384,768]{1,0:T(8,128)(2,1)} %mix.4.refs_2_, bf16[384,768]{1,0:T(8,128)(2,1)} %mix.5.refs_3_), custom_call_target="tpu_custom_call" | custom-call | flops 2415919104 | bytes 9437184 | tf_op jit(solution)/shard_map/gamma/pallas_call | solution.py:199
  91.7 1.6 collective-permute-start.6
  93.3 5.3 %amp.7 = (bf16[384,384]{1,0:T(8,128)(2,1)}, bf16[384,384]{1,0:T(8,128)(2,1)}) custom-call(s32[8]{0:T(128)} %stack.35.sc, bf16[768,2048]{1,0:T(8,128)(2,1)} %bitcast.50, bf16[384,2048]{1,0:T(8,128)(2,1)} %copy-done.2, f32[384,128]{1,0:T(8,128)} %broadcast_in_dim.41.evc, f32[1,768]{1,0:T(1,128)} %broadcast_in_dim.42.evr, f32[64]{0:T(128)} %select_reduce_fusion.1.eo), custom_call_target="tpu_custom_call" | custom-call | flops 1207959552 | bytes 4718592 | tf_op jit(solution)/shard_map/amp/pallas_call | solution.py:150
  99.6 10.7 %collective-permute-done.7.q = bf16[384,384]{1,0:T(8,128)(2,1)S(1)} collective-permute-done((bf16[384,384]{1,0:T(8,128)(2,1)}, bf16[384,384]{1,0:T(8,128)(2,1)S(1)}, u32[]{:S(2)}, u32[]{:S(2)}) %collective-permute-start.7) | collective-permute-done | bytes 294944 | tf_op jit(solution)/shard_map/ppermute | solution.py:171
  111.1 2.8 %mix.7.refs_3_ = bf16[384,768]{1,0:T(8,128)(2,1)} custom-call(s32[8]{0:T(128)} %stack.35.sc, bf16[384,384]{1,0:T(8,128)(2,1)} %get-tuple-element.49.s, bf16[384,384]{1,0:T(8,128)(2,1)} %copy-done.8, bf16[384,384]{1,0:T(8,128)(2,1)} %get-tuple-element.50.w), custom_call_target="tpu_custom_call" | custom-call | flops 589824 | bytes 2064384 | tf_op jit(solution)/shard_map/mix/pallas_call | solution.py:173
  114.7 3.0 %mix.6.refs_2_ = bf16[384,768]{1,0:T(8,128)(2,1)} custom-call(s32[8]{0:T(128)} %stack.35.sc, f32[384,384]{1,0:T(8,128)} %get-tuple-element.47.s, f32[384,384]{1,0:T(8,128)} %copy-done.6, bf16[384,384]{1,0:T(8,128)(2,1)} %get-tuple-element.48.w), custom_call_target="tpu_custom_call" | custom-call | flops 589824 | bytes 2064384 | tf_op jit(solution)/shard_map/mix/pallas_call | solution.py:173
  117.8 7.2 %last.2 = (f32[64,2,8,384]{3,2,1,0:T(8,128)}, f32[64,2,8,384]{3,2,1,0:T(8,128)}) custom-call(s32[8]{0:T(128)} %stack.35.sc, bf16[384,2048]{1,0:T(8,128)(2,1)} %copy-done.1, bf16[384,2048]{1,0:T(8,128)(2,1)} %copy-done.2, bf16[384,768]{1,0:T(8,128)(2,1)} %mix.6.refs_2_, bf16[384,768]{1,0:T(8,128)(2,1)} %mix.7.refs_3_, f32[2048,384]{1,0:T(8,128)} %get-tuple-element.51.refs_4_), custom_call_target="tpu_custom_call" | custom-call | flops 1207959552 | bytes 9437184 | tf_op jit(solution)/shard_map/last/pallas_call | solution.py:217
  124.9 7.3 %last.3 = (f32[64,2,8,384]{3,2,1,0:T(8,128)}, f32[64,2,8,384]{3,2,1,0:T(8,128)}) custom-call(s32[8]{0:T(128)} %stack.35.sc, bf16[384,2048]{1,0:T(8,128)(2,1)} %copy-done.1, bf16[384,2048]{1,0:T(8,128)(2,1)} %copy-done.2, bf16[384,768]{1,0:T(8,128)(2,1)} %mix.6.refs_2_, bf16[384,768]{1,0:T(8,128)(2,1)} %mix.7.refs_3_, f32[2048,384]{1,0:T(8,128)} %get-tuple-element.56.refs_4_), custom_call_target="tpu_custom_call" | custom-call | flops 1207959552 | bytes 9437184 | tf_op jit(solution)/shard_map/last/pallas_call | solution.py:217
  132.9 1.5 collective-permute-start.10
  134.4 1.7 collective-permute-done.9
  137.6 6.5 %collective-permute-done.10 = bf16[64,8,384]{2,1,0:T(8,128)(2,1)S(1)} collective-permute-done((bf16[64,8,384]{2,1,0:T(8,128)(2,1)S(1)}, bf16[64,8,384]{2,1,0:T(8,128)(2,1)S(1)}, u32[]{:S(2)}, u32[]{:S(2)}) %collective-permute-start.10) | collective-permute-done | bytes 393248 | tf_op jit(solution)/shard_map/ppermute | solution.py:248
  144.1 1.5 collective-permute-start.11
  146.5 16.2 %all-to-all-start = ((bf16[64,8,384]{2,1,0:T(8,128)(2,1)}), bf16[64,8,384]{2,1,0:T(8,128)(2,1)S(1)}, u32[]{:S(2)}, u32[]{:S(2)}) async-start(bf16[64,8,384]{2,1,0:T(8,128)(2,1)} %fusion.3), calls=%async_computation | async-start | bytes 786432 | tf_op jit(solution)/shard_map/all_to_all | solution.py:238
  163.7 2.5 %fusion.5 = bf16[64,8,384]{2,1,0:T(8,128)(2,1)} fusion(f32[64,8,384]{2,1,0:T(8,128)} %collective-permute-done.11, f32[64,2,8,384]{3,2,1,0:T(8,128)} %copy-done.5, s32[]{:T(128)S(6)} %select_n.92, f32[64,2,8,384]{3,2,1,0:T(8,128)} %get-tuple-element.57), kind=kLoop, calls=%fused_computation.11 | loop fusion | flops 589824 | bytes 2752516 | tf_op jit(solution)/shard_map/convert_element_type | solution.py:237
  166.2 11.9 %all-to-all-done = bf16[64,8,384]{2,1,0:T(8,128)(2,1)S(1)} async-done(((bf16[64,8,384]{2,1,0:T(8,128)(2,1)}), bf16[64,8,384]{2,1,0:T(8,128)(2,1)S(1)}, u32[]{:S(2)}, u32[]{:S(2)}) %all-to-all-start) | async-done | bytes 393248 | tf_op jit(solution)/shard_map/all_to_all | solution.py:238
  178.1 7.6 %all-to-all-start.1 = ((bf16[64,8,384]{2,1,0:T(8,128)(2,1)}), bf16[64,8,384]{2,1,0:T(8,128)(2,1)S(1)}, u32[]{:S(2)}, u32[]{:S(2)}) async-start(bf16[64,8,384]{2,1,0:T(8,128)(2,1)} %fusion.5), calls=%async_computation.1 | async-start | bytes 786432 | tf_op jit(solution)/shard_map/all_to_all | solution.py:238
  185.7 1.8 fusion.6
  187.6 12.6 %all-to-all-done.1 = bf16[64,8,384]{2,1,0:T(8,128)(2,1)S(1)} async-done(((bf16[64,8,384]{2,1,0:T(8,128)(2,1)}), bf16[64,8,384]{2,1,0:T(8,128)(2,1)S(1)}, u32[]{:S(2)}, u32[]{:S(2)}) %all-to-all-start.1) | async-done | bytes 393248 | tf_op jit(solution)/shard_map/all_to_all | solution.py:238
  200.2 3.2 %convolution_add_fusion = f32[64,8,1024]{2,1,0:T(8,128)} fusion(f32[64,8,1024]{2,1,0:T(8,128)S(1)} %fusion.6, bf16[64,8,384]{2,1,0:T(8,128)(2,1)S(1)} %all-to-all-done.1, bf16[768,1024]{1,0:T(8,128)(2,1)} %param.11), kind=kOutput, calls=%fused_computation | convolution fusion | flops 403177472 | bytes 5373952 | tf_op jit(solution)/shard_map/sbd,dw->sbw/dot_general | solution.py:240
  (47 shorter events, 15.8 us)
Async XLA Ops:
  0.0 25.9 %copy-start.9 = (s32[768]{0:T(1024)S(1)}, s32[768]{0:T(1024)}, u32[]{:S(2)}) copy-start(s32[768]{0:T(1024)} %param.8) | copy-start | bytes 9220
  0.0 25.9 %copy-start.10 = (f32[256]{0:T(256)S(1)}, f32[256]{0:T(256)}, u32[]{:S(2)}) copy-start(f32[256]{0:T(256)} %param.10) | copy-start | bytes 3076
  0.0 27.5 %copy-start.11 = (f32[256]{0:T(256)S(1)}, f32[256]{0:T(256)}, u32[]{:S(2)}) copy-start(f32[256]{0:T(256)} %param.9) | copy-start | bytes 3076
  0.0 27.5 %copy-start.12 = (s32[64]{0:T(128)S(1)}, s32[64]{0:T(128)}, u32[]{:S(2)}) copy-start(s32[64]{0:T(128)} %param.7) | copy-start | bytes 772
  0.0 28.2 %copy-start = (bf16[1,768,2048]{2,1,0:T(8,128)(2,1)S(1)}, bf16[1,768,2048]{2,1,0:T(8,128)(2,1)}, u32[]{:S(2)}) copy-start(bf16[1,768,2048]{2,1,0:T(8,128)(2,1)} %param.6) | copy-start | bytes 9437188
  1.7 20.0 %collective-permute-start = (bf16[384,2048]{1,0:T(8,128)(2,1)S(1)}, bf16[384,2048]{1,0:T(8,128)(2,1)}, u32[]{:S(2)}, u32[]{:S(2)}) collective-permute-start(bf16[384,2048]{1,0:T(8,128)(2,1)S(1)} %dynamic-slice_bitcast_fusion), channel_id=1, source_target_pairs={{0,5},{1,0},{2,7},{3,2},{4,9},{5,36},{6,11},{7,38},{8,13},{9,40},{... | collective-permute-start | bytes 4718600 | tf_op jit(solution)/shard_map/ppermute | solution.py:138
  21.7 22.5 %collective-permute-start.1 = (bf16[384,2048]{1,0:T(8,128)(2,1)}, bf16[384,2048]{1,0:T(8,128)(2,1)}, u32[]{:S(2)}, u32[]{:S(2)}) collective-permute-start(bf16[384,2048]{1,0:T(8,128)(2,1)} %collective-permute-done), channel_id=1, source_target_pairs={{0,29},{1,4},{2,31},{3,6},{4,1},{5,8},{6,3},{7,10},{8,5},{9,12},{1... | collective-permute-start | bytes 4718600 | tf_op jit(solution)/shard_map/ppermute | solution.py:139
  44.3 20.1 %collective-permute-start.2 = (bf16[384,2048]{1,0:T(8,128)(2,1)}, bf16[384,2048]{1,0:T(8,128)(2,1)S(1)}, u32[]{:S(2)}, u32[]{:S(2)}) collective-permute-start(bf16[384,2048]{1,0:T(8,128)(2,1)} %collective-permute-done.1.x.refs_1_), channel_id=1, source_target_pairs={{0,5},{1,254},{2,7},{3,252},{4,9},{5,0},{6,11},{7,2},{8,13},{9,4},... | collective-permute-start | bytes 4718600 | tf_op jit(solution)/shard_map/ppermute | solution.py:189
  44.3 15.5 %collective-permute-start.3 = (f32[384,384]{1,0:T(8,128)}, f32[384,384]{1,0:T(8,128)S(1)}, u32[]{:S(2)}, u32[]{:S(2)}) collective-permute-start(f32[384,384]{1,0:T(8,128)} %get-tuple-element.37.s), channel_id=1, source_target_pairs={{0,2},{1,3},{2,0},{3,1},{4,6},{5,7},{6,4},{7,5},{8,10},{9,11},{10,... | collective-permute-start | bytes 1769480 | tf_op jit(solution)/shard_map/ppermute | solution.py:171
  59.8 0.8 copy-start.7
  64.3 5.3 %copy-start.1 = (bf16[384,2048]{1,0:T(8,128)(2,1)}, bf16[384,2048]{1,0:T(8,128)(2,1)S(1)}, u32[]{:S(2)}) copy-start(bf16[384,2048]{1,0:T(8,128)(2,1)S(1)} %collective-permute-done.2.x.refs_0_) | copy-start | bytes 4718596
  64.3 27.3 %collective-permute-start.4 = (bf16[384,2048]{1,0:T(8,128)(2,1)S(1)}, bf16[384,2048]{1,0:T(8,128)(2,1)S(1)}, u32[]{:S(2)}, u32[]{:S(2)}) collective-permute-start(bf16[384,2048]{1,0:T(8,128)(2,1)S(1)} %collective-permute-done.2.x.refs_0_), channel_id=1, source_target_pairs={{0,255},{1,4},{2,253},{3,6},{4,1},{5,8},{6,3},{7,10},{8,5},{9,12},... | collective-permute-start | bytes 4718600 | tf_op jit(solution)/shard_map/ppermute | solution.py:193
  68.2 13.2 %collective-permute-start.5 = (f32[384,384]{1,0:T(8,128)}, f32[384,384]{1,0:T(8,128)}, u32[]{:S(2)}, u32[]{:S(2)}) collective-permute-start(f32[384,384]{1,0:T(8,128)} %get-tuple-element.42.s), channel_id=1, source_target_pairs={{0,2},{1,3},{2,0},{3,1},{4,6},{5,7},{6,4},{7,5},{8,10},{9,11},{10,... | collective-permute-start | bytes 1769480 | tf_op jit(solution)/shard_map/ppermute | solution.py:171
  91.7 1.6 copy-start.2
  91.7 22.2 %collective-permute-start.6 = (f32[384,384]{1,0:T(8,128)}, f32[384,384]{1,0:T(8,128)S(1)}, u32[]{:S(2)}, u32[]{:S(2)}) collective-permute-start(f32[384,384]{1,0:T(8,128)} %get-tuple-element.47.s), channel_id=1, source_target_pairs={{0,2},{1,3},{2,0},{3,1},{4,6},{5,7},{6,4},{7,5},{8,10},{9,11},{10,... | collective-permute-start | bytes 1769480 | tf_op jit(solution)/shard_map/ppermute | solution.py:171
  98.6 11.8 %collective-permute-start.7 = (bf16[384,384]{1,0:T(8,128)(2,1)}, bf16[384,384]{1,0:T(8,128)(2,1)S(1)}, u32[]{:S(2)}, u32[]{:S(2)}) collective-permute-start(bf16[384,384]{1,0:T(8,128)(2,1)} %get-tuple-element.49.s), channel_id=1, source_target_pairs={{0,2},{1,3},{2,0},{3,1},{4,6},{5,7},{6,4},{7,5},{8,10},{9,11},{10,... | collective-permute-start | bytes 884744 | tf_op jit(solution)/shard_map/ppermute | solution.py:171
  110.3 0.7 copy-start.8
  113.9 0.8 copy-start.6
  124.9 7.3 %collective-permute-start.8 = (f32[64,2,8,384]{3,2,1,0:T(8,128)}, f32[64,2,8,384]{3,2,1,0:T(8,128)S(1)}, u32[]{:S(2)}, u32[]{:S(2)}) collective-permute-start(f32[64,2,8,384]{3,2,1,0:T(8,128)} %get-tuple-element.55), channel_id=1, source_target_pairs={{0,1},{1,0},{2,3},{3,2},{4,5},{5,4},{6,7},{7,6},{8,9},{9,8},{10,11... | collective-permute-start | bytes 4718600 | tf_op jit(solution)/shard_map/ppermute | solution.py:244
  124.9 7.3 %copy-start.3 = (f32[64,2,8,384]{3,2,1,0:T(8,128)S(1)}, f32[64,2,8,384]{3,2,1,0:T(8,128)}, u32[]{:S(2)}) copy-start(f32[64,2,8,384]{3,2,1,0:T(8,128)} %get-tuple-element.52) | copy-start | bytes 4718596
  132.2 4.0 %copy-start.4 = (f32[64,2,8,384]{3,2,1,0:T(8,128)S(1)}, f32[64,2,8,384]{3,2,1,0:T(8,128)}, u32[]{:S(2)}) copy-start(f32[64,2,8,384]{3,2,1,0:T(8,128)} %get-tuple-element.57) | copy-start | bytes 4718596
  132.4 3.8 %collective-permute-start.9 = (f32[64,2,8,384]{3,2,1,0:T(8,128)}, f32[64,2,8,384]{3,2,1,0:T(8,128)S(1)}, u32[]{:S(2)}, u32[]{:S(2)}) collective-permute-start(f32[64,2,8,384]{3,2,1,0:T(8,128)} %get-tuple-element.59), channel_id=1, source_target_pairs={{0,1},{1,0},{2,3},{3,2},{4,5},{5,4},{6,7},{7,6},{8,9},{9,8},{10,11... | collective-permute-start | bytes 4718600 | tf_op jit(solution)/shard_map/ppermute | solution.py:249
  132.9 11.1 %collective-permute-start.10 = (bf16[64,8,384]{2,1,0:T(8,128)(2,1)S(1)}, bf16[64,8,384]{2,1,0:T(8,128)(2,1)S(1)}, u32[]{:S(2)}, u32[]{:S(2)}) collective-permute-start(bf16[64,8,384]{2,1,0:T(8,128)(2,1)S(1)} %fusion.10), channel_id=1, source_target_pairs={{0,2},{1,3},{2,0},{3,1},{4,6},{5,7},{6,4},{7,5},{8,10},{9,11},{10,... | collective-permute-start | bytes 1179656 | tf_op jit(solution)/shard_map/ppermute | solution.py:248
  136.2 1.4 copy-start.5
  144.1 19.7 %collective-permute-start.11 = (f32[64,8,384]{2,1,0:T(8,128)}, f32[64,8,384]{2,1,0:T(8,128)}, u32[]{:S(2)}, u32[]{:S(2)}) collective-permute-start(f32[64,8,384]{2,1,0:T(8,128)} %fusion), channel_id=1, source_target_pairs={{0,2},{1,3},{2,0},{3,1},{4,6},{5,7},{6,4},{7,5},{8,10},{9,11},{10,... | collective-permute-start | bytes 2359304 | tf_op jit(solution)/shard_map/ppermute | solution.py:252
  146.5 31.7 %all-to-all-start = ((bf16[64,8,384]{2,1,0:T(8,128)(2,1)}), bf16[64,8,384]{2,1,0:T(8,128)(2,1)S(1)}, u32[]{:S(2)}, u32[]{:S(2)}) async-start(bf16[64,8,384]{2,1,0:T(8,128)(2,1)} %fusion.3), calls=%async_computation | async-start | bytes 786432 | tf_op jit(solution)/shard_map/all_to_all | solution.py:238
  178.1 22.0 %all-to-all-start.1 = ((bf16[64,8,384]{2,1,0:T(8,128)(2,1)}), bf16[64,8,384]{2,1,0:T(8,128)(2,1)S(1)}, u32[]{:S(2)}, u32[]{:S(2)}) async-start(bf16[64,8,384]{2,1,0:T(8,128)(2,1)} %fusion.5), calls=%async_computation.1 | async-start | bytes 786432 | tf_op jit(solution)/shard_map/all_to_all | solution.py:238

commit v3 on v2

--- a/solution.py
+++ b/solution.py
@@ -6,6 +6,7 @@
 from jax.experimental import pallas as pl
 from jax.experimental.pallas import tpu as pltpu
 from jax.sharding import PartitionSpec as P
+
 
 BOTH = ("occ", "off")
 F32 = jnp.float32
@@ -91,27 +92,44 @@
         w_out[...] = (2.0 * mine - mine.T).astype(BF16)
 
 
-def mix_kernel(sc, s, q, w, o, *, half):
-    h = sc[0]
-    o[:, pl.ds(pl.multiple_of(h * half, half), half)] = w[...]
-    other = 2.0 * s[...].astype(F32) - q[...].astype(F32).T
-    o[:, pl.ds(pl.multiple_of((1 - h) * half, half), half)] = other.astype(BF16)
-
-
-def gamma_kernel(*refs, n, half):
-    xs, ws, outs = refs[:n], refs[n : 2 * n], refs[2 * n :]
+def fill(w, h, group, half, s, q, v):
+    def put(g, at):
+        @pl.when(h == g)
+        def _():
+            w[:, at : at + half] = v[...]
+
+        @pl.when(h != g)
+        def _():
+            w[:, at : at + half] = (2.0 * s[...].astype(F32) - q[...].astype(F32).T).astype(BF16)
+
+    for at, g in enumerate(group):
+        put(g, at * half)
+
+
+def gamma_kernel(sc, *refs, n, half, early):
+    xs, mixes, refs = refs[:n], refs[n : 4 * n], refs[4 * n :]
+    before = refs[:2] if early else None
+    outs, ws = refs[2 if early else 0 :][:2], refs[4 if early else 2 :]
+
+    @pl.when(pl.program_id(0) == 0)
+    def _():
+        for k in range(n):
+            fill(ws[k], sc[0], (0, 1), half, *mixes[3 * k : 3 * k + 3])
+
     res = lax.dot_general(xs[0][...], ws[0][...], TN, preferred_element_type=F32)
     for k in range(1, n):
         res += lax.dot_general(xs[k][...], ws[k][...], TN, preferred_element_type=F32)
-    outs[0][...] = res[:, :half]
-    outs[1][...] = res[:, half:]
-
-
-def last_kernel(sc, *refs, n):
-    xs, ws, early, keep, send = refs[:n], refs[n : 2 * n], refs[2 * n], refs[2 * n + 1], refs[2 * n + 2]
-    res = early[...]
-    for k in range(n):
-        res += lax.dot_general(xs[k][...], ws[k][...], TN, preferred_element_type=F32)
+    for g in range(2):
+        term = res[:, g * half : (g + 1) * half]
+        outs[g][...] = term + before[g][...] if early else term
+
+
+def last_kernel(sc, x, s, q, v, early, keep, send, w, *, half, group):
+    @pl.when(pl.program_id(0) == 0)
+    def _():
+        fill(w, sc[0], (group,), half, s, q, v)
+
+    res = early[...] + lax.dot_general(x[...], w[...], TN, preferred_element_type=F32)
     res = res.reshape(res.shape[0] // 32, 2, 2, 8, res.shape[1])
     a, b = res[:, :, 0], res[:, :, 1]
     first = sc[1] == 0
@@ -167,67 +185,68 @@
             name="amp",
         )(sc, own, x, evc, evr, eo)
 
-    def mix(s, w):
-        q = lax.ppermute(s, BOTH, swap(n_occ, 2))
-        whole = pl.BlockSpec((half, half), lambda t, s: (0, 0))
+    def exchange(s):
+        return lax.ppermute(s, BOTH, swap(n_occ, 2))
+
+    def ring(x, rule):
+        return lax.ppermute(x, BOTH, moves(n_occ, rule))
+
+    tiles = 4
+    tile_p = n_aux // tiles
+    whole = pl.BlockSpec((half, half), lambda t, s: (0, 0))
+    x_spec = pl.BlockSpec((half, tile_p), lambda t, s: (0, t))
+    row_spec = pl.BlockSpec((tile_p, half), lambda t, s: (t, 0))
+
+    def gamma(xs, mixes, early=None):
+        n = len(xs)
         return pl.pallas_call(
-            functools.partial(mix_kernel, half=half),
-            out_shape=sds((half, n_vir), BF16),
+            functools.partial(gamma_kernel, n=n, half=half, early=early is not None),
+            out_shape=(sds((n_aux, half), F32),) * 2,
             grid_spec=pltpu.PrefetchScalarGridSpec(
                 num_scalar_prefetch=1,
-                grid=(1,),
-                in_specs=[whole] * 3,
-                out_specs=pl.BlockSpec((half, n_vir), lambda t, s: (0, 0)),
+                grid=(tiles,),
+                in_specs=[x_spec] * n + [whole] * (3 * n) + ([] if early is None else [row_spec] * 2),
+                out_specs=[row_spec] * 2,
+                scratch_shapes=[pltpu.VMEM((half, n_vir), BF16)] * n,
             ),
-            cost_estimate=cost(half * half * 4, half * half * 14),
-            name="mix",
-        )(sc, s, q, w)
+            cost_estimate=cost(2 * n * n_aux * half * n_vir, 2 * n * n_aux * half + 4 * n_aux * n_vir),
+            name="gamma",
+        )(sc, *xs, *(m for mix in mixes for m in mix), *(early or ()))
 
     y1 = jnp.where(core == 0, x0, x1)
     s1, v1 = amp(y1, 0, F32)
-    x2, s1 = lax.optimization_barrier((x2, s1))
-    x3 = lax.ppermute(x2, BOTH, moves(n_occ, round3))
+    q1 = exchange(s1)
+    x2, _ = lax.optimization_barrier((x2, s1))
+    x3 = ring(x2, round3)
     s2, v2 = amp(x2, 1, F32)
-    w1 = mix(s1, v1)
-    x3, s2, w1 = lax.optimization_barrier((x3, s2, w1))
-    x4 = lax.ppermute(x3, BOTH, moves(n_occ, round4))
+    q2 = exchange(s2)
+    x3, _ = lax.optimization_barrier((x3, s2))
+    x4 = ring(x3, round4)
     s3, v3 = amp(x3, 2, F32)
-    w2 = mix(s2, v2)
-
-    tiles = 4
-    tile_p = n_aux // tiles
-    early = pl.pallas_call(
-        functools.partial(gamma_kernel, n=2, half=half),
-        out_shape=(sds((n_aux, half), F32),) * 2,
-        grid=(tiles,),
-        in_specs=[pl.BlockSpec((half, tile_p), lambda t: (0, t))] * 2
-        + [pl.BlockSpec((half, n_vir), lambda t: (0, 0))] * 2,
-        out_specs=[pl.BlockSpec((tile_p, half), lambda t: (t, 0))] * 2,
-        cost_estimate=cost(4 * n_aux * half * n_vir, 4 * n_aux * half + 4 * n_aux * n_vir),
-        name="gamma",
-    )(y1, x2, w1, w2)
-    x4, s3, early = lax.optimization_barrier((x4, s3, early))
+    q3 = exchange(s3)
+    early = gamma([y1, x2], [(s1, q1, v1), (s2, q2, v2)])
+    x4, _, early = lax.optimization_barrier((x4, s3, early))
     s4, v4 = amp(x4, 3, BF16)
-    w3 = mix(s3, v3)
-    w4 = mix(s4, v4)
+    q4 = exchange(s4)
+    v3, _ = lax.optimization_barrier((v3, s4))
+    early = gamma([x3], [(s3, q3, v3)], early)
 
     groups = tile_p // 32
 
     def last(g, early):
         return pl.pallas_call(
-            functools.partial(last_kernel, n=2),
+            functools.partial(last_kernel, half=half, group=g),
             out_shape=(sds((n_occ, 2, 8, half), F32),) * 2,
             grid_spec=pltpu.PrefetchScalarGridSpec(
                 num_scalar_prefetch=1,
                 grid=(tiles,),
-                in_specs=[pl.BlockSpec((half, tile_p), lambda t, s: (0, t))] * 2
-                + [pl.BlockSpec((half, half), lambda t, s: (0, g))] * 2
-                + [pl.BlockSpec((tile_p, half), lambda t, s: (t, 0))],
+                in_specs=[x_spec] + [whole] * 3 + [row_spec],
                 out_specs=[pl.BlockSpec((groups, 2, 8, half), lambda t, s: (t, 0, 0, 0))] * 2,
+                scratch_shapes=[pltpu.VMEM((half, half), BF16)],
             ),
-            cost_estimate=cost(2 * n_aux * half * n_vir, 4 * n_aux * (n_vir + half)),
+            cost_estimate=cost(n_aux * half * n_vir, 2 * n_aux * (n_vir + half)),
             name="last",
-        )(sc, x3, x4, w3, w4, early)
+        )(sc, x4, s4, q4, v4, early)
 
     def part(keep, got, c):
         a = lax.dynamic_index_in_dim(keep, c, 1, keepdims=False)

time: 205 us -> 206 us (level)
  waiting for transfers between devices: 86.7 us -> 97.5 us
  starting transfers between devices: 42.4 us -> 35.4 us
  Pallas kernels: 55.1 us -> 52.4 us
    ppermute x6, waiting for transfers between devices: 26.3 us -> 34.8 us  [the longest x4 20.2 us: exchange(): return lax.ppermute(s, BOTH, swap(n_occ, 2))]
    ppermute x1, waiting for transfers between devices: 1.03 us -> 9.42 us  [body(): far1 = lax.ppermute(away1, BOTH, swap(n_occ, 2))]
    all_to_all x2, waiting for transfers between devices: 24.5 us -> 17.5 us  [finish(): mine = lax.all_to_all(low, 'occ', split_axis=0, concat_axis=0, tiled=True)]
    all_to_all x2, starting transfers between devices: 23.8 us -> 19.4 us  [finish(): mine = lax.all_to_all(low, 'occ', split_axis=0, concat_axis=0, tiled=True)]
    pallas_call x7 -> x4, Pallas kernels: 33.6 us -> 30.8 us  [the longest x2 17.8 us: gamma(): pl.pallas_call(functools.partial(gamma_kernel, n=n, half=half, early=earl...]
  transfers between devices with their start and end apart: 14 -> 14, of which waited for: 11 -> 10; matrix products, arithmetic and copies ran while one was open for 6% -> 6% of each run, Pallas kernels for 22% -> 23%
where the time goes in v3:
time: 206 us; the launch traced here: 204 us
  waiting for transfers between devices  97.5 us (47%)
  Pallas kernels  52.4 us (25%)
  starting transfers between devices  35.4 us (17%)
  other arithmetic  7.33 us (4%)
  local copies, waits for them, and re-layouts  6.02 us (3%)
  matrix products  5.01 us (2%)
    pallas_call x4, Pallas kernels, amp(): pl.pallas_call(functools.partial(amp_kernel, half=half, steps=steps, slot...  21.6 us
    ppermute x4, waiting for transfers between devices, exchange(): return lax.ppermute(s, BOTH, swap(n_occ, 2))  20.2 us
    all_to_all x2, starting transfers between devices, finish(): mine = lax.all_to_all(low, 'occ', split_axis=0, concat_axis=0, tiled=True)  19.4 us
    ppermute x1, waiting for transfers between devices, body(): x1 = lax.ppermute(x0, BOTH, moves(n_occ, round1))  18.6 us
    pallas_call x2, Pallas kernels, gamma(): pl.pallas_call(functools.partial(gamma_kernel, n=n, half=half, early=earl...  17.8 us
    all_to_all x2, waiting for transfers between devices, finish(): mine = lax.all_to_all(low, 'occ', split_axis=0, concat_axis=0, tiled=True)  17.5 us
    ppermute x2, waiting for transfers between devices, ring(): return lax.ppermute(x, BOTH, moves(n_occ, rule))  14.6 us
    pallas_call x2, Pallas kernels, last(): pl.pallas_call(functools.partial(last_kernel, half=half, group=g), out_sh...  13 us
  transfers between devices with their start and end apart: 14, of which 10 were waited for; matrix products, arithmetic and copies ran while one was open for 6% of the time, Pallas kernels for 23%

profile of v3, /device:TPU:56, one launch (start us, length us, event | category | flops | bytes accessed | tf_op | source)
XLA Modules:
  0.0 203.8 jit_solution(1128919892840891827)
XLA Ops:
  0.0 1.7 dynamic-slice_bitcast_fusion
  1.7 1.4 collective-permute-start
  3.1 18.6 %collective-permute-done = bf16[384,2048]{1,0:T(8,128)(2,1)} collective-permute-done((bf16[384,2048]{1,0:T(8,128)(2,1)S(1)}, bf16[384,2048]{1,0:T(8,128)(2,1)}, u32[]{:S(2)}, u32[]{:S(2)}) %collective-permute-start) | collective-permute-done | bytes 1572896 | tf_op jit(solution)/shard_map/ppermute | solution.py:156
  21.7 4.1 %collective-permute-start.1 = (bf16[384,2048]{1,0:T(8,128)(2,1)}, bf16[384,2048]{1,0:T(8,128)(2,1)}, u32[]{:S(2)}, u32[]{:S(2)}) collective-permute-start(bf16[384,2048]{1,0:T(8,128)(2,1)} %collective-permute-done), channel_id=1, source_target_pairs={{0,29},{1,4},{2,31},{3,6},{4,1},{5,8},{6,3},{7,10},{8,5},{9,12},{1... | collective-permute-start | bytes 4718600 | tf_op jit(solution)/shard_map/ppermute | solution.py:157
  28.3 1.8 broadcast_select_fusion.x.refs_0_
  30.8 5.4 %amp.4 = (f32[384,384]{1,0:T(8,128)}, bf16[384,384]{1,0:T(8,128)(2,1)}) custom-call(s32[8]{0:T(128)} %stack.35.sc, bf16[768,2048]{1,0:T(8,128)(2,1)} %bitcast.47, bf16[384,2048]{1,0:T(8,128)(2,1)} %broadcast_select_fusion.x.refs_0_, f32[384,128]{1,0:T(8,128)} %broadcast_in_dim.41.evc, f32[1,768]{1,0:T(1,128)} %broadcast_in_dim.42.evr, f32[64]{0:T(128)} %select_reduce_fusion.1.eo), custom_call_target="tpu_custom_call" | custom-call | flops 1207959552 | bytes 4718592 | tf_op jit(solution)/shard_map/amp/pallas_call | solution.py:168
  36.3 8.0 %collective-permute-done.1.x.refs_1_ = bf16[384,2048]{1,0:T(8,128)(2,1)} collective-permute-done((bf16[384,2048]{1,0:T(8,128)(2,1)}, bf16[384,2048]{1,0:T(8,128)(2,1)}, u32[]{:S(2)}, u32[]{:S(2)}) %collective-permute-start.1) | collective-permute-done | bytes 1572896 | tf_op jit(solution)/shard_map/ppermute | solution.py:157
  44.3 5.5 %amp.5 = (f32[384,384]{1,0:T(8,128)}, bf16[384,384]{1,0:T(8,128)(2,1)}) custom-call(s32[8]{0:T(128)} %stack.35.sc, bf16[768,2048]{1,0:T(8,128)(2,1)} %bitcast.48, bf16[384,2048]{1,0:T(8,128)(2,1)} %collective-permute-done.1.x.refs_1_, f32[384,128]{1,0:T(8,128)} %broadcast_in_dim.41.evc, f32[1,768]{1,0:T(1,128)} %broadcast_in_dim.42.evr, ...), custom_call_target="tpu_custom_call" | custom-call | flops 1207959552 | bytes 4718592 | tf_op jit(solution)/shard_map/amp/pallas_call | solution.py:168
  49.7 14.6 %collective-permute-done.2.x.refs_0_ = bf16[384,2048]{1,0:T(8,128)(2,1)S(1)} collective-permute-done((bf16[384,2048]{1,0:T(8,128)(2,1)}, bf16[384,2048]{1,0:T(8,128)(2,1)S(1)}, u32[]{:S(2)}, u32[]{:S(2)}) %collective-permute-start.2) | collective-permute-done | bytes 1572896 | tf_op jit(solution)/shard_map/ppermute | solution.py:192
  64.3 3.9 %collective-permute-start.3 = (bf16[384,2048]{1,0:T(8,128)(2,1)S(1)}, bf16[384,2048]{1,0:T(8,128)(2,1)S(1)}, u32[]{:S(2)}, u32[]{:S(2)}) collective-permute-start(bf16[384,2048]{1,0:T(8,128)(2,1)S(1)} %collective-permute-done.2.x.refs_0_), channel_id=1, source_target_pairs={{0,255},{1,4},{2,253},{3,6},{4,1},{5,8},{6,3},{7,10},{8,5},{9,12},... | collective-permute-start | bytes 4718600 | tf_op jit(solution)/shard_map/ppermute | solution.py:192
  68.2 1.5 collective-permute-start.4
  70.2 5.4 %amp.6 = (f32[384,384]{1,0:T(8,128)}, bf16[384,384]{1,0:T(8,128)(2,1)}) custom-call(s32[8]{0:T(128)} %stack.35.sc, bf16[768,2048]{1,0:T(8,128)(2,1)} %bitcast.49, bf16[384,2048]{1,0:T(8,128)(2,1)} %copy-done.2, f32[384,128]{1,0:T(8,128)} %broadcast_in_dim.41.evc, f32[1,768]{1,0:T(1,128)} %broadcast_in_dim.42.evr, f32[64]{0:T(128)} %select_reduce_fusion.1.eo), custom_call_target="tpu_custom_call" | custom-call | flops 1207959552 | bytes 4718592 | tf_op jit(solution)/shard_map/amp/pallas_call | solution.py:168
  75.6 1.5 collective-permute-start.7
  77.1 7.6 %collective-permute-done.4.refs_3_ = f32[384,384]{1,0:T(8,128)} collective-permute-done((f32[384,384]{1,0:T(8,128)}, f32[384,384]{1,0:T(8,128)}, u32[]{:S(2)}, u32[]{:S(2)}) %collective-permute-start.4) | collective-permute-done | bytes 589856 | tf_op jit(solution)/shard_map/ppermute | solution.py:189
  84.7 12.6 %collective-permute-done.5.refs_6_ = f32[384,384]{1,0:T(8,128)} collective-permute-done((f32[384,384]{1,0:T(8,128)}, f32[384,384]{1,0:T(8,128)}, u32[]{:S(2)}, u32[]{:S(2)}) %collective-permute-start.5) | collective-permute-done | bytes 589856 | tf_op jit(solution)/shard_map/ppermute | solution.py:189
  97.3 9.0 %gamma.2 = (f32[2048,384]{1,0:T(8,128)}, f32[2048,384]{1,0:T(8,128)}) custom-call(s32[8]{0:T(128)} %stack.35.sc, bf16[384,2048]{1,0:T(8,128)(2,1)} %broadcast_select_fusion.x.refs_0_, bf16[384,2048]{1,0:T(8,128)(2,1)} %collective-permute-done.1.x.refs_1_, f32[384,384]{1,0:T(8,128)} %get-tuple-element.33.refs_2_, f32[384,384]{1,0:T(8,128)} %collective-permute-done.4.refs_3_, ...), custom_call_target="tpu_custom_call" | custom-call | flops 2415919104 | bytes 9437184 | tf_op jit(solution)/shard_map/gamma/pallas_call | solution.py:202
  106.3 1.1 copy-done.1
  107.5 5.3 %amp.7 = (bf16[384,384]{1,0:T(8,128)(2,1)}, bf16[384,384]{1,0:T(8,128)(2,1)}) custom-call(s32[8]{0:T(128)} %stack.35.sc, bf16[768,2048]{1,0:T(8,128)(2,1)} %bitcast.50, bf16[384,2048]{1,0:T(8,128)(2,1)} %copy-done.1, f32[384,128]{1,0:T(8,128)} %broadcast_in_dim.41.evc, f32[1,768]{1,0:T(1,128)} %broadcast_in_dim.42.evr, f32[64]{0:T(128)} %select_reduce_fusion.1.eo), custom_call_target="tpu_custom_call" | custom-call | flops 1207959552 | bytes 4718592 | tf_op jit(solution)/shard_map/amp/pallas_call | solution.py:168
  112.8 1.5 collective-permute-start.6
  114.3 8.8 %gamma.3 = (f32[2048,384]{1,0:T(8,128)}, f32[2048,384]{1,0:T(8,128)}) custom-call(s32[8]{0:T(128)} %stack.35.sc, bf16[384,2048]{1,0:T(8,128)(2,1)} %copy-done.2, f32[384,384]{1,0:T(8,128)} %get-tuple-element.37.refs_1_, f32[384,384]{1,0:T(8,128)} %collective-permute-done.7.refs_2_, bf16[384,384]{1,0:T(8,128)(2,1)} %get-tuple-element.46.refs_3_, ...), custom_call_target="tpu_custom_call" | custom-call | flops 1207959552 | bytes 7864320 | tf_op jit(solution)/shard_map/gamma/pallas_call | solution.py:202
  123.8 6.3 %last.2 = (f32[64,2,8,384]{3,2,1,0:T(8,128)}, f32[64,2,8,384]{3,2,1,0:T(8,128)}) custom-call(s32[8]{0:T(128)} %stack.35.sc, bf16[384,2048]{1,0:T(8,128)(2,1)} %copy-done.1, bf16[384,384]{1,0:T(8,128)(2,1)} %get-tuple-element.43.s, bf16[384,384]{1,0:T(8,128)(2,1)} %copy-done.6, bf16[384,384]{1,0:T(8,128)(2,1)} %get-tuple-element.44.v, ...), custom_call_target="tpu_custom_call" | custom-call | flops 603979776 | bytes 4718592 | tf_op jit(solution)/shard_map/last/pallas_call | solution.py:237
  130.2 6.6 %last.3 = (f32[64,2,8,384]{3,2,1,0:T(8,128)}, f32[64,2,8,384]{3,2,1,0:T(8,128)}) custom-call(s32[8]{0:T(128)} %stack.35.sc, bf16[384,2048]{1,0:T(8,128)(2,1)} %copy-done.1, bf16[384,384]{1,0:T(8,128)(2,1)} %get-tuple-element.43.s, bf16[384,384]{1,0:T(8,128)(2,1)} %copy-done.6, bf16[384,384]{1,0:T(8,128)(2,1)} %get-tuple-element.44.v, ...), custom_call_target="tpu_custom_call" | custom-call | flops 603979776 | bytes 4718592 | tf_op jit(solution)/shard_map/last/pallas_call | solution.py:237
  138.0 2.7 %collective-permute-done.9 = f32[64,2,8,384]{3,2,1,0:T(8,128)S(1)} collective-permute-done((f32[64,2,8,384]{3,2,1,0:T(8,128)}, f32[64,2,8,384]{3,2,1,0:T(8,128)S(1)}, u32[]{:S(2)}, u32[]{:S(2)}) %collective-permute-start.9) | collective-permute-done | bytes 1572896 | tf_op jit(solution)/shard_map/ppermute | solution.py:268
  142.2 6.5 %collective-permute-done.10 = bf16[64,8,384]{2,1,0:T(8,128)(2,1)S(1)} collective-permute-done((bf16[64,8,384]{2,1,0:T(8,128)(2,1)S(1)}, bf16[64,8,384]{2,1,0:T(8,128)(2,1)S(1)}, u32[]{:S(2)}, u32[]{:S(2)}) %collective-permute-start.10) | collective-permute-done | bytes 393248 | tf_op jit(solution)/shard_map/ppermute | solution.py:267
  150.0 11.4 %all-to-all-start = ((bf16[64,8,384]{2,1,0:T(8,128)(2,1)}), bf16[64,8,384]{2,1,0:T(8,128)(2,1)S(1)}, u32[]{:S(2)}, u32[]{:S(2)}) async-start(bf16[64,8,384]{2,1,0:T(8,128)(2,1)} %fusion.3), calls=%async_computation | async-start | bytes 786432 | tf_op jit(solution)/shard_map/all_to_all | solution.py:257
  161.4 9.4 %collective-permute-done.11 = f32[64,8,384]{2,1,0:T(8,128)} collective-permute-done((f32[64,8,384]{2,1,0:T(8,128)}, f32[64,8,384]{2,1,0:T(8,128)}, u32[]{:S(2)}, u32[]{:S(2)}) %collective-permute-start.11) | collective-permute-done | bytes 786464 | tf_op jit(solution)/shard_map/ppermute | solution.py:271
  170.9 2.5 %fusion.5 = bf16[64,8,384]{2,1,0:T(8,128)(2,1)} fusion(f32[64,8,384]{2,1,0:T(8,128)} %collective-permute-done.11, f32[64,2,8,384]{3,2,1,0:T(8,128)} %copy-done.5, s32[]{:T(128)S(6)} %select_n.92, f32[64,2,8,384]{3,2,1,0:T(8,128)} %get-tuple-element.55), kind=kLoop, calls=%fused_computation.11 | loop fusion | flops 589824 | bytes 2752516 | tf_op jit(solution)/shard_map/convert_element_type | solution.py:256
  173.3 4.8 %all-to-all-done = bf16[64,8,384]{2,1,0:T(8,128)(2,1)S(1)} async-done(((bf16[64,8,384]{2,1,0:T(8,128)(2,1)}), bf16[64,8,384]{2,1,0:T(8,128)(2,1)S(1)}, u32[]{:S(2)}, u32[]{:S(2)}) %all-to-all-start) | async-done | bytes 393248 | tf_op jit(solution)/shard_map/all_to_all | solution.py:257
  178.1 7.9 %all-to-all-start.1 = ((bf16[64,8,384]{2,1,0:T(8,128)(2,1)}), bf16[64,8,384]{2,1,0:T(8,128)(2,1)S(1)}, u32[]{:S(2)}, u32[]{:S(2)}) async-start(bf16[64,8,384]{2,1,0:T(8,128)(2,1)} %fusion.5), calls=%async_computation.1 | async-start | bytes 786432 | tf_op jit(solution)/shard_map/all_to_all | solution.py:257
  186.0 1.8 fusion.6
  187.9 12.7 %all-to-all-done.1 = bf16[64,8,384]{2,1,0:T(8,128)(2,1)S(1)} async-done(((bf16[64,8,384]{2,1,0:T(8,128)(2,1)}), bf16[64,8,384]{2,1,0:T(8,128)(2,1)S(1)}, u32[]{:S(2)}, u32[]{:S(2)}) %all-to-all-start.1) | async-done | bytes 393248 | tf_op jit(solution)/shard_map/all_to_all | solution.py:257
  200.6 3.2 %convolution_add_fusion = f32[64,8,1024]{2,1,0:T(8,128)} fusion(f32[64,8,1024]{2,1,0:T(8,128)S(1)} %fusion.6, bf16[64,8,384]{2,1,0:T(8,128)(2,1)S(1)} %all-to-all-done.1, bf16[768,1024]{1,0:T(8,128)(2,1)} %param.11), kind=kOutput, calls=%fused_computation | convolution fusion | flops 403177472 | bytes 5373952 | tf_op jit(solution)/shard_map/sbd,dw->sbw/dot_general | solution.py:259
  (40 shorter events, 8.5 us)
Async XLA Ops:
  0.0 25.9 %copy-start.7 = (s32[768]{0:T(1024)S(1)}, s32[768]{0:T(1024)}, u32[]{:S(2)}) copy-start(s32[768]{0:T(1024)} %param.8) | copy-start | bytes 9220
  0.0 25.9 %copy-start.8 = (f32[256]{0:T(256)S(1)}, f32[256]{0:T(256)}, u32[]{:S(2)}) copy-start(f32[256]{0:T(256)} %param.10) | copy-start | bytes 3076
  0.0 27.5 %copy-start.9 = (f32[256]{0:T(256)S(1)}, f32[256]{0:T(256)}, u32[]{:S(2)}) copy-start(f32[256]{0:T(256)} %param.9) | copy-start | bytes 3076
  0.0 27.5 %copy-start.10 = (s32[64]{0:T(128)S(1)}, s32[64]{0:T(128)}, u32[]{:S(2)}) copy-start(s32[64]{0:T(128)} %param.7) | copy-start | bytes 772
  0.0 28.3 %copy-start = (bf16[1,768,2048]{2,1,0:T(8,128)(2,1)S(1)}, bf16[1,768,2048]{2,1,0:T(8,128)(2,1)}, u32[]{:S(2)}) copy-start(bf16[1,768,2048]{2,1,0:T(8,128)(2,1)} %param.6) | copy-start | bytes 9437188
  1.7 20.0 %collective-permute-start = (bf16[384,2048]{1,0:T(8,128)(2,1)S(1)}, bf16[384,2048]{1,0:T(8,128)(2,1)}, u32[]{:S(2)}, u32[]{:S(2)}) collective-permute-start(bf16[384,2048]{1,0:T(8,128)(2,1)S(1)} %dynamic-slice_bitcast_fusion), channel_id=1, source_target_pairs={{0,5},{1,0},{2,7},{3,2},{4,9},{5,36},{6,11},{7,38},{8,13},{9,40},{... | collective-permute-start | bytes 4718600 | tf_op jit(solution)/shard_map/ppermute | solution.py:156
  21.7 22.5 %collective-permute-start.1 = (bf16[384,2048]{1,0:T(8,128)(2,1)}, bf16[384,2048]{1,0:T(8,128)(2,1)}, u32[]{:S(2)}, u32[]{:S(2)}) collective-permute-start(bf16[384,2048]{1,0:T(8,128)(2,1)} %collective-permute-done), channel_id=1, source_target_pairs={{0,29},{1,4},{2,31},{3,6},{4,1},{5,8},{6,3},{7,10},{8,5},{9,12},{1... | collective-permute-start | bytes 4718600 | tf_op jit(solution)/shard_map/ppermute | solution.py:157
  44.3 20.1 %collective-permute-start.2 = (bf16[384,2048]{1,0:T(8,128)(2,1)}, bf16[384,2048]{1,0:T(8,128)(2,1)S(1)}, u32[]{:S(2)}, u32[]{:S(2)}) collective-permute-start(bf16[384,2048]{1,0:T(8,128)(2,1)} %collective-permute-done.1.x.refs_1_), channel_id=1, source_target_pairs={{0,5},{1,254},{2,7},{3,252},{4,9},{5,0},{6,11},{7,2},{8,13},{9,4},... | collective-permute-start | bytes 4718600 | tf_op jit(solution)/shard_map/ppermute | solution.py:192
  64.3 5.9 %copy-start.2 = (bf16[384,2048]{1,0:T(8,128)(2,1)}, bf16[384,2048]{1,0:T(8,128)(2,1)S(1)}, u32[]{:S(2)}) copy-start(bf16[384,2048]{1,0:T(8,128)(2,1)S(1)} %collective-permute-done.2.x.refs_0_) | copy-start | bytes 4718596
  64.3 42.0 %collective-permute-start.3 = (bf16[384,2048]{1,0:T(8,128)(2,1)S(1)}, bf16[384,2048]{1,0:T(8,128)(2,1)S(1)}, u32[]{:S(2)}, u32[]{:S(2)}) collective-permute-start(bf16[384,2048]{1,0:T(8,128)(2,1)S(1)} %collective-permute-done.2.x.refs_0_), channel_id=1, source_target_pairs={{0,255},{1,4},{2,253},{3,6},{4,1},{5,8},{6,3},{7,10},{8,5},{9,12},... | collective-permute-start | bytes 4718600 | tf_op jit(solution)/shard_map/ppermute | solution.py:192
  68.2 16.5 %collective-permute-start.4 = (f32[384,384]{1,0:T(8,128)}, f32[384,384]{1,0:T(8,128)}, u32[]{:S(2)}, u32[]{:S(2)}) collective-permute-start(f32[384,384]{1,0:T(8,128)} %get-tuple-element.33.refs_2_), channel_id=1, source_target_pairs={{0,2},{1,3},{2,0},{3,1},{4,6},{5,7},{6,4},{7,5},{8,10},{9,11},{10,... | collective-permute-start | bytes 1769480 | tf_op jit(solution)/shard_map/ppermute | solution.py:189
  69.7 27.7 %collective-permute-start.5 = (f32[384,384]{1,0:T(8,128)}, f32[384,384]{1,0:T(8,128)}, u32[]{:S(2)}, u32[]{:S(2)}) collective-permute-start(f32[384,384]{1,0:T(8,128)} %get-tuple-element.35.refs_5_), channel_id=1, source_target_pairs={{0,2},{1,3},{2,0},{3,1},{4,6},{5,7},{6,4},{7,5},{8,10},{9,11},{10,... | collective-permute-start | bytes 1769480 | tf_op jit(solution)/shard_map/ppermute | solution.py:189
  75.6 38.6 %collective-permute-start.7 = (f32[384,384]{1,0:T(8,128)}, f32[384,384]{1,0:T(8,128)}, u32[]{:S(2)}, u32[]{:S(2)}) collective-permute-start(f32[384,384]{1,0:T(8,128)} %get-tuple-element.37.refs_1_), channel_id=1, source_target_pairs={{0,2},{1,3},{2,0},{3,1},{4,6},{5,7},{6,4},{7,5},{8,10},{9,11},{10,... | collective-permute-start | bytes 1769480 | tf_op jit(solution)/shard_map/ppermute | solution.py:189
  106.3 1.1 copy-start.1
  112.8 10.3 %collective-permute-start.6 = (bf16[384,384]{1,0:T(8,128)(2,1)}, bf16[384,384]{1,0:T(8,128)(2,1)S(1)}, u32[]{:S(2)}, u32[]{:S(2)}) collective-permute-start(bf16[384,384]{1,0:T(8,128)(2,1)} %get-tuple-element.43.s), channel_id=1, source_target_pairs={{0,2},{1,3},{2,0},{3,1},{4,6},{5,7},{6,4},{7,5},{8,10},{9,11},{10,... | collective-permute-start | bytes 884744 | tf_op jit(solution)/shard_map/ppermute | solution.py:189
  123.1 0.7 copy-start.6
  130.2 6.6 %collective-permute-start.8 = (f32[64,2,8,384]{3,2,1,0:T(8,128)}, f32[64,2,8,384]{3,2,1,0:T(8,128)S(1)}, u32[]{:S(2)}, u32[]{:S(2)}) collective-permute-start(f32[64,2,8,384]{3,2,1,0:T(8,128)} %get-tuple-element.53), channel_id=1, source_target_pairs={{0,1},{1,0},{2,3},{3,2},{4,5},{5,4},{6,7},{7,6},{8,9},{9,8},{10,11... | collective-permute-start | bytes 4718600 | tf_op jit(solution)/shard_map/ppermute | solution.py:263
  130.2 6.6 %copy-start.3 = (f32[64,2,8,384]{3,2,1,0:T(8,128)S(1)}, f32[64,2,8,384]{3,2,1,0:T(8,128)}, u32[]{:S(2)}) copy-start(f32[64,2,8,384]{3,2,1,0:T(8,128)} %get-tuple-element.50) | copy-start | bytes 4718596
  136.8 4.0 %copy-start.4 = (f32[64,2,8,384]{3,2,1,0:T(8,128)S(1)}, f32[64,2,8,384]{3,2,1,0:T(8,128)}, u32[]{:S(2)}) copy-start(f32[64,2,8,384]{3,2,1,0:T(8,128)} %get-tuple-element.55) | copy-start | bytes 4718596
  136.9 3.8 %collective-permute-start.9 = (f32[64,2,8,384]{3,2,1,0:T(8,128)}, f32[64,2,8,384]{3,2,1,0:T(8,128)S(1)}, u32[]{:S(2)}, u32[]{:S(2)}) collective-permute-start(f32[64,2,8,384]{3,2,1,0:T(8,128)} %get-tuple-element.57), channel_id=1, source_target_pairs={{0,1},{1,0},{2,3},{3,2},{4,5},{5,4},{6,7},{7,6},{8,9},{9,8},{10,11... | collective-permute-start | bytes 4718600 | tf_op jit(solution)/shard_map/ppermute | solution.py:268
  137.5 11.1 %collective-permute-start.10 = (bf16[64,8,384]{2,1,0:T(8,128)(2,1)S(1)}, bf16[64,8,384]{2,1,0:T(8,128)(2,1)S(1)}, u32[]{:S(2)}, u32[]{:S(2)}) collective-permute-start(bf16[64,8,384]{2,1,0:T(8,128)(2,1)S(1)} %fusion.10), channel_id=1, source_target_pairs={{0,2},{1,3},{2,0},{3,1},{4,6},{5,7},{6,4},{7,5},{8,10},{9,11},{10,... | collective-permute-start | bytes 1179656 | tf_op jit(solution)/shard_map/ppermute | solution.py:267
  140.7 1.4 copy-start.5
  148.6 22.2 %collective-permute-start.11 = (f32[64,8,384]{2,1,0:T(8,128)}, f32[64,8,384]{2,1,0:T(8,128)}, u32[]{:S(2)}, u32[]{:S(2)}) collective-permute-start(f32[64,8,384]{2,1,0:T(8,128)} %fusion), channel_id=1, source_target_pairs={{0,2},{1,3},{2,0},{3,1},{4,6},{5,7},{6,4},{7,5},{8,10},{9,11},{10,... | collective-permute-start | bytes 2359304 | tf_op jit(solution)/shard_map/ppermute | solution.py:271
  150.0 28.1 %all-to-all-start = ((bf16[64,8,384]{2,1,0:T(8,128)(2,1)}), bf16[64,8,384]{2,1,0:T(8,128)(2,1)S(1)}, u32[]{:S(2)}, u32[]{:S(2)}) async-start(bf16[64,8,384]{2,1,0:T(8,128)(2,1)} %fusion.3), calls=%async_computation | async-start | bytes 786432 | tf_op jit(solution)/shard_map/all_to_all | solution.py:257
  178.1 22.5 %all-to-all-start.1 = ((bf16[64,8,384]{2,1,0:T(8,128)(2,1)}), bf16[64,8,384]{2,1,0:T(8,128)(2,1)S(1)}, u32[]{:S(2)}, u32[]{:S(2)}) async-start(bf16[64,8,384]{2,1,0:T(8,128)(2,1)} %fusion.5), calls=%async_computation.1 | async-start | bytes 786432 | tf_op jit(solution)/shard_map/all_to_all | solution.py:257

commit v4 on v3

v4 whole, which is shorter than its diff:
```python
import functools

import jax
import jax.numpy as jnp
from jax import lax
from jax.experimental import pallas as pl
from jax.experimental.pallas import tpu as pltpu
from jax.sharding import PartitionSpec as P


BOTH = ("occ", "off")
F32 = jnp.float32
BF16 = jnp.bfloat16
RING = 8
TN = (((0,), (0,)), ((), ()))
NT = (((1,), (1,)), ((), ()))


def lookup(level, table):
    hits = level[:, None] == jnp.arange(table.shape[0], dtype=jnp.int32)[None, :]
    return jnp.sum(jnp.where(hits, table[None, :], jnp.float32(0.0)), axis=1)


def moves(n_occ, rule):
    pairs = []
    half = n_occ // 2
    for i in range(n_occ):
        for chip in range(2):
            for core in range(2):
                j, to = rule(i, core)
                j %= n_occ
                flip = (i // half) ^ (j // half)
                pairs.append((i * 4 + chip * 2 + core, j * 4 + (chip ^ flip) * 2 + to))
    return pairs


def swap(n_occ, mask):
    return [(i * 4 + o, i * 4 + (o ^ mask)) for i in range(n_occ) for o in range(4)]


def round1(i, core):
    if core == 0:
        return i + 1, 1
    return (i + RING, 0) if i % RING else (i, 0)


def round2(i, core):
    if core == 1:
        return i + 1, 0
    return i - i % RING + (i - 1) % RING, 1


def round3(i, core):
    return (i + 1, 1) if core == 0 else (i - 1, 0)


def round4(i, core):
    return (i + 1, 0) if core == 1 else (i - 1, 1)


def sds(shape, dtype):
    return jax.ShapeDtypeStruct(shape, dtype)


def cost(flops, nbytes):
    return pl.CostEstimate(flops=flops, bytes_accessed=nbytes, transcendentals=0)


def amp_kernel(sc, own, xa, xb, evc, evr, eo, s_out, w_out, acc, *, half, slot):
    t = pl.program_id(0)

    @pl.when(t == 0)
    def _():
        acc[...] = lax.dot_general(xa[...], own[...], NT, preferred_element_type=F32)

    @pl.when(t == 1)
    def _():
        h = sc[0]
        acc[...] += lax.dot_general(xb[...], own[...], NT, preferred_element_type=F32)
        e = jnp.concatenate([evc[...]] * (half // 128), axis=1)

        def amp(first):
            cols = pl.ds(pl.multiple_of(first * half, half), half)
            return acc[:, cols] / (e + evr[:, cols] - eo[sc[3]] - eo[sc[4 + slot]])

        s_out[...] = amp(1 - h).astype(s_out.dtype)
        mine = amp(h)
        w_out[...] = (2.0 * mine - mine.T).astype(BF16)


def fill(w, h, group, half, s, q, v):
    def put(g, at):
        @pl.when(h == g)
        def _():
            w[:, at : at + half] = v[...]

        @pl.when(h != g)
        def _():
            w[:, at : at + half] = (2.0 * s[...].astype(F32) - q[...].astype(F32).T).astype(BF16)

    for at, g in enumerate(group):
        put(g, at * half)


def products(xs, ws):
    first = pl.program_id(0) < pl.num_programs(0) // 2
    res = None
    for (xa, xb), w in zip(xs, ws):
        x = jnp.where(first, xa[...], xb[...])
        term = lax.dot_general(x, w[...], TN, preferred_element_type=F32)
        res = term if res is None else res + term
    return res


def gamma_kernel(sc, *refs, n, half, early):
    xs = [refs[2 * k : 2 * k + 2] for k in range(n)]
    mixes, refs = refs[2 * n : 5 * n], refs[5 * n :]
    before = refs[0] if early else None
    out, ws = refs[1 if early else 0], refs[2 if early else 1 :]

    @pl.when(pl.program_id(0) == 0)
    def _():
        for k in range(n):
            fill(ws[k], sc[0], (0, 1), half, *mixes[3 * k : 3 * k + 3])

    res = products(xs, ws)
    out[...] = res + before[...] if early else res


def last_kernel(sc, xa, xb, s, q, v, early, keep0, keep1, send0, send1, w, *, half):
    @pl.when(pl.program_id(0) == 0)
    def _():
        fill(w, sc[0], (0, 1), half, s, q, v)

    res = early[...] + products([(xa, xb)], [w])
    res = res.reshape(res.shape[0] // 32, 2, 2, 8, res.shape[1])
    a, b = res[:, :, 0], res[:, :, 1]
    first = sc[1] == 0
    keep, send = jnp.where(first, a, b), jnp.where(first, b, a)
    keep0[...] = keep[..., :half]
    keep1[...] = keep[..., half:]
    send0[...] = send[..., :half]
    send1[...] = send[..., half:]


def body(
    factors, occ_level, vir_level, occupied_energy_levels, vir_table, virtual_coefficient_matrix
):
    n_occ = lax.axis_size("occ")
    occ_index = lax.axis_index("occ")
    off_index = lax.axis_index("off")
    chip = off_index // 2
    core = off_index % 2
    own = factors[0]
    n_vir, n_aux = own.shape
    half = n_vir // 2
    h = chip ^ (occ_index // (n_occ // 2))
    partners = [(occ_index - jnp.where(core == 0, a, b)) % n_occ for a, b in ((0, 1), (2, 7), (6, 3), (4, 5))]
    sc = jnp.stack([h, core, chip, occ_index, *partners]).astype(jnp.int32)

    def ring(x, rule):
        return lax.ppermute(x, BOTH, moves(n_occ, rule))

    def exchange(s):
        return lax.ppermute(s, BOTH, swap(n_occ, 2))

    tile = n_aux // 2
    x0 = [lax.dynamic_slice(own, (h * half, p * tile), (half, tile)) for p in range(2)]
    x1 = [ring(x0[p], round1) for p in range(2)]
    x2 = [ring(x1[p], round2) for p in range(2)]

    ev = lookup(vir_level, vir_table)
    eo = lookup(occ_level, occupied_energy_levels)
    evr = ev[None, :]
    evc = jnp.broadcast_to(lax.dynamic_slice_in_dim(ev, h * half, half, 0)[:, None], (half, 128))

    def amp(x, slot, s_dtype):
        return pl.pallas_call(
            functools.partial(amp_kernel, half=half, slot=slot),
            out_shape=(sds((half, half), s_dtype), sds((half, half), BF16)),
            grid_spec=pltpu.PrefetchScalarGridSpec(
                num_scalar_prefetch=1,
                grid=(2,),
                in_specs=[
                    pl.BlockSpec((n_vir, tile), lambda t, s: (0, t)),
                    pl.BlockSpec((half, tile), lambda t, s: (0, 0)),
                    pl.BlockSpec((half, tile), lambda t, s: (0, 0)),
                    pl.BlockSpec((half, 128), lambda t, s: (0, 0)),
                    pl.BlockSpec((1, n_vir), lambda t, s: (0, 0)),
                    pl.BlockSpec(memory_space=pltpu.SMEM),
                ],
                out_specs=[pl.BlockSpec((half, half), lambda t, s: (0, 0))] * 2,
                scratch_shapes=[pltpu.VMEM((half, n_vir), F32)],
            ),
            cost_estimate=cost(2 * n_vir * half * n_aux, 2 * n_aux * (n_vir + half)),
            name="amp",
        )(sc, own, *x, evc, evr, eo)

    tiles = 4
    tile_p = n_aux // tiles
    whole = pl.BlockSpec((half, half), lambda t, s: (0, 0))
    x_specs = [
        pl.BlockSpec((half, tile_p), lambda t, s: (0, jnp.minimum(t, 1))),
        pl.BlockSpec((half, tile_p), lambda t, s: (0, jnp.maximum(t - 2, 0))),
    ]
    row_spec = pl.BlockSpec((tile_p, n_vir), lambda t, s: (t, 0))

    def gamma(xs, mixes, early=()):
        n = len(xs)
        return pl.pallas_call(
            functools.partial(gamma_kernel, n=n, half=half, early=len(early) > 0),
            out_shape=sds((n_aux, n_vir), F32),
            grid_spec=pltpu.PrefetchScalarGridSpec(
                num_scalar_prefetch=1,
                grid=(tiles,),
                in_specs=x_specs * n + [whole] * (3 * n) + [row_spec] * len(early),
                out_specs=row_spec,
                scratch_shapes=[pltpu.VMEM((half, n_vir), BF16)] * n,
            ),
            cost_estimate=cost(2 * n * n_aux * half * n_vir, 2 * n * n_aux * half + 4 * n_aux * n_vir),
            name="gamma",
        )(sc, *(a for x in xs for a in x), *(m for mix in mixes for m in mix), *early)

    y1 = [jnp.where(core == 0, x0[p], x1[p]) for p in range(2)]
    s1, v1 = amp(y1, 0, F32)
    q1 = exchange(s1)
    x3 = [ring(x2[p], round3) for p in range(2)]
    s2, v2 = amp(x2, 1, F32)
    q2 = exchange(s2)
    x4 = [ring(x3[p], round4) for p in range(2)]
    s3, v3 = amp(x3, 2, F32)
    q3 = exchange(s3)
    early = gamma([y1, x2], [(s1, q1, v1), (s2, q2, v2)])
    x4[0], _ = lax.optimization_barrier((x4[0], s3))
    x4[1], early = lax.optimization_barrier((x4[1], early))
    s4, v4 = amp(x4, 3, BF16)
    q4 = exchange(s4)
    v3, _ = lax.optimization_barrier((v3, s4))
    early = gamma([x3], [(s3, q3, v3)], (early,))

    groups = tile_p // 32
    keep0, keep1, send0, send1 = pl.pallas_call(
        functools.partial(last_kernel, half=half),
        out_shape=(sds((n_occ, 2, 8, half), F32),) * 4,
        grid_spec=pltpu.PrefetchScalarGridSpec(
            num_scalar_prefetch=1,
            grid=(tiles,),
            in_specs=x_specs + [whole] * 3 + [row_spec],
            out_specs=[pl.BlockSpec((groups, 2, 8, half), lambda t, s: (t, 0, 0, 0))] * 4,
            scratch_shapes=[pltpu.VMEM((half, n_vir), BF16)],
        ),
        cost_estimate=cost(2 * n_aux * half * n_vir, 2 * n_aux * (4 * n_vir + half)),
        name="last",
    )(sc, *x4, s4, q4, v4, early)

    def part(keep, got, c):
        a = lax.dynamic_index_in_dim(keep, c, 1, keepdims=False)
        return a + lax.dynamic_index_in_dim(got, c, 1, keepdims=False)

    def low(keep, got, far):
        return (part(keep, got, chip) + far.astype(F32)).astype(BF16)

    def finish(g, low):
        mine = lax.all_to_all(low, "occ", split_axis=0, concat_axis=0, tiled=True)
        c = virtual_coefficient_matrix[g * half : (g + 1) * half]
        return jnp.einsum("sbd,dw->sbw", mine, c, preferred_element_type=F32)

    got0 = lax.ppermute(send0, BOTH, swap(n_occ, 1))
    away0 = part(keep0, got0, 1 - chip).astype(BF16)
    far0 = lax.ppermute(away0, BOTH, swap(n_occ, 2))
    got1 = lax.ppermute(send1, BOTH, swap(n_occ, 1))
    away1 = part(keep1, got1, 1 - chip)
    away1, _ = lax.optimization_barrier((away1, far0))
    far1 = lax.ppermute(away1, BOTH, swap(n_occ, 2))
    return finish(1, low(keep1, got1, far1)) + finish(0, low(keep0, got0, far0))


def solution(mesh):
    in_specs = (P("occ", None, None), P(), P(), P(), P(), P())
    out_specs = P(None, ("occ", "off"), None)
    return jax.shard_map(body, mesh=mesh, in_specs=in_specs, out_specs=out_specs, check_vma=False)
```

time: 206 us -> 198 us (0.961)
  waiting for transfers between devices: 97.5 us -> 78.1 us
  starting transfers between devices: 35.4 us -> 44.6 us
  other arithmetic: 7.33 us -> 12 us
  Pallas kernels: 52.4 us -> 48.2 us
    ppermute x2 -> x0, waiting for transfers between devices: 26.6 us -> none  [the longest x1 18.6 us: body(): x1 = lax.ppermute(x0, BOTH, moves(n_occ, round1))]
    ppermute x2 -> x8, waiting for transfers between devices: 14.6 us -> 29.4 us  [ring(): return lax.ppermute(x, BOTH, moves(n_occ, rule))]
    ppermute x2 -> x8, starting transfers between devices: 3.85 us -> 16.1 us  [ring(): return lax.ppermute(x, BOTH, moves(n_occ, rule))]
    ppermute x4, waiting for transfers between devices: 20.2 us -> 11.7 us  [exchange(): return lax.ppermute(s, BOTH, swap(n_occ, 2))]
    ppermute x1, waiting for transfers between devices: 9.42 us -> 2.53 us  [body(): far1 = lax.ppermute(away1, BOTH, swap(n_occ, 2))]
    ppermute x2 -> x0, starting transfers between devices: 5.56 us -> none  [the longest x1 4.13 us: body(): x2 = lax.ppermute(x1, BOTH, moves(n_occ, round2))]
    all_to_all x2, waiting for transfers between devices: 17.5 us -> 22.9 us  [finish(): mine = lax.all_to_all(low, 'occ', split_axis=0, concat_axis=0, tiled=True)]
    pallas_call x8 -> x7, Pallas kernels: 52.4 us -> 48.2 us  [the longest x4 21.8 us: amp(): pl.pallas_call(functools.partial(amp_kernel, half=half, slot=slot), out_s...]
  transfers between devices with their start and end apart: 14 -> 18, of which waited for: 10 -> 9; matrix products, arithmetic and copies ran while one was open for 6% -> 8% of each run, Pallas kernels for 23% -> 20%
where the time goes in v4:
time: 198 us; the launch traced here: 196 us
  waiting for transfers between devices  78.1 us (39%)
  Pallas kernels  48.2 us (24%)
  starting transfers between devices  44.6 us (23%)
  other arithmetic  12 us (6%)
  local copies, waits for them, and re-layouts  8.02 us (4%)
  matrix products  5.01 us (3%)
    ppermute x8, waiting for transfers between devices, ring(): return lax.ppermute(x, BOTH, moves(n_occ, rule))  29.4 us
    all_to_all x2, waiting for transfers between devices, finish(): mine = lax.all_to_all(low, 'occ', split_axis=0, concat_axis=0, tiled=True)  22.9 us
    all_to_all x2, starting transfers between devices, finish(): mine = lax.all_to_all(low, 'occ', split_axis=0, concat_axis=0, tiled=True)  21.9 us
    pallas_call x4, Pallas kernels, amp(): pl.pallas_call(functools.partial(amp_kernel, half=half, slot=slot), out_s...  21.8 us
    pallas_call x2, Pallas kernels, gamma(): pl.pallas_call(functools.partial(gamma_kernel, n=n, half=half, early=len(...  18.1 us
    ppermute x8, starting transfers between devices, ring(): return lax.ppermute(x, BOTH, moves(n_occ, rule))  16.1 us
    ppermute x4, waiting for transfers between devices, exchange(): return lax.ppermute(s, BOTH, swap(n_occ, 2))  11.7 us
    ppermute x1, waiting for transfers between devices, body(): far0 = lax.ppermute(away0, BOTH, swap(n_occ, 2))  8.52 us
  transfers between devices with their start and end apart: 18, of which 9 were waited for; matrix products, arithmetic and copies ran while one was open for 8% of the time, Pallas kernels for 20%

profile of v4, /device:TPU:56, one launch (start us, length us, event | category | flops | bytes accessed | tf_op | source)
XLA Modules:
  0.0 196.2 jit_solution(8358964096851971077)
XLA Ops:
  0.0 1.5 dynamic-slice_bitcast_fusion
  3.0 2.7 %collective-permute-start = (bf16[384,1024]{1,0:T(8,128)(2,1)S(1)}, bf16[384,1024]{1,0:T(8,128)(2,1)S(1)}, u32[]{:S(2)}, u32[]{:S(2)}) collective-permute-start(bf16[384,1024]{1,0:T(8,128)(2,1)S(1)} %get-tuple-element.40), channel_id=1, source_target_pairs={{0,5},{1,0},{2,7},{3,2},{4,9},{5,36},{6,11},{7,38},{8,13},{9,40},{... | collective-permute-start | bytes 2359304 | tf_op jit(solution)/shard_map/ppermute | solution.py:162
  5.7 7.5 %collective-permute-done.4 = bf16[384,1024]{1,0:T(8,128)(2,1)} collective-permute-done((bf16[384,1024]{1,0:T(8,128)(2,1)S(1)}, bf16[384,1024]{1,0:T(8,128)(2,1)}, u32[]{:S(2)}, u32[]{:S(2)}) %collective-permute-start.4) | collective-permute-done | bytes 786464 | tf_op jit(solution)/shard_map/ppermute | solution.py:162
  13.2 4.1 %collective-permute-start.5 = (bf16[384,1024]{1,0:T(8,128)(2,1)}, bf16[384,1024]{1,0:T(8,128)(2,1)S(1)}, u32[]{:S(2)}, u32[]{:S(2)}) collective-permute-start(bf16[384,1024]{1,0:T(8,128)(2,1)} %collective-permute-done.4), channel_id=1, source_target_pairs={{0,29},{1,4},{2,31},{3,6},{4,1},{5,8},{6,3},{7,10},{8,5},{9,12},{1... | collective-permute-start | bytes 2359304 | tf_op jit(solution)/shard_map/ppermute | solution.py:162
  17.3 8.8 %collective-permute-done = bf16[384,1024]{1,0:T(8,128)(2,1)S(1)} collective-permute-done((bf16[384,1024]{1,0:T(8,128)(2,1)S(1)}, bf16[384,1024]{1,0:T(8,128)(2,1)S(1)}, u32[]{:S(2)}, u32[]{:S(2)}) %collective-permute-start) | collective-permute-done | bytes 786464 | tf_op jit(solution)/shard_map/ppermute | solution.py:162
  26.1 5.5 %collective-permute-start.1 = (bf16[384,1024]{1,0:T(8,128)(2,1)S(1)}, bf16[384,1024]{1,0:T(8,128)(2,1)S(1)}, u32[]{:S(2)}, u32[]{:S(2)}) collective-permute-start(bf16[384,1024]{1,0:T(8,128)(2,1)S(1)} %collective-permute-done), channel_id=1, source_target_pairs={{0,29},{1,4},{2,31},{3,6},{4,1},{5,8},{6,3},{7,10},{8,5},{9,12},{1... | collective-permute-start | bytes 2359304 | tf_op jit(solution)/shard_map/ppermute | solution.py:162
  34.0 13.1 %collective-permute-done.1.xa.refs_2_ = bf16[384,1024]{1,0:T(8,128)(2,1)S(1)} collective-permute-done((bf16[384,1024]{1,0:T(8,128)(2,1)S(1)}, bf16[384,1024]{1,0:T(8,128)(2,1)S(1)}, u32[]{:S(2)}, u32[]{:S(2)}) %collective-permute-start.1) | collective-permute-done | bytes 786464 | tf_op jit(solution)/shard_map/ppermute | solution.py:162
  47.1 2.4 %broadcast_select_fusion.xb.refs_1_ = bf16[384,1024]{1,0:T(8,128)(2,1)} fusion(bf16[384,1024]{1,0:T(8,128)(2,1)} %copy-done.6, bf16[384,1024]{1,0:T(8,128)(2,1)} %collective-permute-done.4, pred[]{:T(512)S(6)} %eq.20), kind=kLoop, calls=%fused_computation.19 | loop fusion | flops 393216 | bytes 2359297 | tf_op jit(solution)/shard_map/jit(_where)/select_n | solution.py:224
  51.2 5.5 %amp.5 = (f32[384,384]{1,0:T(8,128)}, bf16[384,384]{1,0:T(8,128)(2,1)}) custom-call(s32[8]{0:T(128)} %stack.35.sc, bf16[768,2048]{1,0:T(8,128)(2,1)} %bitcast.49, bf16[384,1024]{1,0:T(8,128)(2,1)} %broadcast_select_fusion.1.xa.refs_0_, bf16[384,1024]{1,0:T(8,128)(2,1)} %broadcast_select_fusion.xb.refs_1_, f32[384,128]{1,0:T(8,128)} %broadcast_in_dim.41.evc, ...), custom_call_target="tpu_custom_call" | custom-call | flops 1207959552 | bytes 4718592 | tf_op jit(solution)/shard_map/amp/pallas_call | solution.py:178
  56.7 1.5 collective-permute-start.8
  58.2 5.4 %amp.6 = (f32[384,384]{1,0:T(8,128)}, bf16[384,384]{1,0:T(8,128)(2,1)}) custom-call(s32[8]{0:T(128)} %stack.35.sc, bf16[768,2048]{1,0:T(8,128)(2,1)} %bitcast.50, bf16[384,1024]{1,0:T(8,128)(2,1)} %copy-done.3, bf16[384,1024]{1,0:T(8,128)(2,1)} %copy-done.2, f32[384,128]{1,0:T(8,128)} %broadcast_in_dim.41.evc, f32[1,768]{1,0:T(1,128)} %broadcast_in_dim.42.evr, ...), custom_call_target="tpu_custom_call" | custom-call | flops 1207959552 | bytes 4718592 | tf_op jit(solution)/shard_map/amp/pallas_call | solution.py:178
  64.2 2.1 %collective-permute-start.7 = (bf16[384,1024]{1,0:T(8,128)(2,1)S(1)}, bf16[384,1024]{1,0:T(8,128)(2,1)S(1)}, u32[]{:S(2)}, u32[]{:S(2)}) collective-permute-start(bf16[384,1024]{1,0:T(8,128)(2,1)S(1)} %collective-permute-done.6.xb.refs_1_), channel_id=1, source_target_pairs={{0,255},{1,4},{2,253},{3,6},{4,1},{5,8},{6,3},{7,10},{8,5},{9,12},... | collective-permute-start | bytes 2359304 | tf_op jit(solution)/shard_map/ppermute | solution.py:162
  67.2 5.5 %amp.4 = (f32[384,384]{1,0:T(8,128)}, bf16[384,384]{1,0:T(8,128)(2,1)}) custom-call(s32[8]{0:T(128)} %stack.35.sc, bf16[768,2048]{1,0:T(8,128)(2,1)} %bitcast.51, bf16[384,1024]{1,0:T(8,128)(2,1)} %copy-done.1, bf16[384,1024]{1,0:T(8,128)(2,1)} %copy-done, f32[384,128]{1,0:T(8,128)} %broadcast_in_dim.41.evc, f32[1,768]{1,0:T(1,128)} %broadcast_in_dim.42.evr, ...), custom_call_target="tpu_custom_call" | custom-call | flops 1207959552 | bytes 4718592 | tf_op jit(solution)/shard_map/amp/pallas_call | solution.py:178
  72.7 1.5 collective-permute-start.11
  74.2 11.7 %collective-permute-done.9.refs_8_ = f32[384,384]{1,0:T(8,128)} collective-permute-done((f32[384,384]{1,0:T(8,128)}, f32[384,384]{1,0:T(8,128)}, u32[]{:S(2)}, u32[]{:S(2)}) %collective-permute-start.9) | collective-permute-done | bytes 589856 | tf_op jit(solution)/shard_map/ppermute | solution.py:165
  85.9 9.5 %gamma.2.refs_5_ = f32[2048,768]{1,0:T(8,128)} custom-call(s32[8]{0:T(128)} %stack.35.sc, bf16[384,1024]{1,0:T(8,128)(2,1)} %broadcast_select_fusion.1.xa.refs_0_, bf16[384,1024]{1,0:T(8,128)(2,1)} %broadcast_select_fusion.xb.refs_1_, bf16[384,1024]{1,0:T(8,128)(2,1)} %copy-done.3, bf16[384,1024]{1,0:T(8,128)(2,1)} %copy-done.2, ...), custom_call_target="tpu_custom_call" | custom-call | flops 2415919104 | bytes 9437184 | tf_op jit(solution)/shard_map/gamma/pallas_call | solution.py:210
  97.1 5.4 %amp.7 = (bf16[384,384]{1,0:T(8,128)(2,1)}, bf16[384,384]{1,0:T(8,128)(2,1)}) custom-call(s32[8]{0:T(128)} %stack.35.sc, bf16[768,2048]{1,0:T(8,128)(2,1)} %bitcast.52, bf16[384,1024]{1,0:T(8,128)(2,1)} %copy-done.8, bf16[384,1024]{1,0:T(8,128)(2,1)} %copy-done.7, f32[384,128]{1,0:T(8,128)} %broadcast_in_dim.41.evc, f32[1,768]{1,0:T(1,128)} %broadcast_in_dim.42.evr, ...), custom_call_target="tpu_custom_call" | custom-call | flops 1207959552 | bytes 4718592 | tf_op jit(solution)/shard_map/amp/pallas_call | solution.py:178
  102.5 1.5 collective-permute-start.10
  104.0 8.7 %gamma.3.early = f32[2048,768]{1,0:T(8,128)} custom-call(s32[8]{0:T(128)} %stack.35.sc, bf16[384,1024]{1,0:T(8,128)(2,1)} %copy-done.1, bf16[384,1024]{1,0:T(8,128)(2,1)} %copy-done, f32[384,384]{1,0:T(8,128)} %get-tuple-element.22.refs_2_, f32[384,384]{1,0:T(8,128)} %collective-permute-done.11.refs_3_, bf16[384,384]{1,0:T(8,128)(2,1)} %get-tuple-element.32.refs_4_, ...), custom_call_target="tpu_custom_call" | custom-call | flops 1207959552 | bytes 7864320 | tf_op jit(solution)/shard_map/gamma/pallas_call | solution.py:210
  113.4 8.3 %last.1 = (f32[64,2,8,384]{3,2,1,0:T(8,128)}, f32[64,2,8,384]{3,2,1,0:T(8,128)}, f32[64,2,8,384]{3,2,1,0:T(8,128)}, f32[64,2,8,384]{3,2,1,0:T(8,128)}) custom-call(s32[8]{0:T(128)} %stack.35.sc, bf16[384,1024]{1,0:T(8,128)(2,1)} %copy-done.8, bf16[384,1024]{1,0:T(8,128)(2,1)} %copy-done.7, bf16[384,384]{1,0:T(8,128)(2,1)} %get-tuple-element.29.s, ...), custom_call_target="tpu_custom_call" | custom-call | flops 1207959552 | bytes 14155776 | tf_op jit(solution)/shard_map/last/pallas_call | solution.py:242
  122.3 3.1 %collective-permute-done.13 = f32[64,2,8,384]{3,2,1,0:T(8,128)S(1)} collective-permute-done((f32[64,2,8,384]{3,2,1,0:T(8,128)}, f32[64,2,8,384]{3,2,1,0:T(8,128)S(1)}, u32[]{:S(2)}, u32[]{:S(2)}) %collective-permute-start.13) | collective-permute-done | bytes 1572896 | tf_op jit(solution)/shard_map/ppermute | solution.py:268
  128.4 2.1 %add_bitcast_fusion = f32[64,8,384]{2,1,0:T(8,128)} fusion(f32[64,2,8,384]{3,2,1,0:T(8,128)} %collective-permute-done.12, s32[]{:T(128)S(6)} %select_n.99, f32[64,2,8,384]{3,2,1,0:T(8,128)S(1)} %copy-done.9), kind=kLoop, calls=%fused_computation.14 | loop fusion | flops 196608 | bytes 2359300 | tf_op jit(solution)/shard_map/add | solution.py:258
  130.5 8.5 %collective-permute-done.14 = bf16[64,8,384]{2,1,0:T(8,128)(2,1)S(1)} collective-permute-done((bf16[64,8,384]{2,1,0:T(8,128)(2,1)S(1)}, bf16[64,8,384]{2,1,0:T(8,128)(2,1)S(1)}, u32[]{:S(2)}, u32[]{:S(2)}) %collective-permute-start.14) | collective-permute-done | bytes 393248 | tf_op jit(solution)/shard_map/ppermute | solution.py:270
  139.5 2.0 %fusion.6 = bf16[64,8,384]{2,1,0:T(8,128)(2,1)} fusion(bf16[64,8,384]{2,1,0:T(8,128)(2,1)S(1)} %collective-permute-done.14, f32[64,2,8,384]{3,2,1,0:T(8,128)} %copy-done.11, s32[]{:T(128)S(6)} %select_n.98, f32[64,2,8,384]{3,2,1,0:T(8,128)S(1)} %copy-done.10), kind=kLoop, calls=%fused_computation.10 | loop fusion | flops 786432 | bytes 2359300 | tf_op jit(solution)/shard_map/convert_element_type | solution.py:261
  141.5 14.8 %all-to-all-start.1 = ((bf16[64,8,384]{2,1,0:T(8,128)(2,1)}), bf16[64,8,384]{2,1,0:T(8,128)(2,1)S(1)}, u32[]{:S(2)}, u32[]{:S(2)}) async-start(bf16[64,8,384]{2,1,0:T(8,128)(2,1)} %fusion.6), calls=%async_computation.1 | async-start | bytes 786432 | tf_op jit(solution)/shard_map/all_to_all | solution.py:264
  156.4 2.5 %collective-permute-done.15 = f32[64,8,384]{2,1,0:T(8,128)} collective-permute-done((f32[64,8,384]{2,1,0:T(8,128)}, f32[64,8,384]{2,1,0:T(8,128)}, u32[]{:S(2)}, u32[]{:S(2)}) %collective-permute-start.15) | collective-permute-done | bytes 786464 | tf_op jit(solution)/shard_map/ppermute | solution.py:274
  158.9 2.2 %fusion.3 = bf16[64,8,384]{2,1,0:T(8,128)(2,1)} fusion(f32[64,8,384]{2,1,0:T(8,128)} %collective-permute-done.15, f32[64,2,8,384]{3,2,1,0:T(8,128)} %collective-permute-done.12, s32[]{:T(128)S(6)} %select_n.98, f32[64,2,8,384]{3,2,1,0:T(8,128)S(1)} %copy-done.9), kind=kLoop, calls=%fused_computation.6 | loop fusion | flops 589824 | bytes 2752516 | tf_op jit(solution)/shard_map/convert_element_type | solution.py:261
  161.1 10.7 %all-to-all-done.1 = bf16[64,8,384]{2,1,0:T(8,128)(2,1)S(1)} async-done(((bf16[64,8,384]{2,1,0:T(8,128)(2,1)}), bf16[64,8,384]{2,1,0:T(8,128)(2,1)S(1)}, u32[]{:S(2)}, u32[]{:S(2)}) %all-to-all-start.1) | async-done | bytes 393248 | tf_op jit(solution)/shard_map/all_to_all | solution.py:264
  171.8 7.1 %all-to-all-start = ((bf16[64,8,384]{2,1,0:T(8,128)(2,1)}), bf16[64,8,384]{2,1,0:T(8,128)(2,1)S(1)}, u32[]{:S(2)}, u32[]{:S(2)}) async-start(bf16[64,8,384]{2,1,0:T(8,128)(2,1)} %fusion.3), calls=%async_computation | async-start | bytes 786432 | tf_op jit(solution)/shard_map/all_to_all | solution.py:264
  178.9 1.8 fusion.4
  180.8 12.2 %all-to-all-done = bf16[64,8,384]{2,1,0:T(8,128)(2,1)S(1)} async-done(((bf16[64,8,384]{2,1,0:T(8,128)(2,1)}), bf16[64,8,384]{2,1,0:T(8,128)(2,1)S(1)}, u32[]{:S(2)}, u32[]{:S(2)}) %all-to-all-start) | async-done | bytes 393248 | tf_op jit(solution)/shard_map/all_to_all | solution.py:264
  193.0 3.2 %convolution_add_fusion = f32[64,8,1024]{2,1,0:T(8,128)} fusion(f32[64,8,1024]{2,1,0:T(8,128)S(1)} %fusion.4, bf16[64,8,384]{2,1,0:T(8,128)(2,1)S(1)} %all-to-all-done, bf16[768,1024]{1,0:T(8,128)(2,1)} %param.11), kind=kOutput, calls=%fused_computation | convolution fusion | flops 403177472 | bytes 5373952 | tf_op jit(solution)/shard_map/sbd,dw->sbw/dot_general | solution.py:266
  (64 shorter events, 13.5 us)
Async XLA Ops:
  0.0 31.6 %copy-start.15 = (s32[768]{0:T(1024)S(1)}, s32[768]{0:T(1024)}, u32[]{:S(2)}) copy-start(s32[768]{0:T(1024)} %param.8) | copy-start | bytes 9220
  0.0 31.6 %copy-start.16 = (f32[256]{0:T(256)S(1)}, f32[256]{0:T(256)}, u32[]{:S(2)}) copy-start(f32[256]{0:T(256)} %param.10) | copy-start | bytes 3076
  0.0 33.2 %copy-start.17 = (f32[256]{0:T(256)S(1)}, f32[256]{0:T(256)}, u32[]{:S(2)}) copy-start(f32[256]{0:T(256)} %param.9) | copy-start | bytes 3076
  0.0 33.2 %copy-start.18 = (s32[64]{0:T(128)S(1)}, s32[64]{0:T(128)}, u32[]{:S(2)}) copy-start(s32[64]{0:T(128)} %param.7) | copy-start | bytes 772
  1.6 15.7 %copy-start.4 = (bf16[384,1024]{1,0:T(8,128)(2,1)}, bf16[384,1024]{1,0:T(8,128)(2,1)S(1)}, u32[]{:S(2)}) copy-start(bf16[384,1024]{1,0:T(8,128)(2,1)S(1)} %get-tuple-element.40) | copy-start | bytes 2359300
  1.6 24.5 %copy-start.6 = (bf16[384,1024]{1,0:T(8,128)(2,1)}, bf16[384,1024]{1,0:T(8,128)(2,1)S(1)}, u32[]{:S(2)}) copy-start(bf16[384,1024]{1,0:T(8,128)(2,1)S(1)} %get-tuple-element.39) | copy-start | bytes 2359300
  1.6 11.6 %collective-permute-start.4 = (bf16[384,1024]{1,0:T(8,128)(2,1)S(1)}, bf16[384,1024]{1,0:T(8,128)(2,1)}, u32[]{:S(2)}, u32[]{:S(2)}) collective-permute-start(bf16[384,1024]{1,0:T(8,128)(2,1)S(1)} %get-tuple-element.39), channel_id=1, source_target_pairs={{0,5},{1,0},{2,7},{3,2},{4,9},{5,36},{6,11},{7,38},{8,13},{9,40},{... | collective-permute-start | bytes 2359304 | tf_op jit(solution)/shard_map/ppermute | solution.py:162
  3.0 23.1 %collective-permute-start = (bf16[384,1024]{1,0:T(8,128)(2,1)S(1)}, bf16[384,1024]{1,0:T(8,128)(2,1)S(1)}, u32[]{:S(2)}, u32[]{:S(2)}) collective-permute-start(bf16[384,1024]{1,0:T(8,128)(2,1)S(1)} %get-tuple-element.40), channel_id=1, source_target_pairs={{0,5},{1,0},{2,7},{3,2},{4,9},{5,36},{6,11},{7,38},{8,13},{9,40},{... | collective-permute-start | bytes 2359304 | tf_op jit(solution)/shard_map/ppermute | solution.py:162
  13.2 20.8 %collective-permute-start.5 = (bf16[384,1024]{1,0:T(8,128)(2,1)}, bf16[384,1024]{1,0:T(8,128)(2,1)S(1)}, u32[]{:S(2)}, u32[]{:S(2)}) collective-permute-start(bf16[384,1024]{1,0:T(8,128)(2,1)} %collective-permute-done.4), channel_id=1, source_target_pairs={{0,29},{1,4},{2,31},{3,6},{4,1},{5,8},{6,3},{7,10},{8,5},{9,12},{1... | collective-permute-start | bytes 2359304 | tf_op jit(solution)/shard_map/ppermute | solution.py:162
  26.1 7.9 %copy-start.12 = (bf16[384,1024]{1,0:T(8,128)(2,1)}, bf16[384,1024]{1,0:T(8,128)(2,1)S(1)}, u32[]{:S(2)}) copy-start(bf16[384,1024]{1,0:T(8,128)(2,1)S(1)} %collective-permute-done) | copy-start | bytes 2359300
  26.1 21.0 %collective-permute-start.1 = (bf16[384,1024]{1,0:T(8,128)(2,1)S(1)}, bf16[384,1024]{1,0:T(8,128)(2,1)S(1)}, u32[]{:S(2)}, u32[]{:S(2)}) collective-permute-start(bf16[384,1024]{1,0:T(8,128)(2,1)S(1)} %collective-permute-done), channel_id=1, source_target_pairs={{0,29},{1,4},{2,31},{3,6},{4,1},{5,8},{6,3},{7,10},{8,5},{9,12},{1... | collective-permute-start | bytes 2359304 | tf_op jit(solution)/shard_map/ppermute | solution.py:162
  33.2 16.3 %copy-start.5 = (bf16[384,1024]{1,0:T(8,128)(2,1)S(1)}, bf16[384,1024]{1,0:T(8,128)(2,1)}, u32[]{:S(2)}) copy-start(bf16[384,1024]{1,0:T(8,128)(2,1)} %copy-done.4) | copy-start | bytes 2359300
  33.9 16.5 %copy-start.2 = (bf16[384,1024]{1,0:T(8,128)(2,1)}, bf16[384,1024]{1,0:T(8,128)(2,1)S(1)}, u32[]{:S(2)}) copy-start(bf16[384,1024]{1,0:T(8,128)(2,1)S(1)} %collective-permute-done.5.xb.refs_3_) | copy-start | bytes 2359300
  33.9 30.2 %collective-permute-start.6 = (bf16[384,1024]{1,0:T(8,128)(2,1)S(1)}, bf16[384,1024]{1,0:T(8,128)(2,1)S(1)}, u32[]{:S(2)}, u32[]{:S(2)}) collective-permute-start(bf16[384,1024]{1,0:T(8,128)(2,1)S(1)} %collective-permute-done.5.xb.refs_3_), channel_id=1, source_target_pairs={{0,5},{1,254},{2,7},{3,252},{4,9},{5,0},{6,11},{7,2},{8,13},{9,4},... | collective-permute-start | bytes 2359304 | tf_op jit(solution)/shard_map/ppermute | solution.py:162
  47.1 3.4 %copy-start.3 = (bf16[384,1024]{1,0:T(8,128)(2,1)}, bf16[384,1024]{1,0:T(8,128)(2,1)S(1)}, u32[]{:S(2)}) copy-start(bf16[384,1024]{1,0:T(8,128)(2,1)S(1)} %collective-permute-done.1.xa.refs_2_) | copy-start | bytes 2359300
  47.1 2.4 %copy-start.13 = (bf16[384,1024]{1,0:T(8,128)(2,1)S(1)}, bf16[384,1024]{1,0:T(8,128)(2,1)}, u32[]{:S(2)}) copy-start(bf16[384,1024]{1,0:T(8,128)(2,1)} %copy-done.12) | copy-start | bytes 2359300
  47.1 19.3 %collective-permute-start.2 = (bf16[384,1024]{1,0:T(8,128)(2,1)S(1)}, bf16[384,1024]{1,0:T(8,128)(2,1)S(1)}, u32[]{:S(2)}, u32[]{:S(2)}) collective-permute-start(bf16[384,1024]{1,0:T(8,128)(2,1)S(1)} %collective-permute-done.1.xa.refs_2_), channel_id=1, source_target_pairs={{0,5},{1,254},{2,7},{3,252},{4,9},{5,0},{6,11},{7,2},{8,13},{9,4},... | collective-permute-start | bytes 2359304 | tf_op jit(solution)/shard_map/ppermute | solution.py:162
  56.7 17.5 %collective-permute-start.8 = (f32[384,384]{1,0:T(8,128)}, f32[384,384]{1,0:T(8,128)}, u32[]{:S(2)}, u32[]{:S(2)}) collective-permute-start(f32[384,384]{1,0:T(8,128)} %get-tuple-element.24.refs_4_), channel_id=1, source_target_pairs={{0,2},{1,3},{2,0},{3,1},{4,6},{5,7},{6,4},{7,5},{8,10},{9,11},{10,... | collective-permute-start | bytes 1769480 | tf_op jit(solution)/shard_map/ppermute | solution.py:165
  63.6 22.2 %collective-permute-start.9 = (f32[384,384]{1,0:T(8,128)}, f32[384,384]{1,0:T(8,128)}, u32[]{:S(2)}, u32[]{:S(2)}) collective-permute-start(f32[384,384]{1,0:T(8,128)} %get-tuple-element.26.refs_7_), channel_id=1, source_target_pairs={{0,2},{1,3},{2,0},{3,1},{4,6},{5,7},{6,4},{7,5},{8,10},{9,11},{10,... | collective-permute-start | bytes 1769480 | tf_op jit(solution)/shard_map/ppermute | solution.py:165
  64.2 2.3 %copy-start = (bf16[384,1024]{1,0:T(8,128)(2,1)}, bf16[384,1024]{1,0:T(8,128)(2,1)S(1)}, u32[]{:S(2)}) copy-start(bf16[384,1024]{1,0:T(8,128)(2,1)S(1)} %collective-permute-done.6.xb.refs_1_) | copy-start | bytes 2359300
  64.2 31.1 %collective-permute-start.7 = (bf16[384,1024]{1,0:T(8,128)(2,1)S(1)}, bf16[384,1024]{1,0:T(8,128)(2,1)S(1)}, u32[]{:S(2)}, u32[]{:S(2)}) collective-permute-start(bf16[384,1024]{1,0:T(8,128)(2,1)S(1)} %collective-permute-done.6.xb.refs_1_), channel_id=1, source_target_pairs={{0,255},{1,4},{2,253},{3,6},{4,1},{5,8},{6,3},{7,10},{8,5},{9,12},... | collective-permute-start | bytes 2359304 | tf_op jit(solution)/shard_map/ppermute | solution.py:162
  66.3 29.0 %collective-permute-start.3 = (bf16[384,1024]{1,0:T(8,128)(2,1)S(1)}, bf16[384,1024]{1,0:T(8,128)(2,1)S(1)}, u32[]{:S(2)}, u32[]{:S(2)}) collective-permute-start(bf16[384,1024]{1,0:T(8,128)(2,1)S(1)} %collective-permute-done.2.xa.refs_0_), channel_id=1, source_target_pairs={{0,255},{1,4},{2,253},{3,6},{4,1},{5,8},{6,3},{7,10},{8,5},{9,12},... | collective-permute-start | bytes 2359304 | tf_op jit(solution)/shard_map/ppermute | solution.py:162
  72.7 31.3 %collective-permute-start.11 = (f32[384,384]{1,0:T(8,128)}, f32[384,384]{1,0:T(8,128)}, u32[]{:S(2)}, u32[]{:S(2)}) collective-permute-start(f32[384,384]{1,0:T(8,128)} %get-tuple-element.22.refs_2_), channel_id=1, source_target_pairs={{0,2},{1,3},{2,0},{3,1},{4,6},{5,7},{6,4},{7,5},{8,10},{9,11},{10,... | collective-permute-start | bytes 1769480 | tf_op jit(solution)/shard_map/ppermute | solution.py:165
  102.5 10.2 %collective-permute-start.10 = (bf16[384,384]{1,0:T(8,128)(2,1)}, bf16[384,384]{1,0:T(8,128)(2,1)S(1)}, u32[]{:S(2)}, u32[]{:S(2)}) collective-permute-start(bf16[384,384]{1,0:T(8,128)(2,1)} %get-tuple-element.29.s), channel_id=1, source_target_pairs={{0,2},{1,3},{2,0},{3,1},{4,6},{5,7},{6,4},{7,5},{8,10},{9,11},{10,... | collective-permute-start | bytes 884744 | tf_op jit(solution)/shard_map/ppermute | solution.py:165
  121.7 6.7 %copy-start.9 = (f32[64,2,8,384]{3,2,1,0:T(8,128)S(1)}, f32[64,2,8,384]{3,2,1,0:T(8,128)}, u32[]{:S(2)}) copy-start(f32[64,2,8,384]{3,2,1,0:T(8,128)} %get-tuple-element.34) | copy-start | bytes 4718596
  121.7 3.7 %collective-permute-start.13 = (f32[64,2,8,384]{3,2,1,0:T(8,128)}, f32[64,2,8,384]{3,2,1,0:T(8,128)S(1)}, u32[]{:S(2)}, u32[]{:S(2)}) collective-permute-start(f32[64,2,8,384]{3,2,1,0:T(8,128)} %get-tuple-element.37), channel_id=1, source_target_pairs={{0,1},{1,0},{2,3},{3,2},{4,5},{5,4},{6,7},{7,6},{8,9},{9,8},{10,11... | collective-permute-start | bytes 4718600 | tf_op jit(solution)/shard_map/ppermute | solution.py:268
  121.8 6.6 %collective-permute-start.12 = (f32[64,2,8,384]{3,2,1,0:T(8,128)}, f32[64,2,8,384]{3,2,1,0:T(8,128)}, u32[]{:S(2)}, u32[]{:S(2)}) collective-permute-start(f32[64,2,8,384]{3,2,1,0:T(8,128)} %get-tuple-element.35), channel_id=1, source_target_pairs={{0,1},{1,0},{2,3},{3,2},{4,5},{5,4},{6,7},{7,6},{8,9},{9,8},{10,11... | collective-permute-start | bytes 4718600 | tf_op jit(solution)/shard_map/ppermute | solution.py:271
  127.8 11.7 %copy-start.10 = (f32[64,2,8,384]{3,2,1,0:T(8,128)S(1)}, f32[64,2,8,384]{3,2,1,0:T(8,128)}, u32[]{:S(2)}) copy-start(f32[64,2,8,384]{3,2,1,0:T(8,128)} %get-tuple-element.36) | copy-start | bytes 4718596
  127.8 11.2 %collective-permute-start.14 = (bf16[64,8,384]{2,1,0:T(8,128)(2,1)S(1)}, bf16[64,8,384]{2,1,0:T(8,128)(2,1)S(1)}, u32[]{:S(2)}, u32[]{:S(2)}) collective-permute-start(bf16[64,8,384]{2,1,0:T(8,128)(2,1)S(1)} %fusion.10), channel_id=1, source_target_pairs={{0,2},{1,3},{2,0},{3,1},{4,6},{5,7},{6,4},{7,5},{8,10},{9,11},{10,... | collective-permute-start | bytes 1179656 | tf_op jit(solution)/shard_map/ppermute | solution.py:270
  139.1 19.8 %collective-permute-start.15 = (f32[64,8,384]{2,1,0:T(8,128)}, f32[64,8,384]{2,1,0:T(8,128)}, u32[]{:S(2)}, u32[]{:S(2)}) collective-permute-start(f32[64,8,384]{2,1,0:T(8,128)} %add_bitcast_fusion), channel_id=1, source_target_pairs={{0,2},{1,3},{2,0},{3,1},{4,6},{5,7},{6,4},{7,5},{8,10},{9,11},{10,... | collective-permute-start | bytes 2359304 | tf_op jit(solution)/shard_map/ppermute | solution.py:274
  141.5 30.3 %all-to-all-start.1 = ((bf16[64,8,384]{2,1,0:T(8,128)(2,1)}), bf16[64,8,384]{2,1,0:T(8,128)(2,1)S(1)}, u32[]{:S(2)}, u32[]{:S(2)}) async-start(bf16[64,8,384]{2,1,0:T(8,128)(2,1)} %fusion.6), calls=%async_computation.1 | async-start | bytes 786432 | tf_op jit(solution)/shard_map/all_to_all | solution.py:264
  171.8 21.2 %all-to-all-start = ((bf16[64,8,384]{2,1,0:T(8,128)(2,1)}), bf16[64,8,384]{2,1,0:T(8,128)(2,1)S(1)}, u32[]{:S(2)}, u32[]{:S(2)}) async-start(bf16[64,8,384]{2,1,0:T(8,128)(2,1)} %fusion.3), calls=%async_computation | async-start | bytes 786432 | tf_op jit(solution)/shard_map/all_to_all | solution.py:264
  (5 other events, 4.5 us)

commit v5 on v4

--- a/solution.py
+++ b/solution.py
@@ -38,24 +38,28 @@
     return [(i * 4 + o, i * 4 + (o ^ mask)) for i in range(n_occ) for o in range(4)]
 
 
-def round1(i, core):
-    if core == 0:
-        return i + 1, 1
-    return (i + RING, 0) if i % RING else (i, 0)
-
-
-def round2(i, core):
-    if core == 1:
-        return i + 1, 0
-    return i - i % RING + (i - 1) % RING, 1
-
-
-def round3(i, core):
-    return (i + 1, 1) if core == 0 else (i - 1, 0)
-
-
-def round4(i, core):
-    return (i + 1, 0) if core == 1 else (i - 1, 1)
+def up(i, core):
+    return i + 1, core
+
+
+def down(i, core):
+    return i - 1, core
+
+
+def over(i, core):
+    return (i + RING, core) if i % RING else (i, core)
+
+
+def row_down(i, core):
+    return i - i % RING + (i - 1) % RING, core
+
+
+def last_a(i, core):
+    return (i + 1, 0) if core == 0 else (i - 1, 1)
+
+
+def last_b(i, core):
+    return (i - 1, 1) if core == 0 else (i + 1, 0)
 
 
 def sds(shape, dtype):
@@ -155,19 +159,34 @@
     n_vir, n_aux = own.shape
     half = n_vir // 2
     h = chip ^ (occ_index // (n_occ // 2))
-    partners = [(occ_index - jnp.where(core == 0, a, b)) % n_occ for a, b in ((0, 1), (2, 7), (6, 3), (4, 5))]
+    partners = [(occ_index - jnp.where(core == 0, a, b)) % n_occ for a, b in ((1, 0), (2, 7), (3, 6), (4, 5))]
     sc = jnp.stack([h, core, chip, occ_index, *partners]).astype(jnp.int32)
 
-    def ring(x, rule):
-        return lax.ppermute(x, BOTH, moves(n_occ, rule))
+    def send(x, pairs):
+        return lax.ppermute(x, BOTH, pairs)
 
     def exchange(s):
-        return lax.ppermute(s, BOTH, swap(n_occ, 2))
+        return send(s, swap(n_occ, 2))
+
+    def other_core(x):
+        return send(x, swap(n_occ, 1))
+
+    def choose(a, b):
+        return jnp.where(core == 0, a, b)
 
     tile = n_aux // 2
-    x0 = [lax.dynamic_slice(own, (h * half, p * tile), (half, tile)) for p in range(2)]
-    x1 = [ring(x0[p], round1) for p in range(2)]
-    x2 = [ring(x1[p], round2) for p in range(2)]
+    x0m, x0o = [lax.dynamic_slice(own, (h * half, c * tile), (half, tile)) for c in (core, 1 - core)]
+    p1 = send(x0m, moves(n_occ, up))
+    m1 = send(x0m, moves(n_occ, over))
+    p2 = send(p1, moves(n_occ, up))
+    m2 = send(m1, moves(n_occ, row_down))
+    p3 = send(p2, moves(n_occ, up))
+    m3 = send(m2, moves(n_occ, down))
+    a3, b3 = choose(p3, m3), choose(m3, p3)
+    x1 = [choose(p1, x0m), choose(other_core(p1), x0o)]
+    x2 = [choose(p2, m2), other_core(choose(m2, p2))]
+    x3 = [a3, other_core(b3)]
+    x4 = [send(a3, moves(n_occ, last_a)), send(b3, moves(n_occ, last_b))]
 
     ev = lookup(vir_level, vir_table)
     eo = lookup(occ_level, occupied_energy_levels)
@@ -182,7 +201,7 @@
                 num_scalar_prefetch=1,
                 grid=(2,),
                 in_specs=[
-                    pl.BlockSpec((n_vir, tile), lambda t, s: (0, t)),
+                    pl.BlockSpec((n_vir, tile), lambda t, s: (0, (t + s[1]) % 2)),
                     pl.BlockSpec((half, tile), lambda t, s: (0, 0)),
                     pl.BlockSpec((half, tile), lambda t, s: (0, 0)),
                     pl.BlockSpec((half, 128), lambda t, s: (0, 0)),
@@ -203,7 +222,8 @@
         pl.BlockSpec((half, tile_p), lambda t, s: (0, jnp.minimum(t, 1))),
         pl.BlockSpec((half, tile_p), lambda t, s: (0, jnp.maximum(t - 2, 0))),
     ]
-    row_spec = pl.BlockSpec((tile_p, n_vir), lambda t, s: (t, 0))
+    where_p = lambda t, s: (t + 2 * s[1]) % tiles
+    row_spec = pl.BlockSpec((tile_p, n_vir), lambda t, s: (where_p(t, s), 0))
 
     def gamma(xs, mixes, early=()):
         n = len(xs)
@@ -221,18 +241,13 @@
             name="gamma",
         )(sc, *(a for x in xs for a in x), *(m for mix in mixes for m in mix), *early)
 
-    y1 = [jnp.where(core == 0, x0[p], x1[p]) for p in range(2)]
-    s1, v1 = amp(y1, 0, F32)
+    s1, v1 = amp(x1, 0, F32)
     q1 = exchange(s1)
-    x3 = [ring(x2[p], round3) for p in range(2)]
     s2, v2 = amp(x2, 1, F32)
     q2 = exchange(s2)
-    x4 = [ring(x3[p], round4) for p in range(2)]
     s3, v3 = amp(x3, 2, F32)
     q3 = exchange(s3)
-    early = gamma([y1, x2], [(s1, q1, v1), (s2, q2, v2)])
-    x4[0], _ = lax.optimization_barrier((x4[0], s3))
-    x4[1], early = lax.optimization_barrier((x4[1], early))
+    early = gamma([x1, x2], [(s1, q1, v1), (s2, q2, v2)])
     s4, v4 = amp(x4, 3, BF16)
     q4 = exchange(s4)
     v3, _ = lax.optimization_barrier((v3, s4))
@@ -246,7 +261,7 @@
             num_scalar_prefetch=1,
             grid=(tiles,),
             in_specs=x_specs + [whole] * 3 + [row_spec],
-            out_specs=[pl.BlockSpec((groups, 2, 8, half), lambda t, s: (t, 0, 0, 0))] * 4,
+            out_specs=[pl.BlockSpec((groups, 2, 8, half), lambda t, s: (where_p(t, s), 0, 0, 0))] * 4,
             scratch_shapes=[pltpu.VMEM((half, n_vir), BF16)],
         ),
         cost_estimate=cost(2 * n_aux * half * n_vir, 2 * n_aux * (4 * n_vir + half)),

time: 198 us -> 225 us (1.14)
  waiting for transfers between devices: 78.1 us -> 91 us
  starting transfers between devices: 44.6 us -> 56.8 us
  other arithmetic: 12 us -> 14.4 us
    ppermute x12 -> x15, waiting for transfers between devices: 41.1 us -> 53.9 us  [send(): return lax.ppermute(x, BOTH, pairs)]
    all_to_all x2, starting transfers between devices: 21.9 us -> 31.3 us  [finish(): mine = lax.all_to_all(low, 'occ', split_axis=0, concat_axis=0, tiled=True)]
    all_to_all x2, waiting for transfers between devices: 22.9 us -> 26.2 us  [finish(): mine = lax.all_to_all(low, 'occ', split_axis=0, concat_axis=0, tiled=True)]
    ppermute x1, waiting for transfers between devices: 2.53 us -> 0.01 us  [body(): far1 = lax.ppermute(away1, BOTH, swap(n_occ, 2))]
    select_n x2 -> x4, other arithmetic: 3.35 us -> 5.82 us  [choose(): return jnp.where(core == 0, a, b)]
    ppermute x12 -> x15, starting transfers between devices: 21.1 us -> 22.2 us  [send(): return lax.ppermute(x, BOTH, pairs)]
  transfers between devices with their start and end apart: 18 -> 21, of which waited for: 9 -> 12; matrix products, arithmetic and copies ran while one was open for 8% -> 8% of each run, Pallas kernels for 20% -> 18%
where the time goes in v5:
time: 225 us; the launch traced here: 223 us
  waiting for transfers between devices  91 us (40%)
  starting transfers between devices  56.8 us (25%)
  Pallas kernels  48.5 us (22%)
  other arithmetic  14.4 us (6%)
  local copies, waits for them, and re-layouts  6.88 us (3%)
  matrix products  5.01 us (2%)
    ppermute x15, waiting for transfers between devices, send(): return lax.ppermute(x, BOTH, pairs)  53.9 us
    all_to_all x2, starting transfers between devices, finish(): mine = lax.all_to_all(low, 'occ', split_axis=0, concat_axis=0, tiled=True)  31.3 us
    all_to_all x2, waiting for transfers between devices, finish(): mine = lax.all_to_all(low, 'occ', split_axis=0, concat_axis=0, tiled=True)  26.2 us
    ppermute x15, starting transfers between devices, send(): return lax.ppermute(x, BOTH, pairs)  22.2 us
    pallas_call x4, Pallas kernels, amp(): pl.pallas_call(functools.partial(amp_kernel, half=half, slot=slot), out_s...  21.9 us
    pallas_call x2, Pallas kernels, gamma(): pl.pallas_call(functools.partial(gamma_kernel, n=n, half=half, early=len(...  18.1 us
    pallas_call x1, Pallas kernels, body(): pl.pallas_call(functools.partial(last_kernel, half=half), out_shape=(sds(...  8.4 us
    ppermute x1, waiting for transfers between devices, body(): far0 = lax.ppermute(away0, BOTH, swap(n_occ, 2))  7.7 us
  transfers between devices with their start and end apart: 21, of which 12 were waited for; matrix products, arithmetic and copies ran while one was open for 8% of the time, Pallas kernels for 18%

profile of v5, /device:TPU:56, one launch (start us, length us, event | category | flops | bytes accessed | tf_op | source)
XLA Modules:
  0.0 222.7 jit_solution(10095039628596197075)
XLA Ops:
  1.3 2.0 collective-permute-start
  3.3 4.3 %collective-permute-start.3 = (bf16[384,1024]{1,0:T(8,128)(2,1)S(1)}, bf16[384,1024]{1,0:T(8,128)(2,1)S(1)}, u32[]{:S(2)}, u32[]{:S(2)}) collective-permute-start(bf16[384,1024]{1,0:T(8,128)(2,1)S(1)} %dynamic-slice_bitcast_fusion), channel_id=1, source_target_pairs={{0,0},{1,1},{2,2},{3,3},{4,36},{5,37},{6,38},{7,39},{8,40},{9,41},... | collective-permute-start | bytes 2359304 | tf_op jit(solution)/shard_map/ppermute | solution.py:166
  7.6 13.0 %collective-permute-done = bf16[384,1024]{1,0:T(8,128)(2,1)S(1)} collective-permute-done((bf16[384,1024]{1,0:T(8,128)(2,1)S(1)}, bf16[384,1024]{1,0:T(8,128)(2,1)S(1)}, u32[]{:S(2)}, u32[]{:S(2)}) %collective-permute-start) | collective-permute-done | bytes 786464 | tf_op jit(solution)/shard_map/ppermute | solution.py:166
  20.6 1.9 collective-permute-start.1
  22.5 1.6 collective-permute-done.3
  25.0 17.0 %collective-permute-done.1 = bf16[384,1024]{1,0:T(8,128)(2,1)S(1)} collective-permute-done((bf16[384,1024]{1,0:T(8,128)(2,1)S(1)}, bf16[384,1024]{1,0:T(8,128)(2,1)S(1)}, u32[]{:S(2)}, u32[]{:S(2)}) %collective-permute-start.1) | collective-permute-done | bytes 786464 | tf_op jit(solution)/shard_map/ppermute | solution.py:166
  42.5 5.8 %collective-permute-start.5 = (bf16[384,1024]{1,0:T(8,128)(2,1)S(1)}, bf16[384,1024]{1,0:T(8,128)(2,1)}, u32[]{:S(2)}, u32[]{:S(2)}) collective-permute-start(bf16[384,1024]{1,0:T(8,128)(2,1)S(1)} %collective-permute-done.4), channel_id=1, source_target_pairs={{0,254},{1,255},{2,252},{3,253},{4,0},{5,1},{6,2},{7,3},{8,4},{9,5... | collective-permute-start | bytes 2359304 | tf_op jit(solution)/shard_map/ppermute | solution.py:166
  52.4 9.5 %collective-permute-done.2 = bf16[384,1024]{1,0:T(8,128)(2,1)S(1)} collective-permute-done((bf16[384,1024]{1,0:T(8,128)(2,1)S(1)}, bf16[384,1024]{1,0:T(8,128)(2,1)S(1)}, u32[]{:S(2)}, u32[]{:S(2)}) %collective-permute-start.2) | collective-permute-done | bytes 786464 | tf_op jit(solution)/shard_map/ppermute | solution.py:166
  61.9 1.4 collective-permute-done.5
  63.3 2.1 broadcast_select_fusion.3
  66.7 2.7 %collective-permute-start.7 = (bf16[384,1024]{1,0:T(8,128)(2,1)S(1)}, bf16[384,1024]{1,0:T(8,128)(2,1)}, u32[]{:S(2)}, u32[]{:S(2)}) collective-permute-start(bf16[384,1024]{1,0:T(8,128)(2,1)S(1)} %get-tuple-element.35), channel_id=1, source_target_pairs={{0,255},{1,4},{2,253},{3,6},{4,1},{5,8},{6,3},{7,10},{8,5},{9,12},... | collective-permute-start | bytes 2359304 | tf_op jit(solution)/shard_map/ppermute | solution.py:166
  71.4 5.5 %amp.6 = (f32[384,384]{1,0:T(8,128)}, bf16[384,384]{1,0:T(8,128)(2,1)}) custom-call(s32[8]{0:T(128)} %stack.35.sc, bf16[768,2048]{1,0:T(8,128)(2,1)} %bitcast.51, bf16[384,1024]{1,0:T(8,128)(2,1)} %broadcast_select_fusion.2.xa.refs_0_, bf16[384,1024]{1,0:T(8,128)(2,1)} %bitcast_select_fusion.xb.refs_1_, f32[384,128]{1,0:T(8,128)} %broadcast_in_dim.41.evc, ...), custom_call_target="tpu_custom_call" | custom-call | flops 1207959552 | bytes 4718592 | tf_op jit(solution)/shard_map/amp/pallas_call | solution.py:197
  78.3 5.5 %amp.7 = (f32[384,384]{1,0:T(8,128)}, bf16[384,384]{1,0:T(8,128)(2,1)}) custom-call(s32[8]{0:T(128)} %stack.35.sc, bf16[768,2048]{1,0:T(8,128)(2,1)} %bitcast.52, bf16[384,1024]{1,0:T(8,128)(2,1)} %get-tuple-element.34.xa.refs_2_, bf16[384,1024]{1,0:T(8,128)(2,1)} %collective-permute-done.12.xb.refs_3_, f32[384,128]{1,0:T(8,128)} %broadcast_in_dim.41.evc, ...), custom_call_target="tpu_custom_call" | custom-call | flops 1207959552 | bytes 4718592 | tf_op jit(solution)/shard_map/amp/pallas_call | solution.py:197
  84.4 5.5 %amp.5 = (f32[384,384]{1,0:T(8,128)}, bf16[384,384]{1,0:T(8,128)(2,1)}) custom-call(s32[8]{0:T(128)} %stack.35.sc, bf16[768,2048]{1,0:T(8,128)(2,1)} %bitcast.53, bf16[384,1024]{1,0:T(8,128)(2,1)} %get-tuple-element.36.xa.refs_0_, bf16[384,1024]{1,0:T(8,128)(2,1)} %collective-permute-done.9.xb.refs_1_, f32[384,128]{1,0:T(8,128)} %broadcast_in_dim.41.evc, ...), custom_call_target="tpu_custom_call" | custom-call | flops 1207959552 | bytes 4718592 | tf_op jit(solution)/shard_map/amp/pallas_call | solution.py:197
  91.3 5.4 %amp.4 = (bf16[384,384]{1,0:T(8,128)(2,1)}, bf16[384,384]{1,0:T(8,128)(2,1)}) custom-call(s32[8]{0:T(128)} %stack.35.sc, bf16[768,2048]{1,0:T(8,128)(2,1)} %bitcast.54, bf16[384,1024]{1,0:T(8,128)(2,1)} %collective-permute-done.6.xa, bf16[384,1024]{1,0:T(8,128)(2,1)} %collective-permute-done.7.xb, f32[384,128]{1,0:T(8,128)} %broadcast_in_dim.41.evc, ...), custom_call_target="tpu_custom_call" | custom-call | flops 1207959552 | bytes 4718592 | tf_op jit(solution)/shard_map/amp/pallas_call | solution.py:197
  97.4 8.6 %collective-permute-done.14.refs_8_ = f32[384,384]{1,0:T(8,128)S(1)} collective-permute-done((f32[384,384]{1,0:T(8,128)}, f32[384,384]{1,0:T(8,128)S(1)}, u32[]{:S(2)}, u32[]{:S(2)}) %collective-permute-start.14) | collective-permute-done | bytes 589856 | tf_op jit(solution)/shard_map/ppermute | solution.py:166
  106.8 9.5 %gamma.2.refs_5_ = f32[2048,768]{1,0:T(8,128)} custom-call(s32[8]{0:T(128)} %stack.35.sc, bf16[384,1024]{1,0:T(8,128)(2,1)} %broadcast_select_fusion.2.xa.refs_0_, bf16[384,1024]{1,0:T(8,128)(2,1)} %bitcast_select_fusion.xb.refs_1_, bf16[384,1024]{1,0:T(8,128)(2,1)} %get-tuple-element.34.xa.refs_2_, bf16[384,1024]{1,0:T(8,128)(2,1)} %collective-permute-done.12.xb.refs_3_, ...), custom_call_target="tpu_custom_call" | custom-call | flops 2415919104 | bytes 9437184 | tf_op jit(solution)/shard_map/gamma/pallas_call | solution.py:230
  116.3 2.3 %collective-permute-done.10.refs_3_ = f32[384,384]{1,0:T(8,128)S(1)} collective-permute-done((f32[384,384]{1,0:T(8,128)}, f32[384,384]{1,0:T(8,128)S(1)}, u32[]{:S(2)}, u32[]{:S(2)}) %collective-permute-start.10) | collective-permute-done | bytes 589856 | tf_op jit(solution)/shard_map/ppermute | solution.py:166
  119.4 8.7 %gamma.3.early = f32[2048,768]{1,0:T(8,128)} custom-call(s32[8]{0:T(128)} %stack.35.sc, bf16[384,1024]{1,0:T(8,128)(2,1)} %get-tuple-element.36.xa.refs_0_, bf16[384,1024]{1,0:T(8,128)(2,1)} %collective-permute-done.9.xb.refs_1_, f32[384,384]{1,0:T(8,128)} %get-tuple-element.21.refs_2_, f32[384,384]{1,0:T(8,128)} %copy-done.6, ...), custom_call_target="tpu_custom_call" | custom-call | flops 1207959552 | bytes 7864320 | tf_op jit(solution)/shard_map/gamma/pallas_call | solution.py:230
  128.8 8.4 %last.1 = (f32[64,2,8,384]{3,2,1,0:T(8,128)}, f32[64,2,8,384]{3,2,1,0:T(8,128)}, f32[64,2,8,384]{3,2,1,0:T(8,128)}, f32[64,2,8,384]{3,2,1,0:T(8,128)}) custom-call(s32[8]{0:T(128)} %stack.35.sc, bf16[384,1024]{1,0:T(8,128)(2,1)} %collective-permute-done.6.xa, bf16[384,1024]{1,0:T(8,128)(2,1)} %collective-permute-done.7.xb, ...), custom_call_target="tpu_custom_call" | custom-call | flops 1207959552 | bytes 14155776 | tf_op jit(solution)/shard_map/last/pallas_call | solution.py:257
  137.8 3.1 %collective-permute-done.16 = f32[64,2,8,384]{3,2,1,0:T(8,128)S(1)} collective-permute-done((f32[64,2,8,384]{3,2,1,0:T(8,128)}, f32[64,2,8,384]{3,2,1,0:T(8,128)S(1)}, u32[]{:S(2)}, u32[]{:S(2)}) %collective-permute-start.16) | collective-permute-done | bytes 1572896 | tf_op jit(solution)/shard_map/ppermute | solution.py:283
  143.4 1.4 collective-permute-start.17
  144.8 2.1 add_bitcast_fusion
  146.9 7.7 %collective-permute-done.17 = bf16[64,8,384]{2,1,0:T(8,128)(2,1)S(1)} collective-permute-done((bf16[64,8,384]{2,1,0:T(8,128)(2,1)S(1)}, bf16[64,8,384]{2,1,0:T(8,128)(2,1)S(1)}, u32[]{:S(2)}, u32[]{:S(2)}) %collective-permute-start.17) | collective-permute-done | bytes 393248 | tf_op jit(solution)/shard_map/ppermute | solution.py:285
  155.9 2.0 fusion.6
  157.9 25.0 %all-to-all-start.1 = ((bf16[64,8,384]{2,1,0:T(8,128)(2,1)}), bf16[64,8,384]{2,1,0:T(8,128)(2,1)S(1)}, u32[]{:S(2)}, u32[]{:S(2)}) async-start(bf16[64,8,384]{2,1,0:T(8,128)(2,1)} %fusion.6), calls=%async_computation.1 | async-start | bytes 786432 | tf_op jit(solution)/shard_map/all_to_all | solution.py:279
  183.0 2.3 %fusion.3 = bf16[64,8,384]{2,1,0:T(8,128)(2,1)} fusion(f32[64,8,384]{2,1,0:T(8,128)} %collective-permute-done.18, f32[64,2,8,384]{3,2,1,0:T(8,128)} %collective-permute-done.15, s32[]{:T(128)S(6)} %select_n.126, f32[64,2,8,384]{3,2,1,0:T(8,128)S(1)} %copy-done.1), kind=kLoop, calls=%fused_computation.6 | loop fusion | flops 589824 | bytes 2752516 | tf_op jit(solution)/shard_map/convert_element_type | solution.py:276
  185.2 13.2 %all-to-all-done.1 = bf16[64,8,384]{2,1,0:T(8,128)(2,1)S(1)} async-done(((bf16[64,8,384]{2,1,0:T(8,128)(2,1)}), bf16[64,8,384]{2,1,0:T(8,128)(2,1)S(1)}, u32[]{:S(2)}, u32[]{:S(2)}) %all-to-all-start.1) | async-done | bytes 393248 | tf_op jit(solution)/shard_map/all_to_all | solution.py:279
  198.4 6.3 %all-to-all-start = ((bf16[64,8,384]{2,1,0:T(8,128)(2,1)}), bf16[64,8,384]{2,1,0:T(8,128)(2,1)S(1)}, u32[]{:S(2)}, u32[]{:S(2)}) async-start(bf16[64,8,384]{2,1,0:T(8,128)(2,1)} %fusion.3), calls=%async_computation | async-start | bytes 786432 | tf_op jit(solution)/shard_map/all_to_all | solution.py:279
  204.7 1.8 fusion.4
  206.5 13.0 %all-to-all-done = bf16[64,8,384]{2,1,0:T(8,128)(2,1)S(1)} async-done(((bf16[64,8,384]{2,1,0:T(8,128)(2,1)}), bf16[64,8,384]{2,1,0:T(8,128)(2,1)S(1)}, u32[]{:S(2)}, u32[]{:S(2)}) %all-to-all-start) | async-done | bytes 393248 | tf_op jit(solution)/shard_map/all_to_all | solution.py:279
  219.6 3.2 %convolution_add_fusion = f32[64,8,1024]{2,1,0:T(8,128)} fusion(f32[64,8,1024]{2,1,0:T(8,128)S(1)} %fusion.4, bf16[64,8,384]{2,1,0:T(8,128)(2,1)S(1)} %all-to-all-done, bf16[768,1024]{1,0:T(8,128)(2,1)} %param.11), kind=kOutput, calls=%fused_computation | convolution fusion | flops 403177472 | bytes 5373952 | tf_op jit(solution)/shard_map/sbd,dw->sbw/dot_general | solution.py:281
  (58 shorter events, 20.7 us)
Async XLA Ops:
  0.0 48.2 %copy-start.9 = (f32[256]{0:T(256)S(1)}, f32[256]{0:T(256)}, u32[]{:S(2)}) copy-start(f32[256]{0:T(256)} %param.10) | copy-start | bytes 3076
  0.0 48.2 %copy-start.8 = (s32[768]{0:T(1024)S(1)}, s32[768]{0:T(1024)}, u32[]{:S(2)}) copy-start(s32[768]{0:T(1024)} %param.8) | copy-start | bytes 9220
  0.0 49.9 %copy-start.11 = (s32[64]{0:T(128)S(1)}, s32[64]{0:T(128)}, u32[]{:S(2)}) copy-start(s32[64]{0:T(128)} %param.7) | copy-start | bytes 772
  0.0 49.9 %copy-start.10 = (f32[256]{0:T(256)S(1)}, f32[256]{0:T(256)}, u32[]{:S(2)}) copy-start(f32[256]{0:T(256)} %param.9) | copy-start | bytes 3076
  1.3 19.4 %collective-permute-start = (bf16[384,1024]{1,0:T(8,128)(2,1)S(1)}, bf16[384,1024]{1,0:T(8,128)(2,1)S(1)}, u32[]{:S(2)}, u32[]{:S(2)}) collective-permute-start(bf16[384,1024]{1,0:T(8,128)(2,1)S(1)} %dynamic-slice_bitcast_fusion), channel_id=1, source_target_pairs={{0,4},{1,5},{2,6},{3,7},{4,8},{5,9},{6,10},{7,11},{8,12},{9,13},{1... | collective-permute-start | bytes 2359304 | tf_op jit(solution)/shard_map/ppermute | solution.py:166
  3.3 20.9 %collective-permute-start.3 = (bf16[384,1024]{1,0:T(8,128)(2,1)S(1)}, bf16[384,1024]{1,0:T(8,128)(2,1)S(1)}, u32[]{:S(2)}, u32[]{:S(2)}) collective-permute-start(bf16[384,1024]{1,0:T(8,128)(2,1)S(1)} %dynamic-slice_bitcast_fusion), channel_id=1, source_target_pairs={{0,0},{1,1},{2,2},{3,3},{4,36},{5,37},{6,38},{7,39},{8,40},{9,41},... | collective-permute-start | bytes 2359304 | tf_op jit(solution)/shard_map/ppermute | solution.py:166
  20.6 21.4 %collective-permute-start.1 = (bf16[384,1024]{1,0:T(8,128)(2,1)S(1)}, bf16[384,1024]{1,0:T(8,128)(2,1)S(1)}, u32[]{:S(2)}, u32[]{:S(2)}) collective-permute-start(bf16[384,1024]{1,0:T(8,128)(2,1)S(1)} %collective-permute-done), channel_id=1, source_target_pairs={{0,4},{1,5},{2,6},{3,7},{4,8},{5,9},{6,10},{7,11},{8,12},{9,13},{1... | collective-permute-start | bytes 2359304 | tf_op jit(solution)/shard_map/ppermute | solution.py:166
  24.1 18.3 %collective-permute-start.4 = (bf16[384,1024]{1,0:T(8,128)(2,1)S(1)}, bf16[384,1024]{1,0:T(8,128)(2,1)S(1)}, u32[]{:S(2)}, u32[]{:S(2)}) collective-permute-start(bf16[384,1024]{1,0:T(8,128)(2,1)S(1)} %collective-permute-done.3), channel_id=1, source_target_pairs={{0,28},{1,29},{2,30},{3,31},{4,0},{5,1},{6,2},{7,3},{8,4},{9,5},{1... | collective-permute-start | bytes 2359304 | tf_op jit(solution)/shard_map/ppermute | solution.py:166
  42.0 20.0 %collective-permute-start.2 = (bf16[384,1024]{1,0:T(8,128)(2,1)S(1)}, bf16[384,1024]{1,0:T(8,128)(2,1)S(1)}, u32[]{:S(2)}, u32[]{:S(2)}) collective-permute-start(bf16[384,1024]{1,0:T(8,128)(2,1)S(1)} %collective-permute-done.1), channel_id=1, source_target_pairs={{0,4},{1,5},{2,6},{3,7},{4,8},{5,9},{6,10},{7,11},{8,12},{9,13},{1... | collective-permute-start | bytes 2359304 | tf_op jit(solution)/shard_map/ppermute | solution.py:166
  42.5 20.9 %collective-permute-start.5 = (bf16[384,1024]{1,0:T(8,128)(2,1)S(1)}, bf16[384,1024]{1,0:T(8,128)(2,1)}, u32[]{:S(2)}, u32[]{:S(2)}) collective-permute-start(bf16[384,1024]{1,0:T(8,128)(2,1)S(1)} %collective-permute-done.4), channel_id=1, source_target_pairs={{0,254},{1,255},{2,252},{3,253},{4,0},{5,1},{6,2},{7,3},{8,4},{9,5... | collective-permute-start | bytes 2359304 | tf_op jit(solution)/shard_map/ppermute | solution.py:166
  50.6 18.8 %collective-permute-start.11 = (bf16[384,1024]{1,0:T(8,128)(2,1)S(1)}, bf16[384,1024]{1,0:T(8,128)(2,1)S(1)}, u32[]{:S(2)}, u32[]{:S(2)}) collective-permute-start(bf16[384,1024]{1,0:T(8,128)(2,1)S(1)} %collective-permute-done), channel_id=1, source_target_pairs={{0,1},{1,0},{2,3},{3,2},{4,5},{5,4},{6,7},{7,6},{8,9},{9,8},{10,11... | collective-permute-start | bytes 2359304 | tf_op jit(solution)/shard_map/ppermute | solution.py:166
  51.9 13.6 %copy-start = (bf16[1,768,2048]{2,1,0:T(8,128)(2,1)S(1)}, bf16[1,768,2048]{2,1,0:T(8,128)(2,1)}, u32[]{:S(2)}) copy-start(bf16[1,768,2048]{2,1,0:T(8,128)(2,1)} %param.6) | copy-start | bytes 9437188
  51.9 26.4 %collective-permute-start.12 = (bf16[384,1024]{1,0:T(8,128)(2,1)}, bf16[384,1024]{1,0:T(8,128)(2,1)}, u32[]{:S(2)}, u32[]{:S(2)}) collective-permute-start(bf16[384,1024]{1,0:T(8,128)(2,1)} %get-tuple-element.33), channel_id=1, source_target_pairs={{0,1},{1,0},{2,3},{3,2},{4,5},{5,4},{6,7},{7,6},{8,9},{9,8},{10,11... | collective-permute-start | bytes 2359304 | tf_op jit(solution)/shard_map/ppermute | solution.py:166
  65.5 19.0 %collective-permute-start.9 = (bf16[384,1024]{1,0:T(8,128)(2,1)S(1)}, bf16[384,1024]{1,0:T(8,128)(2,1)}, u32[]{:S(2)}, u32[]{:S(2)}) collective-permute-start(bf16[384,1024]{1,0:T(8,128)(2,1)S(1)} %get-tuple-element.35), channel_id=1, source_target_pairs={{0,1},{1,0},{2,3},{3,2},{4,5},{5,4},{6,7},{7,6},{8,9},{9,8},{10,11... | collective-permute-start | bytes 2359304 | tf_op jit(solution)/shard_map/ppermute | solution.py:166
  66.7 24.6 %collective-permute-start.7 = (bf16[384,1024]{1,0:T(8,128)(2,1)S(1)}, bf16[384,1024]{1,0:T(8,128)(2,1)}, u32[]{:S(2)}, u32[]{:S(2)}) collective-permute-start(bf16[384,1024]{1,0:T(8,128)(2,1)S(1)} %get-tuple-element.35), channel_id=1, source_target_pairs={{0,255},{1,4},{2,253},{3,6},{4,1},{5,8},{6,3},{7,10},{8,5},{9,12},... | collective-permute-start | bytes 2359304 | tf_op jit(solution)/shard_map/ppermute | solution.py:166
  69.4 21.9 %collective-permute-start.6 = (bf16[384,1024]{1,0:T(8,128)(2,1)}, bf16[384,1024]{1,0:T(8,128)(2,1)}, u32[]{:S(2)}, u32[]{:S(2)}) collective-permute-start(bf16[384,1024]{1,0:T(8,128)(2,1)} %get-tuple-element.36.xa.refs_0_), channel_id=1, source_target_pairs={{0,4},{1,255},{2,6},{3,253},{4,8},{5,1},{6,10},{7,3},{8,12},{9,5},... | collective-permute-start | bytes 2359304 | tf_op jit(solution)/shard_map/ppermute | solution.py:166
  76.9 20.5 %collective-permute-start.13 = (f32[384,384]{1,0:T(8,128)}, f32[384,384]{1,0:T(8,128)S(1)}, u32[]{:S(2)}, u32[]{:S(2)}) collective-permute-start(f32[384,384]{1,0:T(8,128)} %get-tuple-element.24.refs_4_), channel_id=1, source_target_pairs={{0,2},{1,3},{2,0},{3,1},{4,6},{5,7},{6,4},{7,5},{8,10},{9,11},{10,... | collective-permute-start | bytes 1769480 | tf_op jit(solution)/shard_map/ppermute | solution.py:166
  83.8 22.2 %collective-permute-start.14 = (f32[384,384]{1,0:T(8,128)}, f32[384,384]{1,0:T(8,128)S(1)}, u32[]{:S(2)}, u32[]{:S(2)}) collective-permute-start(f32[384,384]{1,0:T(8,128)} %get-tuple-element.26.refs_7_), channel_id=1, source_target_pairs={{0,2},{1,3},{2,0},{3,1},{4,6},{5,7},{6,4},{7,5},{8,10},{9,11},{10,... | collective-permute-start | bytes 1769480 | tf_op jit(solution)/shard_map/ppermute | solution.py:166
  89.9 28.7 %collective-permute-start.10 = (f32[384,384]{1,0:T(8,128)}, f32[384,384]{1,0:T(8,128)S(1)}, u32[]{:S(2)}, u32[]{:S(2)}) collective-permute-start(f32[384,384]{1,0:T(8,128)} %get-tuple-element.21.refs_2_), channel_id=1, source_target_pairs={{0,2},{1,3},{2,0},{3,1},{4,6},{5,7},{6,4},{7,5},{8,10},{9,11},{10,... | collective-permute-start | bytes 1769480 | tf_op jit(solution)/shard_map/ppermute | solution.py:166
  96.7 31.4 %collective-permute-start.8 = (bf16[384,384]{1,0:T(8,128)(2,1)}, bf16[384,384]{1,0:T(8,128)(2,1)S(1)}, u32[]{:S(2)}, u32[]{:S(2)}) collective-permute-start(bf16[384,384]{1,0:T(8,128)(2,1)} %get-tuple-element.19.s), channel_id=1, source_target_pairs={{0,2},{1,3},{2,0},{3,1},{4,6},{5,7},{6,4},{7,5},{8,10},{9,11},{10,... | collective-permute-start | bytes 884744 | tf_op jit(solution)/shard_map/ppermute | solution.py:166
  97.4 8.6 %copy-start.4 = (f32[384,384]{1,0:T(8,128)}, f32[384,384]{1,0:T(8,128)S(1)}, u32[]{:S(2)}) copy-start(f32[384,384]{1,0:T(8,128)S(1)} %collective-permute-done.13.refs_5_) | copy-start | bytes 1769476
  106.0 0.8 copy-start.5
  118.6 0.8 copy-start.6
  137.2 7.5 %copy-start.1 = (f32[64,2,8,384]{3,2,1,0:T(8,128)S(1)}, f32[64,2,8,384]{3,2,1,0:T(8,128)}, u32[]{:S(2)}) copy-start(f32[64,2,8,384]{3,2,1,0:T(8,128)} %get-tuple-element.28) | copy-start | bytes 4718596
  137.2 3.7 %collective-permute-start.16 = (f32[64,2,8,384]{3,2,1,0:T(8,128)}, f32[64,2,8,384]{3,2,1,0:T(8,128)S(1)}, u32[]{:S(2)}, u32[]{:S(2)}) collective-permute-start(f32[64,2,8,384]{3,2,1,0:T(8,128)} %get-tuple-element.31), channel_id=1, source_target_pairs={{0,1},{1,0},{2,3},{3,2},{4,5},{5,4},{6,7},{7,6},{8,9},{9,8},{10,11... | collective-permute-start | bytes 4718600 | tf_op jit(solution)/shard_map/ppermute | solution.py:283
  137.3 7.4 %collective-permute-start.15 = (f32[64,2,8,384]{3,2,1,0:T(8,128)}, f32[64,2,8,384]{3,2,1,0:T(8,128)}, u32[]{:S(2)}, u32[]{:S(2)}) collective-permute-start(f32[64,2,8,384]{3,2,1,0:T(8,128)} %get-tuple-element.29), channel_id=1, source_target_pairs={{0,1},{1,0},{2,3},{3,2},{4,5},{5,4},{6,7},{7,6},{8,9},{9,8},{10,11... | collective-permute-start | bytes 4718600 | tf_op jit(solution)/shard_map/ppermute | solution.py:286
  140.9 1.2 copy-start.3
  143.3 12.6 %copy-start.2 = (f32[64,2,8,384]{3,2,1,0:T(8,128)S(1)}, f32[64,2,8,384]{3,2,1,0:T(8,128)}, u32[]{:S(2)}) copy-start(f32[64,2,8,384]{3,2,1,0:T(8,128)} %get-tuple-element.30) | copy-start | bytes 4718596
  143.4 11.2 %collective-permute-start.17 = (bf16[64,8,384]{2,1,0:T(8,128)(2,1)S(1)}, bf16[64,8,384]{2,1,0:T(8,128)(2,1)S(1)}, u32[]{:S(2)}, u32[]{:S(2)}) collective-permute-start(bf16[64,8,384]{2,1,0:T(8,128)(2,1)S(1)} %fusion.10), channel_id=1, source_target_pairs={{0,2},{1,3},{2,0},{3,1},{4,6},{5,7},{6,4},{7,5},{8,10},{9,11},{10,... | collective-permute-start | bytes 1179656 | tf_op jit(solution)/shard_map/ppermute | solution.py:285
  154.6 28.4 %collective-permute-start.18 = (f32[64,8,384]{2,1,0:T(8,128)}, f32[64,8,384]{2,1,0:T(8,128)}, u32[]{:S(2)}, u32[]{:S(2)}) collective-permute-start(f32[64,8,384]{2,1,0:T(8,128)} %add_bitcast_fusion), channel_id=1, source_target_pairs={{0,2},{1,3},{2,0},{3,1},{4,6},{5,7},{6,4},{7,5},{8,10},{9,11},{10,... | collective-permute-start | bytes 2359304 | tf_op jit(solution)/shard_map/ppermute | solution.py:289
  157.9 40.5 %all-to-all-start.1 = ((bf16[64,8,384]{2,1,0:T(8,128)(2,1)}), bf16[64,8,384]{2,1,0:T(8,128)(2,1)S(1)}, u32[]{:S(2)}, u32[]{:S(2)}) async-start(bf16[64,8,384]{2,1,0:T(8,128)(2,1)} %fusion.6), calls=%async_computation.1 | async-start | bytes 786432 | tf_op jit(solution)/shard_map/all_to_all | solution.py:279
  198.4 21.2 %all-to-all-start = ((bf16[64,8,384]{2,1,0:T(8,128)(2,1)}), bf16[64,8,384]{2,1,0:T(8,128)(2,1)S(1)}, u32[]{:S(2)}, u32[]{:S(2)}) async-start(bf16[64,8,384]{2,1,0:T(8,128)(2,1)} %fusion.3), calls=%async_computation | async-start | bytes 786432 | tf_op jit(solution)/shard_map/all_to_all | solution.py:279
  (1 other events, 0.7 us)

commit v6 on v4

--- a/solution.py
+++ b/solution.py
@@ -88,18 +88,8 @@
         w_out[...] = (2.0 * mine - mine.T).astype(BF16)
 
 
-def fill(w, h, group, half, s, q, v):
-    def put(g, at):
-        @pl.when(h == g)
-        def _():
-            w[:, at : at + half] = v[...]
-
-        @pl.when(h != g)
-        def _():
-            w[:, at : at + half] = (2.0 * s[...].astype(F32) - q[...].astype(F32).T).astype(BF16)
-
-    for at, g in enumerate(group):
-        put(g, at * half)
+def fill(w, s, q):
+    w[...] = (2.0 * s[...].astype(F32) - q[...].astype(F32).T).astype(BF16)
 
 
 def products(xs, ws):
@@ -112,35 +102,44 @@
     return res
 
 
-def gamma_kernel(sc, *refs, n, half, early):
+def gamma_kernel(sc, *refs, n, half):
     xs = [refs[2 * k : 2 * k + 2] for k in range(n)]
-    mixes, refs = refs[2 * n : 5 * n], refs[5 * n :]
-    before = refs[0] if early else None
-    out, ws = refs[1 if early else 0], refs[2 if early else 1 :]
+    mixes, outs, ws = refs[2 * n : 5 * n], refs[5 * n : 5 * n + 2], refs[5 * n + 2 :]
 
     @pl.when(pl.program_id(0) == 0)
     def _():
         for k in range(n):
-            fill(ws[k], sc[0], (0, 1), half, *mixes[3 * k : 3 * k + 3])
+            s, q, v = mixes[3 * k : 3 * k + 3]
+            ws[k][:, :half] = v[...]
+            ws[k][:, half:] = (2.0 * s[...].astype(F32) - q[...].astype(F32).T).astype(BF16)
 
     res = products(xs, ws)
-    out[...] = res + before[...] if early else res
-
-
-def last_kernel(sc, xa, xb, s, q, v, early, keep0, keep1, send0, send1, w, *, half):
-    @pl.when(pl.program_id(0) == 0)
-    def _():
-        fill(w, sc[0], (0, 1), half, s, q, v)
-
-    res = early[...] + products([(xa, xb)], [w])
+    outs[0][...] = res[:, :half]
+    outs[1][...] = res[:, half:]
+
+
+def last_kernel(sc, *refs, n, mixed):
+    xs = [refs[2 * k : 2 * k + 2] for k in range(n)]
+    per = 2 if mixed else 1
+    mixes, refs = refs[2 * n : (2 + per) * n], refs[(2 + per) * n :]
+    early, keep, send, ws = refs[0], refs[1], refs[2], refs[3:]
+    if mixed:
+
+        @pl.when(pl.program_id(0) == 0)
+        def _():
+            for k in range(n):
+                fill(ws[k], *mixes[2 * k : 2 * k + 2])
+
+    else:
+        ws = mixes
+    res = early[...] + products(xs, ws)
     res = res.reshape(res.shape[0] // 32, 2, 2, 8, res.shape[1])
     a, b = res[:, :, 0], res[:, :, 1]
     first = sc[1] == 0
-    keep, send = jnp.where(first, a, b), jnp.where(first, b, a)
-    keep0[...] = keep[..., :half]
-    keep1[...] = keep[..., half:]
-    send0[...] = send[..., :half]
-    send1[...] = send[..., half:]
+    kept, sent = jnp.where(first, a, b), jnp.where(first, b, a)
+    for c in range(2):
+        keep[c] = kept[:, c]
+        send[c] = sent[:, c]
 
 
 def body(
@@ -203,27 +202,30 @@
         pl.BlockSpec((half, tile_p), lambda t, s: (0, jnp.minimum(t, 1))),
         pl.BlockSpec((half, tile_p), lambda t, s: (0, jnp.maximum(t - 2, 0))),
     ]
-    row_spec = pl.BlockSpec((tile_p, n_vir), lambda t, s: (t, 0))
-
-    def gamma(xs, mixes, early=()):
+    row_spec = pl.BlockSpec((tile_p, half), lambda t, s: (t, 0))
+
+    def gamma(xs, mixes):
         n = len(xs)
         return pl.pallas_call(
-            functools.partial(gamma_kernel, n=n, half=half, early=len(early) > 0),
-            out_shape=sds((n_aux, n_vir), F32),
+            functools.partial(gamma_kernel, n=n, half=half),
+            out_shape=(sds((n_aux, half), F32),) * 2,
             grid_spec=pltpu.PrefetchScalarGridSpec(
                 num_scalar_prefetch=1,
                 grid=(tiles,),
-                in_specs=x_specs * n + [whole] * (3 * n) + [row_spec] * len(early),
-                out_specs=row_spec,
+                in_specs=x_specs * n + [whole] * (3 * n),
+                out_specs=[row_spec] * 2,
                 scratch_shapes=[pltpu.VMEM((half, n_vir), BF16)] * n,
             ),
             cost_estimate=cost(2 * n * n_aux * half * n_vir, 2 * n * n_aux * half + 4 * n_aux * n_vir),
             name="gamma",
-        )(sc, *(a for x in xs for a in x), *(m for mix in mixes for m in mix), *early)
+        )(sc, *(a for x in xs for a in x), *(m for mix in mixes for m in mix))
 
     y1 = [jnp.where(core == 0, x0[p], x1[p]) for p in range(2)]
     s1, v1 = amp(y1, 0, F32)
     q1 = exchange(s1)
+    c_halves = virtual_coefficient_matrix.reshape(2, half, -1)
+    c_own = jnp.where(chip == 0, c_halves, c_halves[::-1])
+    x2[0], c_own = lax.optimization_barrier((x2[0], c_own))
     x3 = [ring(x2[p], round3) for p in range(2)]
     s2, v2 = amp(x2, 1, F32)
     q2 = exchange(s2)
@@ -235,44 +237,49 @@
     x4[1], early = lax.optimization_barrier((x4[1], early))
     s4, v4 = amp(x4, 3, BF16)
     q4 = exchange(s4)
-    v3, _ = lax.optimization_barrier((v3, s4))
-    early = gamma([x3], [(s3, q3, v3)], (early,))
 
     groups = tile_p // 32
-    keep0, keep1, send0, send1 = pl.pallas_call(
-        functools.partial(last_kernel, half=half),
-        out_shape=(sds((n_occ, 2, 8, half), F32),) * 4,
-        grid_spec=pltpu.PrefetchScalarGridSpec(
-            num_scalar_prefetch=1,
-            grid=(tiles,),
-            in_specs=x_specs + [whole] * 3 + [row_spec],
-            out_specs=[pl.BlockSpec((groups, 2, 8, half), lambda t, s: (t, 0, 0, 0))] * 4,
-            scratch_shapes=[pltpu.VMEM((half, n_vir), BF16)],
-        ),
-        cost_estimate=cost(2 * n_aux * half * n_vir, 2 * n_aux * (4 * n_vir + half)),
-        name="last",
-    )(sc, *x4, s4, q4, v4, early)
+
+    def last(xs, mixes, early):
+        n, mixed = len(xs), len(mixes) == 2 * len(xs)
+        return pl.pallas_call(
+            functools.partial(last_kernel, n=n, mixed=mixed),
+            out_shape=(sds((2, n_occ, 8, half), F32),) * 2,
+            grid_spec=pltpu.PrefetchScalarGridSpec(
+                num_scalar_prefetch=1,
+                grid=(tiles,),
+                in_specs=x_specs * n + [whole] * len(mixes) + [row_spec],
+                out_specs=[pl.BlockSpec((2, groups, 8, half), lambda t, s: (0, t, 0, 0))] * 2,
+                scratch_shapes=[pltpu.VMEM((half, half), BF16)] * (n if mixed else 0),
+            ),
+            cost_estimate=cost(n * n_aux * half * n_vir, 2 * n_aux * (n_vir + n * half)),
+            name="last",
+        )(sc, *(a for x in xs for a in x), *mixes, early)
 
     def part(keep, got, c):
-        a = lax.dynamic_index_in_dim(keep, c, 1, keepdims=False)
-        return a + lax.dynamic_index_in_dim(got, c, 1, keepdims=False)
+        a = lax.dynamic_index_in_dim(keep, c, 0, keepdims=False)
+        return a + lax.dynamic_index_in_dim(got, c, 0, keepdims=False)
 
     def low(keep, got, far):
         return (part(keep, got, chip) + far.astype(F32)).astype(BF16)
 
-    def finish(g, low):
+    def finish(low, c):
         mine = lax.all_to_all(low, "occ", split_axis=0, concat_axis=0, tiled=True)
-        c = virtual_coefficient_matrix[g * half : (g + 1) * half]
-        return jnp.einsum("sbd,dw->sbw", mine, c, preferred_element_type=F32)
-
+        mine = mine.reshape(2, n_occ // 2 * low.shape[1], half)
+        return jnp.einsum("zsd,zdw->zsw", mine, c, preferred_element_type=F32)
+
+    keep0, send0 = last([x3, x4], [v3, v4], early[0])
+    early1, send0 = lax.optimization_barrier((early[1], send0))
     got0 = lax.ppermute(send0, BOTH, swap(n_occ, 1))
     away0 = part(keep0, got0, 1 - chip).astype(BF16)
     far0 = lax.ppermute(away0, BOTH, swap(n_occ, 2))
+    keep1, send1 = last([x3, x4], [s3, q3, s4, q4], early1)
     got1 = lax.ppermute(send1, BOTH, swap(n_occ, 1))
     away1 = part(keep1, got1, 1 - chip)
     away1, _ = lax.optimization_barrier((away1, far0))
     far1 = lax.ppermute(away1, BOTH, swap(n_occ, 2))
-    return finish(1, low(keep1, got1, far1)) + finish(0, low(keep0, got0, far0))
+    out = finish(low(keep0, got0, far1), c_own) + finish(low(keep1, got1, far0), c_own[::-1])
+    return out.reshape(n_occ, -1, out.shape[-1])
 
 
 def solution(mesh):

time: 198 us -> 193 us (0.975)
  waiting for transfers between devices: 78.1 us -> 69.6 us
  starting transfers between devices: 44.6 us -> 51.9 us
  Pallas kernels: 48.2 us -> 46 us
    ppermute x4, waiting for transfers between devices: 11.7 us -> 7.75 us  [exchange(): return lax.ppermute(s, BOTH, swap(n_occ, 2))]
    ppermute x1, waiting for transfers between devices: 3.11 us -> 0.01 us  [body(): got0 = lax.ppermute(send0, BOTH, swap(n_occ, 1))]
    ppermute x1, starting transfers between devices: 0.09 us -> 3.19 us  [body(): got0 = lax.ppermute(send0, BOTH, swap(n_occ, 1))]
    ppermute x8, waiting for transfers between devices: 29.4 us -> 26.4 us  [ring(): return lax.ppermute(x, BOTH, moves(n_occ, rule))]
    ppermute x8, starting transfers between devices: 16.1 us -> 18.3 us  [ring(): return lax.ppermute(x, BOTH, moves(n_occ, rule))]
    pallas_call x3, Pallas kernels: 26.4 us -> 24.2 us  [the longest x2 15.1 us: last(): pl.pallas_call(functools.partial(last_kernel, n=n, mixed=mixed), out_shap...]
    all_to_all x2, starting transfers between devices: 21.9 us -> 24.1 us  [finish(): mine = lax.all_to_all(low, 'occ', split_axis=0, concat_axis=0, tiled=True)]
    unnamed x38 -> x24, local copies, waits for them, and re-layouts: 4.46 us -> 3.33 us
  transfers between devices with their start and end apart: 18 -> 18, of which waited for: 9 -> 9; matrix products, arithmetic and copies ran while one was open for 8% -> 8% of each run, Pallas kernels for 20% -> 24%
where the time goes in v6:
time: 193 us; the launch traced here: 191 us
  waiting for transfers between devices  69.6 us (36%)
  starting transfers between devices  51.9 us (27%)
  Pallas kernels  46 us (24%)
  other arithmetic  10.4 us (5%)
  local copies, waits for them, and re-layouts  7.1 us (4%)
  matrix products  5.67 us (3%)
    ppermute x8, waiting for transfers between devices, ring(): return lax.ppermute(x, BOTH, moves(n_occ, rule))  26.4 us
    all_to_all x2, starting transfers between devices, finish(): mine = lax.all_to_all(low, 'occ', split_axis=0, concat_axis=0, tiled=True)  24.1 us
    all_to_all x2, waiting for transfers between devices, finish(): mine = lax.all_to_all(low, 'occ', split_axis=0, concat_axis=0, tiled=True)  22.1 us
    pallas_call x4, Pallas kernels, amp(): pl.pallas_call(functools.partial(amp_kernel, half=half, slot=slot), out_s...  21.8 us
    ppermute x8, starting transfers between devices, ring(): return lax.ppermute(x, BOTH, moves(n_occ, rule))  18.3 us
    pallas_call x2, Pallas kernels, last(): pl.pallas_call(functools.partial(last_kernel, n=n, mixed=mixed), out_shap...  15.1 us
    pallas_call x1, Pallas kernels, gamma(): pl.pallas_call(functools.partial(gamma_kernel, n=n, half=half), out_shape...  9.01 us
    ppermute x1, waiting for transfers between devices, body(): far0 = lax.ppermute(away0, BOTH, swap(n_occ, 2))  8.46 us
  transfers between devices with their start and end apart: 18, of which 9 were waited for; matrix products, arithmetic and copies ran while one was open for 8% of the time, Pallas kernels for 24%

profile of v6, /device:TPU:56, one launch (start us, length us, event | category | flops | bytes accessed | tf_op | source)
XLA Modules:
  0.0 190.7 jit_solution(10266523735583764)
XLA Ops:
  0.0 1.6 dynamic-slice_bitcast_fusion.1
  1.6 1.4 collective-permute-start
  3.1 2.7 %collective-permute-start.3 = (bf16[384,1024]{1,0:T(8,128)(2,1)S(1)}, bf16[384,1024]{1,0:T(8,128)(2,1)}, u32[]{:S(2)}, u32[]{:S(2)}) collective-permute-start(bf16[384,1024]{1,0:T(8,128)(2,1)S(1)} %get-tuple-element.52), channel_id=1, source_target_pairs={{0,5},{1,0},{2,7},{3,2},{4,9},{5,36},{6,11},{7,38},{8,13},{9,40},{... | collective-permute-start | bytes 2359304 | tf_op jit(solution)/shard_map/ppermute | solution.py:161
  5.8 7.5 %collective-permute-done = bf16[384,1024]{1,0:T(8,128)(2,1)} collective-permute-done((bf16[384,1024]{1,0:T(8,128)(2,1)S(1)}, bf16[384,1024]{1,0:T(8,128)(2,1)}, u32[]{:S(2)}, u32[]{:S(2)}) %collective-permute-start) | collective-permute-done | bytes 786464 | tf_op jit(solution)/shard_map/ppermute | solution.py:161
  13.2 4.1 %collective-permute-start.1 = (bf16[384,1024]{1,0:T(8,128)(2,1)}, bf16[384,1024]{1,0:T(8,128)(2,1)}, u32[]{:S(2)}, u32[]{:S(2)}) collective-permute-start(bf16[384,1024]{1,0:T(8,128)(2,1)} %collective-permute-done), channel_id=1, source_target_pairs={{0,29},{1,4},{2,31},{3,6},{4,1},{5,8},{6,3},{7,10},{8,5},{9,12},{1... | collective-permute-start | bytes 2359304 | tf_op jit(solution)/shard_map/ppermute | solution.py:161
  17.4 8.8 %collective-permute-done.3 = bf16[384,1024]{1,0:T(8,128)(2,1)} collective-permute-done((bf16[384,1024]{1,0:T(8,128)(2,1)S(1)}, bf16[384,1024]{1,0:T(8,128)(2,1)}, u32[]{:S(2)}, u32[]{:S(2)}) %collective-permute-start.3) | collective-permute-done | bytes 786464 | tf_op jit(solution)/shard_map/ppermute | solution.py:161
  26.2 5.6 %collective-permute-start.4 = (bf16[384,1024]{1,0:T(8,128)(2,1)}, bf16[384,1024]{1,0:T(8,128)(2,1)}, u32[]{:S(2)}, u32[]{:S(2)}) collective-permute-start(bf16[384,1024]{1,0:T(8,128)(2,1)} %collective-permute-done.3), channel_id=1, source_target_pairs={{0,29},{1,4},{2,31},{3,6},{4,1},{5,8},{6,3},{7,10},{8,5},{9,12},{1... | collective-permute-start | bytes 2359304 | tf_op jit(solution)/shard_map/ppermute | solution.py:161
  34.2 1.6 reverse_select_fusion
  35.8 10.1 %collective-permute-done.4.xb.refs_3_ = bf16[384,1024]{1,0:T(8,128)(2,1)} collective-permute-done((bf16[384,1024]{1,0:T(8,128)(2,1)}, bf16[384,1024]{1,0:T(8,128)(2,1)}, u32[]{:S(2)}, u32[]{:S(2)}) %collective-permute-start.4) | collective-permute-done | bytes 786464 | tf_op jit(solution)/shard_map/ppermute | solution.py:161
  48.6 5.4 %amp.5 = (f32[384,384]{1,0:T(8,128)}, bf16[384,384]{1,0:T(8,128)(2,1)}) custom-call(s32[8]{0:T(128)} %stack.35.sc, bf16[768,2048]{1,0:T(8,128)(2,1)} %bitcast.33, bf16[384,1024]{1,0:T(8,128)(2,1)} %broadcast_select_fusion.1.xa.refs_0_, bf16[384,1024]{1,0:T(8,128)(2,1)} %broadcast_select_fusion.xb.refs_1_, f32[384,128]{1,0:T(8,128)} %broadcast_in_dim.41.evc, ...), custom_call_target="tpu_custom_call" | custom-call | flops 1207959552 | bytes 4718592 | tf_op jit(solution)/shard_map/amp/pallas_call | solution.py:177
  54.1 1.5 collective-permute-start.8
  55.6 5.5 %amp.6 = (f32[384,384]{1,0:T(8,128)}, bf16[384,384]{1,0:T(8,128)(2,1)}) custom-call(s32[8]{0:T(128)} %stack.35.sc, bf16[768,2048]{1,0:T(8,128)(2,1)} %bitcast.34, bf16[384,1024]{1,0:T(8,128)(2,1)} %collective-permute-done.1.xa.refs_2_, bf16[384,1024]{1,0:T(8,128)(2,1)} %collective-permute-done.4.xb.refs_3_, f32[384,128]{1,0:T(8,128)} %broadcast_in_dim.41.evc, ...), custom_call_target="tpu_custom_call" | custom-call | flops 1207959552 | bytes 4718592 | tf_op jit(solution)/shard_map/amp/pallas_call | solution.py:177
  61.6 4.3 %collective-permute-start.7 = (bf16[384,1024]{1,0:T(8,128)(2,1)S(1)}, bf16[384,1024]{1,0:T(8,128)(2,1)S(1)}, u32[]{:S(2)}, u32[]{:S(2)}) collective-permute-start(bf16[384,1024]{1,0:T(8,128)(2,1)S(1)} %collective-permute-done.5.xb.refs_1_), channel_id=1, source_target_pairs={{0,255},{1,4},{2,253},{3,6},{4,1},{5,8},{6,3},{7,10},{8,5},{9,12},... | collective-permute-start | bytes 2359304 | tf_op jit(solution)/shard_map/ppermute | solution.py:161
  66.8 5.5 %amp.4 = (f32[384,384]{1,0:T(8,128)}, bf16[384,384]{1,0:T(8,128)(2,1)}) custom-call(s32[8]{0:T(128)} %stack.35.sc, bf16[768,2048]{1,0:T(8,128)(2,1)} %bitcast.35, bf16[384,1024]{1,0:T(8,128)(2,1)} %copy-done, bf16[384,1024]{1,0:T(8,128)(2,1)} %copy-done.1, f32[384,128]{1,0:T(8,128)} %broadcast_in_dim.41.evc, f32[1,768]{1,0:T(1,128)} %broadcast_in_dim.42.evr, ...), custom_call_target="tpu_custom_call" | custom-call | flops 1207959552 | bytes 4718592 | tf_op jit(solution)/shard_map/amp/pallas_call | solution.py:177
  72.3 1.5 collective-permute-start.11
  73.8 7.7 %collective-permute-done.9.refs_8_ = f32[384,384]{1,0:T(8,128)} collective-permute-done((f32[384,384]{1,0:T(8,128)}, f32[384,384]{1,0:T(8,128)}, u32[]{:S(2)}, u32[]{:S(2)}) %collective-permute-start.9) | collective-permute-done | bytes 589856 | tf_op jit(solution)/shard_map/ppermute | solution.py:164
  81.6 9.0 %gamma.1 = (f32[2048,384]{1,0:T(8,128)}, f32[2048,384]{1,0:T(8,128)}) custom-call(s32[8]{0:T(128)} %stack.35.sc, bf16[384,1024]{1,0:T(8,128)(2,1)} %broadcast_select_fusion.1.xa.refs_0_, bf16[384,1024]{1,0:T(8,128)(2,1)} %broadcast_select_fusion.xb.refs_1_, bf16[384,1024]{1,0:T(8,128)(2,1)} %collective-permute-done.1.xa.refs_2_, ...), custom_call_target="tpu_custom_call" | custom-call | flops 2415919104 | bytes 9437184 | tf_op jit(solution)/shard_map/gamma/pallas_call | solution.py:209
  92.4 5.4 %amp.7 = (bf16[384,384]{1,0:T(8,128)(2,1)}, bf16[384,384]{1,0:T(8,128)(2,1)}) custom-call(s32[8]{0:T(128)} %stack.35.sc, bf16[768,2048]{1,0:T(8,128)(2,1)} %bitcast.36, bf16[384,1024]{1,0:T(8,128)(2,1)} %copy-done.3, bf16[384,1024]{1,0:T(8,128)(2,1)} %copy-done.2, f32[384,128]{1,0:T(8,128)} %broadcast_in_dim.41.evc, f32[1,768]{1,0:T(1,128)} %broadcast_in_dim.42.evr, ...), custom_call_target="tpu_custom_call" | custom-call | flops 1207959552 | bytes 4718592 | tf_op jit(solution)/shard_map/amp/pallas_call | solution.py:177
  97.8 1.5 collective-permute-start.12
  99.3 7.2 %last.2 = (f32[2,64,8,384]{3,2,1,0:T(8,128)}, f32[2,64,8,384]{3,2,1,0:T(8,128)}) custom-call(s32[8]{0:T(128)} %stack.35.sc, bf16[384,1024]{1,0:T(8,128)(2,1)} %copy-done, bf16[384,1024]{1,0:T(8,128)(2,1)} %copy-done.1, bf16[384,1024]{1,0:T(8,128)(2,1)} %copy-done.3, bf16[384,1024]{1,0:T(8,128)(2,1)} %copy-done.2, ...), custom_call_target="tpu_custom_call" | custom-call | flops 1207959552 | bytes 6291456 | tf_op jit(solution)/shard_map/last/pallas_call | solution.py:245
  106.5 3.2 %collective-permute-start.10 = (f32[2,64,8,384]{3,2,1,0:T(8,128)}, f32[2,64,8,384]{3,2,1,0:T(8,128)}, u32[]{:S(2)}, u32[]{:S(2)}) collective-permute-start(f32[2,64,8,384]{3,2,1,0:T(8,128)} %get-tuple-element.44), channel_id=1, source_target_pairs={{0,1},{1,0},{2,3},{3,2},{4,5},{5,4},{6,7},{7,6},{8,9},{9,8},{10,11... | collective-permute-start | bytes 4718600 | tf_op jit(solution)/shard_map/ppermute | solution.py:273
  110.4 7.9 %last.3 = (f32[2,64,8,384]{3,2,1,0:T(8,128)}, f32[2,64,8,384]{3,2,1,0:T(8,128)}) custom-call(s32[8]{0:T(128)} %stack.35.sc, bf16[384,1024]{1,0:T(8,128)(2,1)} %copy-done, bf16[384,1024]{1,0:T(8,128)(2,1)} %copy-done.1, bf16[384,1024]{1,0:T(8,128)(2,1)} %copy-done.3, bf16[384,1024]{1,0:T(8,128)(2,1)} %copy-done.2, f32[384,384]{1,0:T(8,128)} %get-tuple-element.29.refs_4_, ...), custom_call_target="tpu_custom_call" | custom-call | flops 1207959552 | bytes 6291456 | tf_op jit(solution)/shard_map/last/pallas_call | solution.py:245
  118.5 1.5 fusion.2
  123.1 8.5 %collective-permute-done.14 = bf16[64,8,384]{2,1,0:T(8,128)(2,1)S(1)} collective-permute-done((bf16[64,8,384]{2,1,0:T(8,128)(2,1)S(1)}, bf16[64,8,384]{2,1,0:T(8,128)(2,1)S(1)}, u32[]{:S(2)}, u32[]{:S(2)}) %collective-permute-start.14) | collective-permute-done | bytes 393248 | tf_op jit(solution)/shard_map/ppermute | solution.py:275
  132.9 15.4 %all-to-all-start.1 = ((bf16[64,8,384]{2,1,0:T(8,128)(2,1)}), bf16[64,8,384]{2,1,0:T(8,128)(2,1)S(1)}, u32[]{:S(2)}, u32[]{:S(2)}) async-start(bf16[64,8,384]{2,1,0:T(8,128)(2,1)} %fusion), calls=%async_computation.1 | async-start | bytes 786432 | tf_op jit(solution)/shard_map/all_to_all | solution.py:267
  148.4 3.5 %collective-permute-done.15 = f32[64,8,384]{2,1,0:T(8,128)} collective-permute-done((f32[64,8,384]{2,1,0:T(8,128)}, f32[64,8,384]{2,1,0:T(8,128)}, u32[]{:S(2)}, u32[]{:S(2)}) %collective-permute-start.15) | collective-permute-done | bytes 786464 | tf_op jit(solution)/shard_map/ppermute | solution.py:280
  151.9 2.5 %fusion.1 = bf16[64,8,384]{2,1,0:T(8,128)(2,1)} fusion(f32[64,8,384]{2,1,0:T(8,128)} %collective-permute-done.15, f32[2,64,8,384]{3,2,1,0:T(8,128)} %collective-permute-done.10, s32[]{:T(128)S(6)} %select_n.108, f32[2,64,8,384]{3,2,1,0:T(8,128)} %get-tuple-element.41), kind=kLoop, calls=%fused_computation.5 | loop fusion | flops 589824 | bytes 2752516 | tf_op jit(solution)/shard_map/convert_element_type | solution.py:264
  154.3 9.6 %all-to-all-done.1 = bf16[64,8,384]{2,1,0:T(8,128)(2,1)S(1)} async-done(((bf16[64,8,384]{2,1,0:T(8,128)(2,1)}), bf16[64,8,384]{2,1,0:T(8,128)(2,1)S(1)}, u32[]{:S(2)}, u32[]{:S(2)}) %all-to-all-start.1) | async-done | bytes 393248 | tf_op jit(solution)/shard_map/all_to_all | solution.py:267
  163.9 8.7 %all-to-all-start = ((bf16[64,8,384]{2,1,0:T(8,128)(2,1)}), bf16[64,8,384]{2,1,0:T(8,128)(2,1)S(1)}, u32[]{:S(2)}, u32[]{:S(2)}) async-start(bf16[64,8,384]{2,1,0:T(8,128)(2,1)} %fusion.1), calls=%async_computation | async-start | bytes 786432 | tf_op jit(solution)/shard_map/all_to_all | solution.py:267
  172.6 2.0 %fusion.3 = f32[2,256,1024]{2,1,0:T(8,128)} fusion(bf16[2,256,384]{2,1,0:T(8,128)(2,1)S(1)} %bitcast.39, bf16[2,384,1024]{2,1,0:T(8,128)(2,1)S(1)} %copy-done.4), kind=kOutput, calls=%fused_computation.17 | convolution fusion | flops 402653184 | bytes 4063232 | tf_op jit(solution)/shard_map/zsd,zdw->zsw/dot_general | solution.py:269
  174.7 12.4 %all-to-all-done = bf16[64,8,384]{2,1,0:T(8,128)(2,1)S(1)} async-done(((bf16[64,8,384]{2,1,0:T(8,128)(2,1)}), bf16[64,8,384]{2,1,0:T(8,128)(2,1)S(1)}, u32[]{:S(2)}, u32[]{:S(2)}) %all-to-all-start) | async-done | bytes 393248 | tf_op jit(solution)/shard_map/all_to_all | solution.py:267
  187.1 3.6 %convolution_add_fusion = f32[2,256,1024]{2,1,0:T(8,128)} fusion(f32[2,256,1024]{2,1,0:T(8,128)} %fusion.3, bf16[2,256,384]{2,1,0:T(8,128)(2,1)S(1)} %bitcast.37, bf16[2,384,1024]{2,1,0:T(8,128)(2,1)S(1)} %copy-done.4), kind=kOutput, calls=%fused_computation.1 | convolution fusion | flops 403177472 | bytes 6160384 | tf_op jit(solution)/shard_map/zsd,zdw->zsw/dot_general | solution.py:269
  (51 shorter events, 13.7 us)
Async XLA Ops:
  0.0 31.8 %copy-start.8 = (s32[768]{0:T(1024)S(1)}, s32[768]{0:T(1024)}, u32[]{:S(2)}) copy-start(s32[768]{0:T(1024)} %param.8) | copy-start | bytes 9220
  0.0 31.8 %copy-start.9 = (f32[256]{0:T(256)S(1)}, f32[256]{0:T(256)}, u32[]{:S(2)}) copy-start(f32[256]{0:T(256)} %param.10) | copy-start | bytes 3076
  0.0 33.4 %copy-start.10 = (f32[256]{0:T(256)S(1)}, f32[256]{0:T(256)}, u32[]{:S(2)}) copy-start(f32[256]{0:T(256)} %param.9) | copy-start | bytes 3076
  0.0 33.4 %copy-start.11 = (s32[64]{0:T(128)S(1)}, s32[64]{0:T(128)}, u32[]{:S(2)}) copy-start(s32[64]{0:T(128)} %param.7) | copy-start | bytes 772
  0.0 34.2 %copy-start.6 = (bf16[768,1024]{1,0:T(8,128)(2,1)S(1)}, bf16[768,1024]{1,0:T(8,128)(2,1)}, u32[]{:S(2)}) copy-start(bf16[768,1024]{1,0:T(8,128)(2,1)} %param.11) | copy-start | bytes 4718596
  1.6 11.6 %collective-permute-start = (bf16[384,1024]{1,0:T(8,128)(2,1)S(1)}, bf16[384,1024]{1,0:T(8,128)(2,1)}, u32[]{:S(2)}, u32[]{:S(2)}) collective-permute-start(bf16[384,1024]{1,0:T(8,128)(2,1)S(1)} %get-tuple-element.51), channel_id=1, source_target_pairs={{0,5},{1,0},{2,7},{3,2},{4,9},{5,36},{6,11},{7,38},{8,13},{9,40},{... | collective-permute-start | bytes 2359304 | tf_op jit(solution)/shard_map/ppermute | solution.py:161
  3.1 23.1 %collective-permute-start.3 = (bf16[384,1024]{1,0:T(8,128)(2,1)S(1)}, bf16[384,1024]{1,0:T(8,128)(2,1)}, u32[]{:S(2)}, u32[]{:S(2)}) collective-permute-start(bf16[384,1024]{1,0:T(8,128)(2,1)S(1)} %get-tuple-element.52), channel_id=1, source_target_pairs={{0,5},{1,0},{2,7},{3,2},{4,9},{5,36},{6,11},{7,38},{8,13},{9,40},{... | collective-permute-start | bytes 2359304 | tf_op jit(solution)/shard_map/ppermute | solution.py:161
  13.2 22.5 %collective-permute-start.1 = (bf16[384,1024]{1,0:T(8,128)(2,1)}, bf16[384,1024]{1,0:T(8,128)(2,1)}, u32[]{:S(2)}, u32[]{:S(2)}) collective-permute-start(bf16[384,1024]{1,0:T(8,128)(2,1)} %collective-permute-done), channel_id=1, source_target_pairs={{0,29},{1,4},{2,31},{3,6},{4,1},{5,8},{6,3},{7,10},{8,5},{9,12},{1... | collective-permute-start | bytes 2359304 | tf_op jit(solution)/shard_map/ppermute | solution.py:161
  26.2 19.7 %collective-permute-start.4 = (bf16[384,1024]{1,0:T(8,128)(2,1)}, bf16[384,1024]{1,0:T(8,128)(2,1)}, u32[]{:S(2)}, u32[]{:S(2)}) collective-permute-start(bf16[384,1024]{1,0:T(8,128)(2,1)} %collective-permute-done.3), channel_id=1, source_target_pairs={{0,29},{1,4},{2,31},{3,6},{4,1},{5,8},{6,3},{7,10},{8,5},{9,12},{1... | collective-permute-start | bytes 2359304 | tf_op jit(solution)/shard_map/ppermute | solution.py:161
  35.8 30.2 %collective-permute-start.2 = (bf16[384,1024]{1,0:T(8,128)(2,1)}, bf16[384,1024]{1,0:T(8,128)(2,1)S(1)}, u32[]{:S(2)}, u32[]{:S(2)}) collective-permute-start(bf16[384,1024]{1,0:T(8,128)(2,1)} %collective-permute-done.1.xa.refs_2_), channel_id=1, source_target_pairs={{0,5},{1,254},{2,7},{3,252},{4,9},{5,0},{6,11},{7,2},{8,13},{9,4},... | collective-permute-start | bytes 2359304 | tf_op jit(solution)/shard_map/ppermute | solution.py:161
  45.9 15.7 %collective-permute-start.5 = (bf16[384,1024]{1,0:T(8,128)(2,1)}, bf16[384,1024]{1,0:T(8,128)(2,1)S(1)}, u32[]{:S(2)}, u32[]{:S(2)}) collective-permute-start(bf16[384,1024]{1,0:T(8,128)(2,1)} %collective-permute-done.4.xb.refs_3_), channel_id=1, source_target_pairs={{0,5},{1,254},{2,7},{3,252},{4,9},{5,0},{6,11},{7,2},{8,13},{9,4},... | collective-permute-start | bytes 2359304 | tf_op jit(solution)/shard_map/ppermute | solution.py:161
  54.1 19.7 %collective-permute-start.8 = (f32[384,384]{1,0:T(8,128)}, f32[384,384]{1,0:T(8,128)}, u32[]{:S(2)}, u32[]{:S(2)}) collective-permute-start(f32[384,384]{1,0:T(8,128)} %get-tuple-element.31.refs_4_), channel_id=1, source_target_pairs={{0,2},{1,3},{2,0},{3,1},{4,6},{5,7},{6,4},{7,5},{8,10},{9,11},{10,... | collective-permute-start | bytes 1769480 | tf_op jit(solution)/shard_map/ppermute | solution.py:164
  61.0 20.5 %collective-permute-start.9 = (f32[384,384]{1,0:T(8,128)}, f32[384,384]{1,0:T(8,128)}, u32[]{:S(2)}, u32[]{:S(2)}) collective-permute-start(f32[384,384]{1,0:T(8,128)} %get-tuple-element.33.refs_7_), channel_id=1, source_target_pairs={{0,2},{1,3},{2,0},{3,1},{4,6},{5,7},{6,4},{7,5},{8,10},{9,11},{10,... | collective-permute-start | bytes 1769480 | tf_op jit(solution)/shard_map/ppermute | solution.py:164
  61.6 4.5 %copy-start.1 = (bf16[384,1024]{1,0:T(8,128)(2,1)}, bf16[384,1024]{1,0:T(8,128)(2,1)S(1)}, u32[]{:S(2)}) copy-start(bf16[384,1024]{1,0:T(8,128)(2,1)S(1)} %collective-permute-done.5.xb.refs_1_) | copy-start | bytes 2359300
  61.6 29.0 %collective-permute-start.7 = (bf16[384,1024]{1,0:T(8,128)(2,1)S(1)}, bf16[384,1024]{1,0:T(8,128)(2,1)S(1)}, u32[]{:S(2)}, u32[]{:S(2)}) collective-permute-start(bf16[384,1024]{1,0:T(8,128)(2,1)S(1)} %collective-permute-done.5.xb.refs_1_), channel_id=1, source_target_pairs={{0,255},{1,4},{2,253},{3,6},{4,1},{5,8},{6,3},{7,10},{8,5},{9,12},... | collective-permute-start | bytes 2359304 | tf_op jit(solution)/shard_map/ppermute | solution.py:161
  65.9 0.9 copy-start
  65.9 24.7 %collective-permute-start.6 = (bf16[384,1024]{1,0:T(8,128)(2,1)S(1)}, bf16[384,1024]{1,0:T(8,128)(2,1)S(1)}, u32[]{:S(2)}, u32[]{:S(2)}) collective-permute-start(bf16[384,1024]{1,0:T(8,128)(2,1)S(1)} %collective-permute-done.2.xa.refs_0_), channel_id=1, source_target_pairs={{0,255},{1,4},{2,253},{3,6},{4,1},{5,8},{6,3},{7,10},{8,5},{9,12},... | collective-permute-start | bytes 2359304 | tf_op jit(solution)/shard_map/ppermute | solution.py:161
  72.3 37.4 %collective-permute-start.11 = (f32[384,384]{1,0:T(8,128)}, f32[384,384]{1,0:T(8,128)}, u32[]{:S(2)}, u32[]{:S(2)}) collective-permute-start(f32[384,384]{1,0:T(8,128)} %get-tuple-element.29.refs_4_), channel_id=1, source_target_pairs={{0,2},{1,3},{2,0},{3,1},{4,6},{5,7},{6,4},{7,5},{8,10},{9,11},{10,... | collective-permute-start | bytes 1769480 | tf_op jit(solution)/shard_map/ppermute | solution.py:164
  90.6 0.9 copy-start.2
  91.5 0.9 copy-start.3
  97.8 11.9 %collective-permute-start.12 = (bf16[384,384]{1,0:T(8,128)(2,1)}, bf16[384,384]{1,0:T(8,128)(2,1)S(1)}, u32[]{:S(2)}, u32[]{:S(2)}) collective-permute-start(bf16[384,384]{1,0:T(8,128)(2,1)} %get-tuple-element.45.refs_6_), channel_id=1, source_target_pairs={{0,2},{1,3},{2,0},{3,1},{4,6},{5,7},{6,4},{7,5},{8,10},{9,11},{10,... | collective-permute-start | bytes 884744 | tf_op jit(solution)/shard_map/ppermute | solution.py:164
  106.5 12.0 %collective-permute-start.10 = (f32[2,64,8,384]{3,2,1,0:T(8,128)}, f32[2,64,8,384]{3,2,1,0:T(8,128)}, u32[]{:S(2)}, u32[]{:S(2)}) collective-permute-start(f32[2,64,8,384]{3,2,1,0:T(8,128)} %get-tuple-element.44), channel_id=1, source_target_pairs={{0,1},{1,0},{2,3},{3,2},{4,5},{5,4},{6,7},{7,6},{8,9},{9,8},{10,11... | collective-permute-start | bytes 4718600 | tf_op jit(solution)/shard_map/ppermute | solution.py:273
  109.7 0.7 copy-start.7
  118.4 3.7 %copy-start.5 = (f32[2,64,8,384]{3,2,1,0:T(8,128)S(1)}, f32[2,64,8,384]{3,2,1,0:T(8,128)}, u32[]{:S(2)}) copy-start(f32[2,64,8,384]{3,2,1,0:T(8,128)} %get-tuple-element.47) | copy-start | bytes 4718596
  118.4 3.7 %collective-permute-start.13 = (f32[2,64,8,384]{3,2,1,0:T(8,128)}, f32[2,64,8,384]{3,2,1,0:T(8,128)S(1)}, u32[]{:S(2)}, u32[]{:S(2)}) collective-permute-start(f32[2,64,8,384]{3,2,1,0:T(8,128)} %get-tuple-element.48), channel_id=1, source_target_pairs={{0,1},{1,0},{2,3},{3,2},{4,5},{5,4},{6,7},{7,6},{8,9},{9,8},{10,11... | collective-permute-start | bytes 4718600 | tf_op jit(solution)/shard_map/ppermute | solution.py:277
  120.0 11.5 %collective-permute-start.14 = (bf16[64,8,384]{2,1,0:T(8,128)(2,1)S(1)}, bf16[64,8,384]{2,1,0:T(8,128)(2,1)S(1)}, u32[]{:S(2)}, u32[]{:S(2)}) collective-permute-start(bf16[64,8,384]{2,1,0:T(8,128)(2,1)S(1)} %fusion.2), channel_id=1, source_target_pairs={{0,2},{1,3},{2,0},{3,1},{4,6},{5,7},{6,4},{7,5},{8,10},{9,11},{10,... | collective-permute-start | bytes 1179656 | tf_op jit(solution)/shard_map/ppermute | solution.py:275
  131.5 20.3 %collective-permute-start.15 = (f32[64,8,384]{2,1,0:T(8,128)}, f32[64,8,384]{2,1,0:T(8,128)}, u32[]{:S(2)}, u32[]{:S(2)}) collective-permute-start(f32[64,8,384]{2,1,0:T(8,128)} %add_bitcast_fusion), channel_id=1, source_target_pairs={{0,2},{1,3},{2,0},{3,1},{4,6},{5,7},{6,4},{7,5},{8,10},{9,11},{10,... | collective-permute-start | bytes 2359304 | tf_op jit(solution)/shard_map/ppermute | solution.py:280
  132.9 31.0 %all-to-all-start.1 = ((bf16[64,8,384]{2,1,0:T(8,128)(2,1)}), bf16[64,8,384]{2,1,0:T(8,128)(2,1)S(1)}, u32[]{:S(2)}, u32[]{:S(2)}) async-start(bf16[64,8,384]{2,1,0:T(8,128)(2,1)} %fusion), calls=%async_computation.1 | async-start | bytes 786432 | tf_op jit(solution)/shard_map/all_to_all | solution.py:267
  148.3 24.3 %copy-start.4 = (bf16[2,384,1024]{2,1,0:T(8,128)(2,1)S(1)}, bf16[2,384,1024]{2,1,0:T(8,128)(2,1)}, u32[]{:S(2)}) copy-start(bf16[2,384,1024]{2,1,0:T(8,128)(2,1)} %reverse_select_fusion) | copy-start | bytes 4718596
  163.9 23.2 %all-to-all-start = ((bf16[64,8,384]{2,1,0:T(8,128)(2,1)}), bf16[64,8,384]{2,1,0:T(8,128)(2,1)S(1)}, u32[]{:S(2)}, u32[]{:S(2)}) async-start(bf16[64,8,384]{2,1,0:T(8,128)(2,1)} %fusion.1), calls=%async_computation | async-start | bytes 786432 | tf_op jit(solution)/shard_map/all_to_all | solution.py:267

commit v7 on v6

--- a/solution.py
+++ b/solution.py
@@ -88,51 +88,43 @@
         w_out[...] = (2.0 * mine - mine.T).astype(BF16)
 
 
-def fill(w, s, q):
-    w[...] = (2.0 * s[...].astype(F32) - q[...].astype(F32).T).astype(BF16)
-
-
-def products(xs, ws):
+def joined(xs):
     first = pl.program_id(0) < pl.num_programs(0) // 2
-    res = None
-    for (xa, xb), w in zip(xs, ws):
-        x = jnp.where(first, xa[...], xb[...])
-        term = lax.dot_general(x, w[...], TN, preferred_element_type=F32)
-        res = term if res is None else res + term
-    return res
+    return jnp.concatenate([jnp.where(first, xa[...], xb[...]) for xa, xb in xs], axis=0)
+
+
+def mix(s, q):
+    return (2.0 * s[...].astype(F32) - q[...].astype(F32).T).astype(BF16)
 
 
 def gamma_kernel(sc, *refs, n, half):
     xs = [refs[2 * k : 2 * k + 2] for k in range(n)]
-    mixes, outs, ws = refs[2 * n : 5 * n], refs[5 * n : 5 * n + 2], refs[5 * n + 2 :]
+    mixes, outs, w = refs[2 * n : 5 * n], refs[5 * n : 5 * n + 2], refs[5 * n + 2]
 
     @pl.when(pl.program_id(0) == 0)
     def _():
         for k in range(n):
             s, q, v = mixes[3 * k : 3 * k + 3]
-            ws[k][:, :half] = v[...]
-            ws[k][:, half:] = (2.0 * s[...].astype(F32) - q[...].astype(F32).T).astype(BF16)
-
-    res = products(xs, ws)
+            w[k * half : (k + 1) * half, :half] = v[...]
+            w[k * half : (k + 1) * half, half:] = mix(s, q)
+
+    res = lax.dot_general(joined(xs), w[...], TN, preferred_element_type=F32)
     outs[0][...] = res[:, :half]
     outs[1][...] = res[:, half:]
 
 
-def last_kernel(sc, *refs, n, mixed):
+def last_kernel(sc, *refs, n, half, mixed):
     xs = [refs[2 * k : 2 * k + 2] for k in range(n)]
     per = 2 if mixed else 1
     mixes, refs = refs[2 * n : (2 + per) * n], refs[(2 + per) * n :]
-    early, keep, send, ws = refs[0], refs[1], refs[2], refs[3:]
-    if mixed:
-
-        @pl.when(pl.program_id(0) == 0)
-        def _():
-            for k in range(n):
-                fill(ws[k], *mixes[2 * k : 2 * k + 2])
-
-    else:
-        ws = mixes
-    res = early[...] + products(xs, ws)
+    early, keep, send, w = refs
+
+    @pl.when(pl.program_id(0) == 0)
+    def _():
+        for k in range(n):
+            w[k * half : (k + 1) * half, :] = mix(*mixes[2 * k : 2 * k + 2]) if mixed else mixes[k][...]
+
+    res = early[...] + lax.dot_general(joined(xs), w[...], TN, preferred_element_type=F32)
     res = res.reshape(res.shape[0] // 32, 2, 2, 8, res.shape[1])
     a, b = res[:, :, 0], res[:, :, 1]
     first = sc[1] == 0
@@ -195,12 +187,12 @@
             name="amp",
         )(sc, own, *x, evc, evr, eo)
 
-    tiles = 4
+    tiles = 2
     tile_p = n_aux // tiles
     whole = pl.BlockSpec((half, half), lambda t, s: (0, 0))
     x_specs = [
-        pl.BlockSpec((half, tile_p), lambda t, s: (0, jnp.minimum(t, 1))),
-        pl.BlockSpec((half, tile_p), lambda t, s: (0, jnp.maximum(t - 2, 0))),
+        pl.BlockSpec((half, tile_p), lambda t, s: (0, jnp.minimum(t, tiles // 2 - 1))),
+        pl.BlockSpec((half, tile_p), lambda t, s: (0, jnp.maximum(t - tiles // 2, 0))),
     ]
     row_spec = pl.BlockSpec((tile_p, half), lambda t, s: (t, 0))
 
@@ -214,7 +206,7 @@
                 grid=(tiles,),
                 in_specs=x_specs * n + [whole] * (3 * n),
                 out_specs=[row_spec] * 2,
-                scratch_shapes=[pltpu.VMEM((half, n_vir), BF16)] * n,
+                scratch_shapes=[pltpu.VMEM((n * half, n_vir), BF16)],
             ),
             cost_estimate=cost(2 * n * n_aux * half * n_vir, 2 * n * n_aux * half + 4 * n_aux * n_vir),
             name="gamma",
@@ -243,14 +235,14 @@
     def last(xs, mixes, early):
         n, mixed = len(xs), len(mixes) == 2 * len(xs)
         return pl.pallas_call(
-            functools.partial(last_kernel, n=n, mixed=mixed),
+            functools.partial(last_kernel, n=n, half=half, mixed=mixed),
             out_shape=(sds((2, n_occ, 8, half), F32),) * 2,
             grid_spec=pltpu.PrefetchScalarGridSpec(
                 num_scalar_prefetch=1,
                 grid=(tiles,),
                 in_specs=x_specs * n + [whole] * len(mixes) + [row_spec],
                 out_specs=[pl.BlockSpec((2, groups, 8, half), lambda t, s: (0, t, 0, 0))] * 2,
-                scratch_shapes=[pltpu.VMEM((half, half), BF16)] * (n if mixed else 0),
+                scratch_shapes=[pltpu.VMEM((n * half, half), BF16)],
             ),
             cost_estimate=cost(n * n_aux * half * n_vir, 2 * n_aux * (n_vir + n * half)),
             name="last",
@@ -275,10 +267,11 @@
     far0 = lax.ppermute(away0, BOTH, swap(n_occ, 2))
     keep1, send1 = last([x3, x4], [s3, q3, s4, q4], early1)
     got1 = lax.ppermute(send1, BOTH, swap(n_occ, 1))
-    away1 = part(keep1, got1, 1 - chip)
-    away1, _ = lax.optimization_barrier((away1, far0))
+    away1 = part(keep1, got1, 1 - chip).astype(BF16)
+    far0, _ = lax.optimization_barrier((far0, away1))
     far1 = lax.ppermute(away1, BOTH, swap(n_occ, 2))
-    out = finish(low(keep0, got0, far1), c_own) + finish(low(keep1, got1, far0), c_own[::-1])
+    low1 = low(keep1, got1, far0)
+    out = finish(low(keep0, got0, far1), c_own) + finish(low1, c_own[::-1])
     return out.reshape(n_occ, -1, out.shape[-1])
 
 

time: 193 us -> 196 us (1.016)
  starting transfers between devices: 51.9 us -> 55.2 us
    ppermute x1, waiting for transfers between devices: 3.5 us -> 13 us  [body(): far1 = lax.ppermute(away1, BOTH, swap(n_occ, 2))]
    all_to_all x2, waiting for transfers between devices: 22.1 us -> 14.2 us  [finish(): mine = lax.all_to_all(low, 'occ', split_axis=0, concat_axis=0, tiled=True)]
    all_to_all x2, starting transfers between devices: 24.1 us -> 27.9 us  [finish(): mine = lax.all_to_all(low, 'occ', split_axis=0, concat_axis=0, tiled=True)]
    convert_element_type x0 -> x1, other arithmetic: none -> 2.2 us  [body(): away1 = part(keep1, got1, 1 - chip).astype(BF16)]
  transfers between devices with their start and end apart: 18 -> 18, of which waited for: 9 -> 9; matrix products, arithmetic and copies ran while one was open for 8% -> 7% of each run, Pallas kernels for 24% -> 23%
where the time goes in v7:
time: 196 us; the launch traced here: 194 us
  waiting for transfers between devices  70.4 us (36%)
  starting transfers between devices  55.2 us (28%)
  Pallas kernels  44.4 us (23%)
  other arithmetic  11.7 us (6%)
  local copies, waits for them, and re-layouts  6.95 us (4%)
  matrix products  5.66 us (3%)
    all_to_all x2, starting transfers between devices, finish(): mine = lax.all_to_all(low, 'occ', split_axis=0, concat_axis=0, tiled=True)  27.9 us
    ppermute x8, waiting for transfers between devices, ring(): return lax.ppermute(x, BOTH, moves(n_occ, rule))  26.5 us
    pallas_call x4, Pallas kernels, amp(): pl.pallas_call(functools.partial(amp_kernel, half=half, slot=slot), out_s...  21.8 us
    ppermute x8, starting transfers between devices, ring(): return lax.ppermute(x, BOTH, moves(n_occ, rule))  18.3 us
    all_to_all x2, waiting for transfers between devices, finish(): mine = lax.all_to_all(low, 'occ', split_axis=0, concat_axis=0, tiled=True)  14.2 us
    pallas_call x2, Pallas kernels, last(): pl.pallas_call(functools.partial(last_kernel, n=n, half=half, mixed=mixed...  13.7 us
    ppermute x1, waiting for transfers between devices, body(): far1 = lax.ppermute(away1, BOTH, swap(n_occ, 2))  13 us
    pallas_call x1, Pallas kernels, gamma(): pl.pallas_call(functools.partial(gamma_kernel, n=n, half=half), out_shape...  8.87 us
  transfers between devices with their start and end apart: 18, of which 9 were waited for; matrix products, arithmetic and copies ran while one was open for 7% of the time, Pallas kernels for 23%

profile of v7, /device:TPU:56, one launch (start us, length us, event | category | flops | bytes accessed | tf_op | source)
XLA Modules:
  0.0 194.4 jit_solution(14402569191378480739)
XLA Ops:
  0.0 1.6 dynamic-slice_bitcast_fusion.1
  3.1 2.7 %collective-permute-start.3 = (bf16[384,1024]{1,0:T(8,128)(2,1)S(1)}, bf16[384,1024]{1,0:T(8,128)(2,1)}, u32[]{:S(2)}, u32[]{:S(2)}) collective-permute-start(bf16[384,1024]{1,0:T(8,128)(2,1)S(1)} %get-tuple-element.52), channel_id=1, source_target_pairs={{0,5},{1,0},{2,7},{3,2},{4,9},{5,36},{6,11},{7,38},{8,13},{9,40},{... | collective-permute-start | bytes 2359304 | tf_op jit(solution)/shard_map/ppermute | solution.py:153
  5.8 7.5 %collective-permute-done = bf16[384,1024]{1,0:T(8,128)(2,1)} collective-permute-done((bf16[384,1024]{1,0:T(8,128)(2,1)S(1)}, bf16[384,1024]{1,0:T(8,128)(2,1)}, u32[]{:S(2)}, u32[]{:S(2)}) %collective-permute-start) | collective-permute-done | bytes 786464 | tf_op jit(solution)/shard_map/ppermute | solution.py:153
  13.2 4.1 %collective-permute-start.1 = (bf16[384,1024]{1,0:T(8,128)(2,1)}, bf16[384,1024]{1,0:T(8,128)(2,1)}, u32[]{:S(2)}, u32[]{:S(2)}) collective-permute-start(bf16[384,1024]{1,0:T(8,128)(2,1)} %collective-permute-done), channel_id=1, source_target_pairs={{0,29},{1,4},{2,31},{3,6},{4,1},{5,8},{6,3},{7,10},{8,5},{9,12},{1... | collective-permute-start | bytes 2359304 | tf_op jit(solution)/shard_map/ppermute | solution.py:153
  17.4 8.8 %collective-permute-done.3 = bf16[384,1024]{1,0:T(8,128)(2,1)} collective-permute-done((bf16[384,1024]{1,0:T(8,128)(2,1)S(1)}, bf16[384,1024]{1,0:T(8,128)(2,1)}, u32[]{:S(2)}, u32[]{:S(2)}) %collective-permute-start.3) | collective-permute-done | bytes 786464 | tf_op jit(solution)/shard_map/ppermute | solution.py:153
  26.2 5.6 %collective-permute-start.4 = (bf16[384,1024]{1,0:T(8,128)(2,1)}, bf16[384,1024]{1,0:T(8,128)(2,1)}, u32[]{:S(2)}, u32[]{:S(2)}) collective-permute-start(bf16[384,1024]{1,0:T(8,128)(2,1)} %collective-permute-done.3), channel_id=1, source_target_pairs={{0,29},{1,4},{2,31},{3,6},{4,1},{5,8},{6,3},{7,10},{8,5},{9,12},{1... | collective-permute-start | bytes 2359304 | tf_op jit(solution)/shard_map/ppermute | solution.py:153
  34.1 1.6 reverse_select_fusion
  35.7 10.3 %collective-permute-done.4.xb.refs_3_ = bf16[384,1024]{1,0:T(8,128)(2,1)} collective-permute-done((bf16[384,1024]{1,0:T(8,128)(2,1)}, bf16[384,1024]{1,0:T(8,128)(2,1)}, u32[]{:S(2)}, u32[]{:S(2)}) %collective-permute-start.4) | collective-permute-done | bytes 786464 | tf_op jit(solution)/shard_map/ppermute | solution.py:153
  48.7 5.5 %amp.5 = (f32[384,384]{1,0:T(8,128)}, bf16[384,384]{1,0:T(8,128)(2,1)}) custom-call(s32[8]{0:T(128)} %stack.35.sc, bf16[768,2048]{1,0:T(8,128)(2,1)} %bitcast.33, bf16[384,1024]{1,0:T(8,128)(2,1)} %broadcast_select_fusion.1.xa.refs_0_, bf16[384,1024]{1,0:T(8,128)(2,1)} %broadcast_select_fusion.xb.refs_1_, f32[384,128]{1,0:T(8,128)} %broadcast_in_dim.41.evc, ...), custom_call_target="tpu_custom_call" | custom-call | flops 1207959552 | bytes 4718592 | tf_op jit(solution)/shard_map/amp/pallas_call | solution.py:169
  54.2 1.5 collective-permute-start.8
  55.7 5.5 %amp.6 = (f32[384,384]{1,0:T(8,128)}, bf16[384,384]{1,0:T(8,128)(2,1)}) custom-call(s32[8]{0:T(128)} %stack.35.sc, bf16[768,2048]{1,0:T(8,128)(2,1)} %bitcast.34, bf16[384,1024]{1,0:T(8,128)(2,1)} %collective-permute-done.1.xa.refs_2_, bf16[384,1024]{1,0:T(8,128)(2,1)} %collective-permute-done.4.xb.refs_3_, f32[384,128]{1,0:T(8,128)} %broadcast_in_dim.41.evc, ...), custom_call_target="tpu_custom_call" | custom-call | flops 1207959552 | bytes 4718592 | tf_op jit(solution)/shard_map/amp/pallas_call | solution.py:169
  61.7 4.3 %collective-permute-start.7 = (bf16[384,1024]{1,0:T(8,128)(2,1)S(1)}, bf16[384,1024]{1,0:T(8,128)(2,1)S(1)}, u32[]{:S(2)}, u32[]{:S(2)}) collective-permute-start(bf16[384,1024]{1,0:T(8,128)(2,1)S(1)} %collective-permute-done.5.xb.refs_1_), channel_id=1, source_target_pairs={{0,255},{1,4},{2,253},{3,6},{4,1},{5,8},{6,3},{7,10},{8,5},{9,12},... | collective-permute-start | bytes 2359304 | tf_op jit(solution)/shard_map/ppermute | solution.py:153
  66.9 5.5 %amp.4 = (f32[384,384]{1,0:T(8,128)}, bf16[384,384]{1,0:T(8,128)(2,1)}) custom-call(s32[8]{0:T(128)} %stack.35.sc, bf16[768,2048]{1,0:T(8,128)(2,1)} %bitcast.35, bf16[384,1024]{1,0:T(8,128)(2,1)} %copy-done, bf16[384,1024]{1,0:T(8,128)(2,1)} %copy-done.1, f32[384,128]{1,0:T(8,128)} %broadcast_in_dim.41.evc, f32[1,768]{1,0:T(1,128)} %broadcast_in_dim.42.evr, ...), custom_call_target="tpu_custom_call" | custom-call | flops 1207959552 | bytes 4718592 | tf_op jit(solution)/shard_map/amp/pallas_call | solution.py:169
  72.4 1.5 collective-permute-start.11
  73.9 7.8 %collective-permute-done.9.refs_8_ = f32[384,384]{1,0:T(8,128)} collective-permute-done((f32[384,384]{1,0:T(8,128)}, f32[384,384]{1,0:T(8,128)}, u32[]{:S(2)}, u32[]{:S(2)}) %collective-permute-start.9) | collective-permute-done | bytes 589856 | tf_op jit(solution)/shard_map/ppermute | solution.py:156
  81.7 8.9 %gamma.1 = (f32[2048,384]{1,0:T(8,128)}, f32[2048,384]{1,0:T(8,128)}) custom-call(s32[8]{0:T(128)} %stack.35.sc, bf16[384,1024]{1,0:T(8,128)(2,1)} %broadcast_select_fusion.1.xa.refs_0_, bf16[384,1024]{1,0:T(8,128)(2,1)} %broadcast_select_fusion.xb.refs_1_, bf16[384,1024]{1,0:T(8,128)(2,1)} %collective-permute-done.1.xa.refs_2_, ...), custom_call_target="tpu_custom_call" | custom-call | flops 2415919104 | bytes 9437184 | tf_op jit(solution)/shard_map/gamma/pallas_call | solution.py:201
  92.3 5.4 %amp.7 = (bf16[384,384]{1,0:T(8,128)(2,1)}, bf16[384,384]{1,0:T(8,128)(2,1)}) custom-call(s32[8]{0:T(128)} %stack.35.sc, bf16[768,2048]{1,0:T(8,128)(2,1)} %bitcast.36, bf16[384,1024]{1,0:T(8,128)(2,1)} %copy-done.3, bf16[384,1024]{1,0:T(8,128)(2,1)} %copy-done.2, f32[384,128]{1,0:T(8,128)} %broadcast_in_dim.41.evc, f32[1,768]{1,0:T(1,128)} %broadcast_in_dim.42.evr, ...), custom_call_target="tpu_custom_call" | custom-call | flops 1207959552 | bytes 4718592 | tf_op jit(solution)/shard_map/amp/pallas_call | solution.py:169
  97.7 1.5 collective-permute-start.12
  99.2 6.5 %last.2 = (f32[2,64,8,384]{3,2,1,0:T(8,128)}, f32[2,64,8,384]{3,2,1,0:T(8,128)}) custom-call(s32[8]{0:T(128)} %stack.35.sc, bf16[384,1024]{1,0:T(8,128)(2,1)} %copy-done, bf16[384,1024]{1,0:T(8,128)(2,1)} %copy-done.1, bf16[384,1024]{1,0:T(8,128)(2,1)} %copy-done.3, bf16[384,1024]{1,0:T(8,128)(2,1)} %copy-done.2, ...), custom_call_target="tpu_custom_call" | custom-call | flops 1207959552 | bytes 6291456 | tf_op jit(solution)/shard_map/last/pallas_call | solution.py:237
  105.7 3.3 %collective-permute-start.10 = (f32[2,64,8,384]{3,2,1,0:T(8,128)}, f32[2,64,8,384]{3,2,1,0:T(8,128)S(1)}, u32[]{:S(2)}, u32[]{:S(2)}) collective-permute-start(f32[2,64,8,384]{3,2,1,0:T(8,128)} %get-tuple-element.44), channel_id=1, source_target_pairs={{0,1},{1,0},{2,3},{3,2},{4,5},{5,4},{6,7},{7,6},{8,9},{9,8},{10,11... | collective-permute-start | bytes 4718600 | tf_op jit(solution)/shard_map/ppermute | solution.py:265
  109.7 7.2 %last.3 = (f32[2,64,8,384]{3,2,1,0:T(8,128)}, f32[2,64,8,384]{3,2,1,0:T(8,128)}) custom-call(s32[8]{0:T(128)} %stack.35.sc, bf16[384,1024]{1,0:T(8,128)(2,1)} %copy-done, bf16[384,1024]{1,0:T(8,128)(2,1)} %copy-done.1, bf16[384,1024]{1,0:T(8,128)(2,1)} %copy-done.3, bf16[384,1024]{1,0:T(8,128)(2,1)} %copy-done.2, f32[384,384]{1,0:T(8,128)} %get-tuple-element.29.refs_4_, ...), custom_call_target="tpu_custom_call" | custom-call | flops 1207959552 | bytes 6291456 | tf_op jit(solution)/shard_map/last/pallas_call | solution.py:237
  118.4 2.2 %collective-permute-done.13 = f32[2,64,8,384]{3,2,1,0:T(8,128)} collective-permute-done((f32[2,64,8,384]{3,2,1,0:T(8,128)}, f32[2,64,8,384]{3,2,1,0:T(8,128)}, u32[]{:S(2)}, u32[]{:S(2)}) %collective-permute-start.13) | collective-permute-done | bytes 1572896 | tf_op jit(solution)/shard_map/ppermute | solution.py:269
  120.6 2.2 %fusion.2 = bf16[64,8,384]{2,1,0:T(8,128)(2,1)} fusion(f32[2,64,8,384]{3,2,1,0:T(8,128)} %collective-permute-done.13, s32[]{:T(128)S(6)} %select_n.109, f32[2,64,8,384]{3,2,1,0:T(8,128)} %get-tuple-element.47), kind=kLoop, calls=%fused_computation.14 | loop fusion | flops 393216 | bytes 1966084 | tf_op jit(solution)/shard_map/convert_element_type | solution.py:270
  122.8 6.7 %collective-permute-done.15 = bf16[64,8,384]{2,1,0:T(8,128)(2,1)S(1)} collective-permute-done((bf16[64,8,384]{2,1,0:T(8,128)(2,1)}, bf16[64,8,384]{2,1,0:T(8,128)(2,1)S(1)}, u32[]{:S(2)}, u32[]{:S(2)}) %collective-permute-start.15) | collective-permute-done | bytes 393248 | tf_op jit(solution)/shard_map/ppermute | solution.py:267
  129.5 2.0 %fusion = bf16[64,8,384]{2,1,0:T(8,128)(2,1)} fusion(bf16[64,8,384]{2,1,0:T(8,128)(2,1)S(1)} %collective-permute-done.15, f32[2,64,8,384]{3,2,1,0:T(8,128)} %collective-permute-done.13, s32[]{:T(128)S(6)} %select_n.108, f32[2,64,8,384]{3,2,1,0:T(8,128)S(1)} %copy-done.7), kind=kLoop, calls=%fused_computation.3 | loop fusion | flops 786432 | bytes 2359300 | tf_op jit(solution)/shard_map/convert_element_type | solution.py:256
  131.5 15.6 %all-to-all-start.1 = ((bf16[64,8,384]{2,1,0:T(8,128)(2,1)}), bf16[64,8,384]{2,1,0:T(8,128)(2,1)S(1)}, u32[]{:S(2)}, u32[]{:S(2)}) async-start(bf16[64,8,384]{2,1,0:T(8,128)(2,1)} %fusion), calls=%async_computation.1 | async-start | bytes 786432 | tf_op jit(solution)/shard_map/all_to_all | solution.py:259
  147.2 13.0 %collective-permute-done.14 = bf16[64,8,384]{2,1,0:T(8,128)(2,1)S(1)} collective-permute-done((bf16[64,8,384]{2,1,0:T(8,128)(2,1)}, bf16[64,8,384]{2,1,0:T(8,128)(2,1)S(1)}, u32[]{:S(2)}, u32[]{:S(2)}) %collective-permute-start.14) | collective-permute-done | bytes 393248 | tf_op jit(solution)/shard_map/ppermute | solution.py:272
  160.2 2.0 %fusion.1 = bf16[64,8,384]{2,1,0:T(8,128)(2,1)} fusion(bf16[64,8,384]{2,1,0:T(8,128)(2,1)S(1)} %collective-permute-done.14, f32[2,64,8,384]{3,2,1,0:T(8,128)} %copy-done.6, s32[]{:T(128)S(6)} %select_n.108, f32[2,64,8,384]{3,2,1,0:T(8,128)S(1)} %copy-done.5), kind=kLoop, calls=%fused_computation.5 | loop fusion | flops 786432 | bytes 2359300 | tf_op jit(solution)/shard_map/convert_element_type | solution.py:256
  162.9 12.3 %all-to-all-start = ((bf16[64,8,384]{2,1,0:T(8,128)(2,1)}), bf16[64,8,384]{2,1,0:T(8,128)(2,1)S(1)}, u32[]{:S(2)}, u32[]{:S(2)}) async-start(bf16[64,8,384]{2,1,0:T(8,128)(2,1)} %fusion.1), calls=%async_computation | async-start | bytes 786432 | tf_op jit(solution)/shard_map/all_to_all | solution.py:259
  175.2 2.0 %fusion.4 = f32[2,256,1024]{2,1,0:T(8,128)} fusion(bf16[2,256,384]{2,1,0:T(8,128)(2,1)S(1)} %bitcast.39, bf16[2,384,1024]{2,1,0:T(8,128)(2,1)S(1)} %copy-done.4), kind=kOutput, calls=%fused_computation.18 | convolution fusion | flops 402653184 | bytes 4063232 | tf_op jit(solution)/shard_map/zsd,zdw->zsw/dot_general | solution.py:261
  177.2 13.5 %all-to-all-done = bf16[64,8,384]{2,1,0:T(8,128)(2,1)S(1)} async-done(((bf16[64,8,384]{2,1,0:T(8,128)(2,1)}), bf16[64,8,384]{2,1,0:T(8,128)(2,1)S(1)}, u32[]{:S(2)}, u32[]{:S(2)}) %all-to-all-start) | async-done | bytes 393248 | tf_op jit(solution)/shard_map/all_to_all | solution.py:259
  190.8 3.6 %convolution_add_fusion = f32[2,256,1024]{2,1,0:T(8,128)} fusion(f32[2,256,1024]{2,1,0:T(8,128)} %fusion.4, bf16[2,256,384]{2,1,0:T(8,128)(2,1)S(1)} %bitcast.37, bf16[2,384,1024]{2,1,0:T(8,128)(2,1)S(1)} %copy-done.4), kind=kOutput, calls=%fused_computation.1 | convolution fusion | flops 403177472 | bytes 6160384 | tf_op jit(solution)/shard_map/zsd,zdw->zsw/dot_general | solution.py:261
  (55 shorter events, 12.7 us)
Async XLA Ops:
  0.0 31.8 %copy-start.10 = (s32[768]{0:T(1024)S(1)}, s32[768]{0:T(1024)}, u32[]{:S(2)}) copy-start(s32[768]{0:T(1024)} %param.8) | copy-start | bytes 9220
  0.0 31.8 %copy-start.11 = (f32[256]{0:T(256)S(1)}, f32[256]{0:T(256)}, u32[]{:S(2)}) copy-start(f32[256]{0:T(256)} %param.10) | copy-start | bytes 3076
  0.0 33.3 %copy-start.12 = (f32[256]{0:T(256)S(1)}, f32[256]{0:T(256)}, u32[]{:S(2)}) copy-start(f32[256]{0:T(256)} %param.9) | copy-start | bytes 3076
  0.0 33.3 %copy-start.13 = (s32[64]{0:T(128)S(1)}, s32[64]{0:T(128)}, u32[]{:S(2)}) copy-start(s32[64]{0:T(128)} %param.7) | copy-start | bytes 772
  0.0 34.1 %copy-start.8 = (bf16[768,1024]{1,0:T(8,128)(2,1)S(1)}, bf16[768,1024]{1,0:T(8,128)(2,1)}, u32[]{:S(2)}) copy-start(bf16[768,1024]{1,0:T(8,128)(2,1)} %param.11) | copy-start | bytes 4718596
  1.6 11.6 %collective-permute-start = (bf16[384,1024]{1,0:T(8,128)(2,1)S(1)}, bf16[384,1024]{1,0:T(8,128)(2,1)}, u32[]{:S(2)}, u32[]{:S(2)}) collective-permute-start(bf16[384,1024]{1,0:T(8,128)(2,1)S(1)} %get-tuple-element.51), channel_id=1, source_target_pairs={{0,5},{1,0},{2,7},{3,2},{4,9},{5,36},{6,11},{7,38},{8,13},{9,40},{... | collective-permute-start | bytes 2359304 | tf_op jit(solution)/shard_map/ppermute | solution.py:153
  3.1 23.1 %collective-permute-start.3 = (bf16[384,1024]{1,0:T(8,128)(2,1)S(1)}, bf16[384,1024]{1,0:T(8,128)(2,1)}, u32[]{:S(2)}, u32[]{:S(2)}) collective-permute-start(bf16[384,1024]{1,0:T(8,128)(2,1)S(1)} %get-tuple-element.52), channel_id=1, source_target_pairs={{0,5},{1,0},{2,7},{3,2},{4,9},{5,36},{6,11},{7,38},{8,13},{9,40},{... | collective-permute-start | bytes 2359304 | tf_op jit(solution)/shard_map/ppermute | solution.py:153
  13.2 22.4 %collective-permute-start.1 = (bf16[384,1024]{1,0:T(8,128)(2,1)}, bf16[384,1024]{1,0:T(8,128)(2,1)}, u32[]{:S(2)}, u32[]{:S(2)}) collective-permute-start(bf16[384,1024]{1,0:T(8,128)(2,1)} %collective-permute-done), channel_id=1, source_target_pairs={{0,29},{1,4},{2,31},{3,6},{4,1},{5,8},{6,3},{7,10},{8,5},{9,12},{1... | collective-permute-start | bytes 2359304 | tf_op jit(solution)/shard_map/ppermute | solution.py:153
  26.2 19.8 %collective-permute-start.4 = (bf16[384,1024]{1,0:T(8,128)(2,1)}, bf16[384,1024]{1,0:T(8,128)(2,1)}, u32[]{:S(2)}, u32[]{:S(2)}) collective-permute-start(bf16[384,1024]{1,0:T(8,128)(2,1)} %collective-permute-done.3), channel_id=1, source_target_pairs={{0,29},{1,4},{2,31},{3,6},{4,1},{5,8},{6,3},{7,10},{8,5},{9,12},{1... | collective-permute-start | bytes 2359304 | tf_op jit(solution)/shard_map/ppermute | solution.py:153
  35.7 30.3 %collective-permute-start.2 = (bf16[384,1024]{1,0:T(8,128)(2,1)}, bf16[384,1024]{1,0:T(8,128)(2,1)S(1)}, u32[]{:S(2)}, u32[]{:S(2)}) collective-permute-start(bf16[384,1024]{1,0:T(8,128)(2,1)} %collective-permute-done.1.xa.refs_2_), channel_id=1, source_target_pairs={{0,5},{1,254},{2,7},{3,252},{4,9},{5,0},{6,11},{7,2},{8,13},{9,4},... | collective-permute-start | bytes 2359304 | tf_op jit(solution)/shard_map/ppermute | solution.py:153
  46.0 15.7 %collective-permute-start.5 = (bf16[384,1024]{1,0:T(8,128)(2,1)}, bf16[384,1024]{1,0:T(8,128)(2,1)S(1)}, u32[]{:S(2)}, u32[]{:S(2)}) collective-permute-start(bf16[384,1024]{1,0:T(8,128)(2,1)} %collective-permute-done.4.xb.refs_3_), channel_id=1, source_target_pairs={{0,5},{1,254},{2,7},{3,252},{4,9},{5,0},{6,11},{7,2},{8,13},{9,4},... | collective-permute-start | bytes 2359304 | tf_op jit(solution)/shard_map/ppermute | solution.py:153
  54.2 19.7 %collective-permute-start.8 = (f32[384,384]{1,0:T(8,128)}, f32[384,384]{1,0:T(8,128)}, u32[]{:S(2)}, u32[]{:S(2)}) collective-permute-start(f32[384,384]{1,0:T(8,128)} %get-tuple-element.31.refs_4_), channel_id=1, source_target_pairs={{0,2},{1,3},{2,0},{3,1},{4,6},{5,7},{6,4},{7,5},{8,10},{9,11},{10,... | collective-permute-start | bytes 1769480 | tf_op jit(solution)/shard_map/ppermute | solution.py:156
  61.1 20.5 %collective-permute-start.9 = (f32[384,384]{1,0:T(8,128)}, f32[384,384]{1,0:T(8,128)}, u32[]{:S(2)}, u32[]{:S(2)}) collective-permute-start(f32[384,384]{1,0:T(8,128)} %get-tuple-element.33.refs_7_), channel_id=1, source_target_pairs={{0,2},{1,3},{2,0},{3,1},{4,6},{5,7},{6,4},{7,5},{8,10},{9,11},{10,... | collective-permute-start | bytes 1769480 | tf_op jit(solution)/shard_map/ppermute | solution.py:156
  61.7 4.5 %copy-start.1 = (bf16[384,1024]{1,0:T(8,128)(2,1)}, bf16[384,1024]{1,0:T(8,128)(2,1)S(1)}, u32[]{:S(2)}) copy-start(bf16[384,1024]{1,0:T(8,128)(2,1)S(1)} %collective-permute-done.5.xb.refs_1_) | copy-start | bytes 2359300
  61.7 28.9 %collective-permute-start.7 = (bf16[384,1024]{1,0:T(8,128)(2,1)S(1)}, bf16[384,1024]{1,0:T(8,128)(2,1)S(1)}, u32[]{:S(2)}, u32[]{:S(2)}) collective-permute-start(bf16[384,1024]{1,0:T(8,128)(2,1)S(1)} %collective-permute-done.5.xb.refs_1_), channel_id=1, source_target_pairs={{0,255},{1,4},{2,253},{3,6},{4,1},{5,8},{6,3},{7,10},{8,5},{9,12},... | collective-permute-start | bytes 2359304 | tf_op jit(solution)/shard_map/ppermute | solution.py:153
  66.0 0.9 copy-start
  66.0 24.5 %collective-permute-start.6 = (bf16[384,1024]{1,0:T(8,128)(2,1)S(1)}, bf16[384,1024]{1,0:T(8,128)(2,1)S(1)}, u32[]{:S(2)}, u32[]{:S(2)}) collective-permute-start(bf16[384,1024]{1,0:T(8,128)(2,1)S(1)} %collective-permute-done.2.xa.refs_0_), channel_id=1, source_target_pairs={{0,255},{1,4},{2,253},{3,6},{4,1},{5,8},{6,3},{7,10},{8,5},{9,12},... | collective-permute-start | bytes 2359304 | tf_op jit(solution)/shard_map/ppermute | solution.py:153
  72.4 36.6 %collective-permute-start.11 = (f32[384,384]{1,0:T(8,128)}, f32[384,384]{1,0:T(8,128)}, u32[]{:S(2)}, u32[]{:S(2)}) collective-permute-start(f32[384,384]{1,0:T(8,128)} %get-tuple-element.29.refs_4_), channel_id=1, source_target_pairs={{0,2},{1,3},{2,0},{3,1},{4,6},{5,7},{6,4},{7,5},{8,10},{9,11},{10,... | collective-permute-start | bytes 1769480 | tf_op jit(solution)/shard_map/ppermute | solution.py:156
  90.5 0.9 copy-start.2
  91.4 0.9 copy-start.3
  97.7 11.3 %collective-permute-start.12 = (bf16[384,384]{1,0:T(8,128)(2,1)}, bf16[384,384]{1,0:T(8,128)(2,1)S(1)}, u32[]{:S(2)}, u32[]{:S(2)}) collective-permute-start(bf16[384,384]{1,0:T(8,128)(2,1)} %get-tuple-element.45.refs_6_), channel_id=1, source_target_pairs={{0,2},{1,3},{2,0},{3,1},{4,6},{5,7},{6,4},{7,5},{8,10},{9,11},{10,... | collective-permute-start | bytes 884744 | tf_op jit(solution)/shard_map/ppermute | solution.py:156
  105.7 11.2 %copy-start.5 = (f32[2,64,8,384]{3,2,1,0:T(8,128)S(1)}, f32[2,64,8,384]{3,2,1,0:T(8,128)}, u32[]{:S(2)}) copy-start(f32[2,64,8,384]{3,2,1,0:T(8,128)} %get-tuple-element.41) | copy-start | bytes 4718596
  105.7 11.2 %collective-permute-start.10 = (f32[2,64,8,384]{3,2,1,0:T(8,128)}, f32[2,64,8,384]{3,2,1,0:T(8,128)S(1)}, u32[]{:S(2)}, u32[]{:S(2)}) collective-permute-start(f32[2,64,8,384]{3,2,1,0:T(8,128)} %get-tuple-element.44), channel_id=1, source_target_pairs={{0,1},{1,0},{2,3},{3,2},{4,5},{5,4},{6,7},{7,6},{8,9},{9,8},{10,11... | collective-permute-start | bytes 4718600 | tf_op jit(solution)/shard_map/ppermute | solution.py:265
  109.0 0.7 copy-start.9
  116.9 3.8 %collective-permute-start.13 = (f32[2,64,8,384]{3,2,1,0:T(8,128)}, f32[2,64,8,384]{3,2,1,0:T(8,128)}, u32[]{:S(2)}, u32[]{:S(2)}) collective-permute-start(f32[2,64,8,384]{3,2,1,0:T(8,128)} %get-tuple-element.48), channel_id=1, source_target_pairs={{0,1},{1,0},{2,3},{3,2},{4,5},{5,4},{6,7},{7,6},{8,9},{9,8},{10,11... | collective-permute-start | bytes 4718600 | tf_op jit(solution)/shard_map/ppermute | solution.py:269
  116.9 5.9 %copy-start.6 = (f32[2,64,8,384]{3,2,1,0:T(8,128)}, f32[2,64,8,384]{3,2,1,0:T(8,128)S(1)}, u32[]{:S(2)}) copy-start(f32[2,64,8,384]{3,2,1,0:T(8,128)S(1)} %collective-permute-done.10) | copy-start | bytes 4718596
  117.8 11.7 %collective-permute-start.15 = (bf16[64,8,384]{2,1,0:T(8,128)(2,1)}, bf16[64,8,384]{2,1,0:T(8,128)(2,1)S(1)}, u32[]{:S(2)}, u32[]{:S(2)}) collective-permute-start(bf16[64,8,384]{2,1,0:T(8,128)(2,1)} %fusion.3), channel_id=1, source_target_pairs={{0,2},{1,3},{2,0},{3,1},{4,6},{5,7},{6,4},{7,5},{8,10},{9,11},{10,... | collective-permute-start | bytes 1179656 | tf_op jit(solution)/shard_map/ppermute | solution.py:267
  118.4 11.1 %copy-start.7 = (f32[2,64,8,384]{3,2,1,0:T(8,128)S(1)}, f32[2,64,8,384]{3,2,1,0:T(8,128)}, u32[]{:S(2)}) copy-start(f32[2,64,8,384]{3,2,1,0:T(8,128)} %get-tuple-element.47) | copy-start | bytes 4718596
  131.5 31.4 %all-to-all-start.1 = ((bf16[64,8,384]{2,1,0:T(8,128)(2,1)}), bf16[64,8,384]{2,1,0:T(8,128)(2,1)S(1)}, u32[]{:S(2)}, u32[]{:S(2)}) async-start(bf16[64,8,384]{2,1,0:T(8,128)(2,1)} %fusion), calls=%async_computation.1 | async-start | bytes 786432 | tf_op jit(solution)/shard_map/all_to_all | solution.py:259
  147.1 28.1 %copy-start.4 = (bf16[2,384,1024]{2,1,0:T(8,128)(2,1)S(1)}, bf16[2,384,1024]{2,1,0:T(8,128)(2,1)}, u32[]{:S(2)}) copy-start(bf16[2,384,1024]{2,1,0:T(8,128)(2,1)} %reverse_select_fusion) | copy-start | bytes 4718596
  147.1 13.1 %collective-permute-start.14 = (bf16[64,8,384]{2,1,0:T(8,128)(2,1)}, bf16[64,8,384]{2,1,0:T(8,128)(2,1)S(1)}, u32[]{:S(2)}, u32[]{:S(2)}) collective-permute-start(bf16[64,8,384]{2,1,0:T(8,128)(2,1)} %fusion.2), channel_id=1, source_target_pairs={{0,2},{1,3},{2,0},{3,1},{4,6},{5,7},{6,4},{7,5},{8,10},{9,11},{10,... | collective-permute-start | bytes 1179656 | tf_op jit(solution)/shard_map/ppermute | solution.py:272
  162.9 27.9 %all-to-all-start = ((bf16[64,8,384]{2,1,0:T(8,128)(2,1)}), bf16[64,8,384]{2,1,0:T(8,128)(2,1)S(1)}, u32[]{:S(2)}, u32[]{:S(2)}) async-start(bf16[64,8,384]{2,1,0:T(8,128)(2,1)} %fusion.1), calls=%async_computation | async-start | bytes 786432 | tf_op jit(solution)/shard_map/all_to_all | solution.py:259

commit v8 on v7

--- a/solution.py
+++ b/solution.py
@@ -216,7 +216,9 @@
     s1, v1 = amp(y1, 0, F32)
     q1 = exchange(s1)
     c_halves = virtual_coefficient_matrix.reshape(2, half, -1)
-    c_own = jnp.where(chip == 0, c_halves, c_halves[::-1])
+    c_flip = c_halves[::-1]
+    c_both = [jnp.concatenate([c[0], c[1]], axis=0) for c in (c_halves, c_flip)]
+    c_own = jnp.where(chip == 0, jnp.stack(c_both), jnp.stack(c_both[::-1]))
     x2[0], c_own = lax.optimization_barrier((x2[0], c_own))
     x3 = [ring(x2[p], round3) for p in range(2)]
     s2, v2 = amp(x2, 1, F32)
@@ -255,11 +257,6 @@
     def low(keep, got, far):
         return (part(keep, got, chip) + far.astype(F32)).astype(BF16)
 
-    def finish(low, c):
-        mine = lax.all_to_all(low, "occ", split_axis=0, concat_axis=0, tiled=True)
-        mine = mine.reshape(2, n_occ // 2 * low.shape[1], half)
-        return jnp.einsum("zsd,zdw->zsw", mine, c, preferred_element_type=F32)
-
     keep0, send0 = last([x3, x4], [v3, v4], early[0])
     early1, send0 = lax.optimization_barrier((early[1], send0))
     got0 = lax.ppermute(send0, BOTH, swap(n_occ, 1))
@@ -268,10 +265,11 @@
     keep1, send1 = last([x3, x4], [s3, q3, s4, q4], early1)
     got1 = lax.ppermute(send1, BOTH, swap(n_occ, 1))
     away1 = part(keep1, got1, 1 - chip).astype(BF16)
-    far0, _ = lax.optimization_barrier((far0, away1))
     far1 = lax.ppermute(away1, BOTH, swap(n_occ, 2))
-    low1 = low(keep1, got1, far0)
-    out = finish(low(keep0, got0, far1), c_own) + finish(low1, c_own[::-1])
+    gamma_low = jnp.concatenate([low(keep0, got0, far1), low(keep1, got1, far0)], axis=2)
+    mine = lax.all_to_all(gamma_low, "occ", split_axis=0, concat_axis=0, tiled=True)
+    mine = mine.reshape(2, n_occ // 2 * mine.shape[1], n_vir)
+    out = jnp.einsum("zsd,zdw->zsw", mine, c_own, preferred_element_type=F32)
     return out.reshape(n_occ, -1, out.shape[-1])
 
 

time: 196 us -> 178 us (0.908)
  blocking collectives: 0 us -> 37.4 us
  starting transfers between devices: 55.2 us -> 28.7 us
  waiting for transfers between devices: 70.4 us -> 46.2 us
  matrix products: 5.66 us -> 2.32 us
    all_to_all x0 -> x1, blocking collectives: none -> 37.4 us  [body(): lax.all_to_all(gamma_low, 'occ', split_axis=0, concat_axis=0, tiled=True)]
    all_to_all x2 -> x0, starting transfers between devices: 27.9 us -> none  [finish(): mine = lax.all_to_all(low, 'occ', split_axis=0, concat_axis=0, tiled=True)]
    all_to_all x2 -> x0, waiting for transfers between devices: 14.2 us -> none  [finish(): mine = lax.all_to_all(low, 'occ', split_axis=0, concat_axis=0, tiled=True)]
    ppermute x1, waiting for transfers between devices: 13 us -> 6.57 us  [body(): far1 = lax.ppermute(away1, BOTH, swap(n_occ, 2))]
    dot_general x2 -> x1, matrix products: 5.66 us -> 2.32 us  [body(): out = jnp.einsum('zsd,zdw->zsw', mine, c_own, preferred_element_type=F32)]
    ppermute x1, waiting for transfers between devices: 2.25 us -> 0.19 us  [body(): got1 = lax.ppermute(send1, BOTH, swap(n_occ, 1))]
    ppermute x8, waiting for transfers between devices: 26.5 us -> 24.5 us  [ring(): return lax.ppermute(x, BOTH, moves(n_occ, rule))]
  transfers between devices with their start and end apart: 18 -> 16, of which waited for: 9 -> 8; matrix products, arithmetic and copies ran while one was open for 7% -> 7% of each run, Pallas kernels for 23% -> 25%
where the time goes in v8:
time: 178 us; the launch traced here: 177 us
  waiting for transfers between devices  46.2 us (26%)
  Pallas kernels  44.3 us (25%)
  blocking collectives  37.4 us (21%)
  starting transfers between devices  28.7 us (16%)
  other arithmetic  10.8 us (6%)
  local copies, waits for them, and re-layouts  6.78 us (4%)
  matrix products  2.32 us (1%)
    all_to_all x1, blocking collectives, body(): lax.all_to_all(gamma_low, 'occ', split_axis=0, concat_axis=0, tiled=True)  37.4 us
    ppermute x8, waiting for transfers between devices, ring(): return lax.ppermute(x, BOTH, moves(n_occ, rule))  24.5 us
    pallas_call x4, Pallas kernels, amp(): pl.pallas_call(functools.partial(amp_kernel, half=half, slot=slot), out_s...  21.7 us
    ppermute x8, starting transfers between devices, ring(): return lax.ppermute(x, BOTH, moves(n_occ, rule))  19.4 us
    pallas_call x2, Pallas kernels, last(): pl.pallas_call(functools.partial(last_kernel, n=n, half=half, mixed=mixed...  13.7 us
    pallas_call x1, Pallas kernels, gamma(): pl.pallas_call(functools.partial(gamma_kernel, n=n, half=half), out_shape...  8.85 us
    ppermute x1, waiting for transfers between devices, body(): far0 = lax.ppermute(away0, BOTH, swap(n_occ, 2))  7.96 us
    ppermute x4, waiting for transfers between devices, exchange(): return lax.ppermute(s, BOTH, swap(n_occ, 2))  7.01 us
  transfers between devices with their start and end apart: 16, of which 8 were waited for; matrix products, arithmetic and copies ran while one was open for 7% of the time, Pallas kernels for 25%

profile of v8, /device:TPU:56, one launch (start us, length us, event | category | flops | bytes accessed | tf_op | source)
XLA Modules:
  0.0 176.7 jit_solution(17709693506739725453)
XLA Ops:
  0.0 1.6 dynamic-slice_bitcast_fusion.1
  2.6 1.4 collective-permute-start.3
  3.9 2.7 %collective-permute-start = (bf16[384,1024]{1,0:T(8,128)(2,1)S(1)}, bf16[384,1024]{1,0:T(8,128)(2,1)}, u32[]{:S(2)}, u32[]{:S(2)}) collective-permute-start(bf16[384,1024]{1,0:T(8,128)(2,1)S(1)} %get-tuple-element.49), channel_id=1, source_target_pairs={{0,5},{1,0},{2,7},{3,2},{4,9},{5,36},{6,11},{7,38},{8,13},{9,40},{... | collective-permute-start | bytes 2359304 | tf_op jit(solution)/shard_map/ppermute | solution.py:153
  6.9 7.2 %collective-permute-done.3 = bf16[384,1024]{1,0:T(8,128)(2,1)} collective-permute-done((bf16[384,1024]{1,0:T(8,128)(2,1)S(1)}, bf16[384,1024]{1,0:T(8,128)(2,1)}, u32[]{:S(2)}, u32[]{:S(2)}) %collective-permute-start.3) | collective-permute-done | bytes 786464 | tf_op jit(solution)/shard_map/ppermute | solution.py:153
  14.1 4.1 %collective-permute-start.4 = (bf16[384,1024]{1,0:T(8,128)(2,1)}, bf16[384,1024]{1,0:T(8,128)(2,1)}, u32[]{:S(2)}, u32[]{:S(2)}) collective-permute-start(bf16[384,1024]{1,0:T(8,128)(2,1)} %collective-permute-done.3), channel_id=1, source_target_pairs={{0,29},{1,4},{2,31},{3,6},{4,1},{5,8},{6,3},{7,10},{8,5},{9,12},{1... | collective-permute-start | bytes 2359304 | tf_op jit(solution)/shard_map/ppermute | solution.py:153
  18.2 8.8 %collective-permute-done = bf16[384,1024]{1,0:T(8,128)(2,1)} collective-permute-done((bf16[384,1024]{1,0:T(8,128)(2,1)S(1)}, bf16[384,1024]{1,0:T(8,128)(2,1)}, u32[]{:S(2)}, u32[]{:S(2)}) %collective-permute-start) | collective-permute-done | bytes 786464 | tf_op jit(solution)/shard_map/ppermute | solution.py:153
  27.0 5.6 %collective-permute-start.1 = (bf16[384,1024]{1,0:T(8,128)(2,1)}, bf16[384,1024]{1,0:T(8,128)(2,1)}, u32[]{:S(2)}, u32[]{:S(2)}) collective-permute-start(bf16[384,1024]{1,0:T(8,128)(2,1)} %collective-permute-done), channel_id=1, source_target_pairs={{0,29},{1,4},{2,31},{3,6},{4,1},{5,8},{6,3},{7,10},{8,5},{9,12},{1... | collective-permute-start | bytes 2359304 | tf_op jit(solution)/shard_map/ppermute | solution.py:153
  35.0 1.3 copy-done.1
  36.8 5.8 %collective-permute-done.1.xa.refs_2_ = bf16[384,1024]{1,0:T(8,128)(2,1)} collective-permute-done((bf16[384,1024]{1,0:T(8,128)(2,1)}, bf16[384,1024]{1,0:T(8,128)(2,1)}, u32[]{:S(2)}, u32[]{:S(2)}) %collective-permute-start.1) | collective-permute-done | bytes 786464 | tf_op jit(solution)/shard_map/ppermute | solution.py:153
  42.6 1.7 collective-permute-start.5
  47.1 5.5 %amp.5 = (f32[384,384]{1,0:T(8,128)}, bf16[384,384]{1,0:T(8,128)(2,1)}) custom-call(s32[8]{0:T(128)} %stack.49.sc, bf16[768,2048]{1,0:T(8,128)(2,1)} %bitcast.32, bf16[384,1024]{1,0:T(8,128)(2,1)} %broadcast_select_fusion.1.xa.refs_0_, bf16[384,1024]{1,0:T(8,128)(2,1)} %broadcast_select_fusion.xb.refs_1_, f32[384,128]{1,0:T(8,128)} %broadcast_in_dim.41.evc, ...), custom_call_target="tpu_custom_call" | custom-call | flops 1207959552 | bytes 4718592 | tf_op jit(solution)/shard_map/amp/pallas_call | solution.py:169
  52.6 1.5 collective-permute-start.8
  54.1 5.4 %amp.6 = (f32[384,384]{1,0:T(8,128)}, bf16[384,384]{1,0:T(8,128)(2,1)}) custom-call(s32[8]{0:T(128)} %stack.49.sc, bf16[768,2048]{1,0:T(8,128)(2,1)} %bitcast.33, bf16[384,1024]{1,0:T(8,128)(2,1)} %collective-permute-done.1.xa.refs_2_, bf16[384,1024]{1,0:T(8,128)(2,1)} %collective-permute-done.4.xb.refs_3_, f32[384,128]{1,0:T(8,128)} %broadcast_in_dim.41.evc, ...), custom_call_target="tpu_custom_call" | custom-call | flops 1207959552 | bytes 4718592 | tf_op jit(solution)/shard_map/amp/pallas_call | solution.py:169
  60.0 2.7 %collective-permute-done.5.xb.refs_1_ = bf16[384,1024]{1,0:T(8,128)(2,1)} collective-permute-done((bf16[384,1024]{1,0:T(8,128)(2,1)}, bf16[384,1024]{1,0:T(8,128)(2,1)}, u32[]{:S(2)}, u32[]{:S(2)}) %collective-permute-start.5) | collective-permute-done | bytes 786464 | tf_op jit(solution)/shard_map/ppermute | solution.py:153
  62.7 3.9 %collective-permute-start.7 = (bf16[384,1024]{1,0:T(8,128)(2,1)}, bf16[384,1024]{1,0:T(8,128)(2,1)}, u32[]{:S(2)}, u32[]{:S(2)}) collective-permute-start(bf16[384,1024]{1,0:T(8,128)(2,1)} %collective-permute-done.5.xb.refs_1_), channel_id=1, source_target_pairs={{0,255},{1,4},{2,253},{3,6},{4,1},{5,8},{6,3},{7,10},{8,5},{9,12},... | collective-permute-start | bytes 2359304 | tf_op jit(solution)/shard_map/ppermute | solution.py:153
  66.6 5.5 %amp.4 = (f32[384,384]{1,0:T(8,128)}, bf16[384,384]{1,0:T(8,128)(2,1)}) custom-call(s32[8]{0:T(128)} %stack.49.sc, bf16[768,2048]{1,0:T(8,128)(2,1)} %bitcast.34, bf16[384,1024]{1,0:T(8,128)(2,1)} %collective-permute-done.2.xa.refs_0_, bf16[384,1024]{1,0:T(8,128)(2,1)} %collective-permute-done.5.xb.refs_1_, f32[384,128]{1,0:T(8,128)} %broadcast_in_dim.41.evc, ...), custom_call_target="tpu_custom_call" | custom-call | flops 1207959552 | bytes 4718592 | tf_op jit(solution)/shard_map/amp/pallas_call | solution.py:169
  72.1 1.5 collective-permute-start.11
  73.6 7.0 %collective-permute-done.9.refs_8_ = f32[384,384]{1,0:T(8,128)} collective-permute-done((f32[384,384]{1,0:T(8,128)}, f32[384,384]{1,0:T(8,128)}, u32[]{:S(2)}, u32[]{:S(2)}) %collective-permute-start.9) | collective-permute-done | bytes 589856 | tf_op jit(solution)/shard_map/ppermute | solution.py:156
  80.6 8.9 %gamma.1 = (f32[2048,384]{1,0:T(8,128)}, f32[2048,384]{1,0:T(8,128)}) custom-call(s32[8]{0:T(128)} %stack.49.sc, bf16[384,1024]{1,0:T(8,128)(2,1)} %broadcast_select_fusion.1.xa.refs_0_, bf16[384,1024]{1,0:T(8,128)(2,1)} %broadcast_select_fusion.xb.refs_1_, bf16[384,1024]{1,0:T(8,128)(2,1)} %collective-permute-done.1.xa.refs_2_, ...), custom_call_target="tpu_custom_call" | custom-call | flops 2415919104 | bytes 9437184 | tf_op jit(solution)/shard_map/gamma/pallas_call | solution.py:201
  89.5 5.4 %amp.7 = (bf16[384,384]{1,0:T(8,128)(2,1)}, bf16[384,384]{1,0:T(8,128)(2,1)}) custom-call(s32[8]{0:T(128)} %stack.49.sc, bf16[768,2048]{1,0:T(8,128)(2,1)} %bitcast.35, bf16[384,1024]{1,0:T(8,128)(2,1)} %collective-permute-done.6.xa.refs_2_, bf16[384,1024]{1,0:T(8,128)(2,1)} %collective-permute-done.7.xb.refs_3_, f32[384,128]{1,0:T(8,128)} %broadcast_in_dim.41.evc, ...), custom_call_target="tpu_custom_call" | custom-call | flops 1207959552 | bytes 4718592 | tf_op jit(solution)/shard_map/amp/pallas_call | solution.py:169
  94.8 1.5 collective-permute-start.12
  96.3 6.5 %last.2 = (f32[2,64,8,384]{3,2,1,0:T(8,128)}, f32[2,64,8,384]{3,2,1,0:T(8,128)}) custom-call(s32[8]{0:T(128)} %stack.49.sc, bf16[384,1024]{1,0:T(8,128)(2,1)} %collective-permute-done.2.xa.refs_0_, bf16[384,1024]{1,0:T(8,128)(2,1)} %collective-permute-done.5.xb.refs_1_, bf16[384,1024]{1,0:T(8,128)(2,1)} %collective-permute-done.6.xa.refs_2_, ...), custom_call_target="tpu_custom_call" | custom-call | flops 1207959552 | bytes 6291456 | tf_op jit(solution)/shard_map/last/pallas_call | solution.py:239
  102.9 2.1 %collective-permute-start.10 = (f32[2,64,8,384]{3,2,1,0:T(8,128)}, f32[2,64,8,384]{3,2,1,0:T(8,128)}, u32[]{:S(2)}, u32[]{:S(2)}) collective-permute-start(f32[2,64,8,384]{3,2,1,0:T(8,128)} %get-tuple-element.43), channel_id=1, source_target_pairs={{0,1},{1,0},{2,3},{3,2},{4,5},{5,4},{6,7},{7,6},{8,9},{9,8},{10,11... | collective-permute-start | bytes 4718600 | tf_op jit(solution)/shard_map/ppermute | solution.py:262
  105.7 7.2 %last.3 = (f32[2,64,8,384]{3,2,1,0:T(8,128)}, f32[2,64,8,384]{3,2,1,0:T(8,128)}) custom-call(s32[8]{0:T(128)} %stack.49.sc, bf16[384,1024]{1,0:T(8,128)(2,1)} %collective-permute-done.2.xa.refs_0_, bf16[384,1024]{1,0:T(8,128)(2,1)} %collective-permute-done.5.xb.refs_1_, bf16[384,1024]{1,0:T(8,128)(2,1)} %collective-permute-done.6.xa.refs_2_, ...), custom_call_target="tpu_custom_call" | custom-call | flops 1207959552 | bytes 6291456 | tf_op jit(solution)/shard_map/last/pallas_call | solution.py:239
  112.9 2.3 %fusion.3 = bf16[64,8,384]{2,1,0:T(8,128)(2,1)} fusion(f32[2,64,8,384]{3,2,1,0:T(8,128)} %collective-permute-done.10, s32[]{:T(128)S(6)} %select_n.109, f32[2,64,8,384]{3,2,1,0:T(8,128)} %get-tuple-element.40), kind=kLoop, calls=%fused_computation.16 | loop fusion | flops 393216 | bytes 1966084 | tf_op jit(solution)/shard_map/convert_element_type | solution.py:263
  116.6 2.0 %fusion.2 = bf16[64,8,384]{2,1,0:T(8,128)(2,1)} fusion(f32[2,64,8,384]{3,2,1,0:T(8,128)} %collective-permute-done.13, s32[]{:T(128)S(6)} %select_n.109, f32[2,64,8,384]{3,2,1,0:T(8,128)S(1)} %copy-done.7), kind=kLoop, calls=%fused_computation.15 | loop fusion | flops 393216 | bytes 1966084 | tf_op jit(solution)/shard_map/convert_element_type | solution.py:267
  119.5 8.0 %collective-permute-done.15 = bf16[64,8,384]{2,1,0:T(8,128)(2,1)S(1)} collective-permute-done((bf16[64,8,384]{2,1,0:T(8,128)(2,1)}, bf16[64,8,384]{2,1,0:T(8,128)(2,1)S(1)}, u32[]{:S(2)}, u32[]{:S(2)}) %collective-permute-start.15) | collective-permute-done | bytes 393248 | tf_op jit(solution)/shard_map/ppermute | solution.py:264
  127.4 1.5 fusion
  128.9 6.6 %collective-permute-done.14 = bf16[64,8,384]{2,1,0:T(8,128)(2,1)} collective-permute-done((bf16[64,8,384]{2,1,0:T(8,128)(2,1)}, bf16[64,8,384]{2,1,0:T(8,128)(2,1)}, u32[]{:S(2)}, u32[]{:S(2)}) %collective-permute-start.14) | collective-permute-done | bytes 393248 | tf_op jit(solution)/shard_map/ppermute | solution.py:268
  135.5 1.4 fusion.1
  136.9 37.4 %all_to_all.5 = bf16[64,8,768]{2,1,0:T(8,128)(2,1)S(1)} all-to-all(bf16[64,8,768]{2,1,0:T(8,128)(2,1)S(1)} %pad_maximum_fusion), channel_id=1, replica_groups=mesh['occ'=64,'off'=4] {'occ'}, dimensions={0} | all-to-all | bytes 1572864 | tf_op jit(solution)/shard_map/all_to_all | solution.py:270
  174.3 2.3 %fusion.5 = f32[2,256,1024]{2,1,0:T(8,128)} fusion(bf16[2,256,768]{2,1,0:T(8,128)(2,1)S(1)} %bitcast.37, bf16[2,768,1024]{2,1,0:T(8,128)(2,1)S(1)} %maximum_select_fusion), kind=kOutput, calls=%fused_computation.20 | convolution fusion | flops 805306368 | bytes 6029312 | tf_op jit(solution)/shard_map/zsd,zdw->zsw/dot_general | solution.py:272
  (52 shorter events, 10.5 us)
Async XLA Ops:
  0.0 6.6 %copy-start.9 = (s32[768]{0:T(1024)S(1)}, s32[768]{0:T(1024)}, u32[]{:S(2)}) copy-start(s32[768]{0:T(1024)} %param.8) | copy-start | bytes 9220
  0.0 6.6 %copy-start.10 = (f32[256]{0:T(256)S(1)}, f32[256]{0:T(256)}, u32[]{:S(2)}) copy-start(f32[256]{0:T(256)} %param.10) | copy-start | bytes 3076
  0.0 32.6 %copy-start.11 = (f32[256]{0:T(256)S(1)}, f32[256]{0:T(256)}, u32[]{:S(2)}) copy-start(f32[256]{0:T(256)} %param.9) | copy-start | bytes 3076
  0.0 32.6 %copy-start.12 = (s32[64]{0:T(128)S(1)}, s32[64]{0:T(128)}, u32[]{:S(2)}) copy-start(s32[64]{0:T(128)} %param.7) | copy-start | bytes 772
  0.0 34.7 %copy-start = (bf16[768,1024]{1,0:T(8,128)(2,1)S(1)}, bf16[768,1024]{1,0:T(8,128)(2,1)}, u32[]{:S(2)}) copy-start(bf16[768,1024]{1,0:T(8,128)(2,1)} %param.11) | copy-start | bytes 4718596
  1.7 0.9 copy-start.2
  1.7 12.4 %copy-start.4 = (bf16[384,1024]{1,0:T(8,128)(2,1)}, bf16[384,1024]{1,0:T(8,128)(2,1)S(1)}, u32[]{:S(2)}) copy-start(bf16[384,1024]{1,0:T(8,128)(2,1)S(1)} %get-tuple-element.49) | copy-start | bytes 2359300
  2.6 11.5 %collective-permute-start.3 = (bf16[384,1024]{1,0:T(8,128)(2,1)S(1)}, bf16[384,1024]{1,0:T(8,128)(2,1)}, u32[]{:S(2)}, u32[]{:S(2)}) collective-permute-start(bf16[384,1024]{1,0:T(8,128)(2,1)S(1)} %get-tuple-element.50), channel_id=1, source_target_pairs={{0,5},{1,0},{2,7},{3,2},{4,9},{5,36},{6,11},{7,38},{8,13},{9,40},{... | collective-permute-start | bytes 2359304 | tf_op jit(solution)/shard_map/ppermute | solution.py:153
  3.9 23.1 %collective-permute-start = (bf16[384,1024]{1,0:T(8,128)(2,1)S(1)}, bf16[384,1024]{1,0:T(8,128)(2,1)}, u32[]{:S(2)}, u32[]{:S(2)}) collective-permute-start(bf16[384,1024]{1,0:T(8,128)(2,1)S(1)} %get-tuple-element.49), channel_id=1, source_target_pairs={{0,5},{1,0},{2,7},{3,2},{4,9},{5,36},{6,11},{7,38},{8,13},{9,40},{... | collective-permute-start | bytes 2359304 | tf_op jit(solution)/shard_map/ppermute | solution.py:153
  14.1 28.5 %collective-permute-start.4 = (bf16[384,1024]{1,0:T(8,128)(2,1)}, bf16[384,1024]{1,0:T(8,128)(2,1)}, u32[]{:S(2)}, u32[]{:S(2)}) collective-permute-start(bf16[384,1024]{1,0:T(8,128)(2,1)} %collective-permute-done.3), channel_id=1, source_target_pairs={{0,29},{1,4},{2,31},{3,6},{4,1},{5,8},{6,3},{7,10},{8,5},{9,12},{1... | collective-permute-start | bytes 2359304 | tf_op jit(solution)/shard_map/ppermute | solution.py:153
  27.0 15.6 %collective-permute-start.1 = (bf16[384,1024]{1,0:T(8,128)(2,1)}, bf16[384,1024]{1,0:T(8,128)(2,1)}, u32[]{:S(2)}, u32[]{:S(2)}) collective-permute-start(bf16[384,1024]{1,0:T(8,128)(2,1)} %collective-permute-done), channel_id=1, source_target_pairs={{0,29},{1,4},{2,31},{3,6},{4,1},{5,8},{6,3},{7,10},{8,5},{9,12},{1... | collective-permute-start | bytes 2359304 | tf_op jit(solution)/shard_map/ppermute | solution.py:153
  34.8 1.4 copy-start.1
  36.2 8.1 %copy-start.5 = (bf16[384,1024]{1,0:T(8,128)(2,1)S(1)}, bf16[384,1024]{1,0:T(8,128)(2,1)}, u32[]{:S(2)}) copy-start(bf16[384,1024]{1,0:T(8,128)(2,1)} %copy-done.4) | copy-start | bytes 2359300
  36.7 8.6 %copy-start.3 = (bf16[384,1024]{1,0:T(8,128)(2,1)S(1)}, bf16[384,1024]{1,0:T(8,128)(2,1)}, u32[]{:S(2)}) copy-start(bf16[384,1024]{1,0:T(8,128)(2,1)} %copy-done.2) | copy-start | bytes 2359300
  42.6 24.0 %collective-permute-start.2 = (bf16[384,1024]{1,0:T(8,128)(2,1)}, bf16[384,1024]{1,0:T(8,128)(2,1)}, u32[]{:S(2)}, u32[]{:S(2)}) collective-permute-start(bf16[384,1024]{1,0:T(8,128)(2,1)} %collective-permute-done.1.xa.refs_2_), channel_id=1, source_target_pairs={{0,5},{1,254},{2,7},{3,252},{4,9},{5,0},{6,11},{7,2},{8,13},{9,4},... | collective-permute-start | bytes 2359304 | tf_op jit(solution)/shard_map/ppermute | solution.py:153
  42.6 20.2 %collective-permute-start.5 = (bf16[384,1024]{1,0:T(8,128)(2,1)}, bf16[384,1024]{1,0:T(8,128)(2,1)}, u32[]{:S(2)}, u32[]{:S(2)}) collective-permute-start(bf16[384,1024]{1,0:T(8,128)(2,1)} %collective-permute-done.4.xb.refs_3_), channel_id=1, source_target_pairs={{0,5},{1,254},{2,7},{3,252},{4,9},{5,0},{6,11},{7,2},{8,13},{9,4},... | collective-permute-start | bytes 2359304 | tf_op jit(solution)/shard_map/ppermute | solution.py:153
  52.6 21.0 %collective-permute-start.8 = (f32[384,384]{1,0:T(8,128)}, f32[384,384]{1,0:T(8,128)}, u32[]{:S(2)}, u32[]{:S(2)}) collective-permute-start(f32[384,384]{1,0:T(8,128)} %get-tuple-element.30.refs_4_), channel_id=1, source_target_pairs={{0,2},{1,3},{2,0},{3,1},{4,6},{5,7},{6,4},{7,5},{8,10},{9,11},{10,... | collective-permute-start | bytes 1769480 | tf_op jit(solution)/shard_map/ppermute | solution.py:156
  59.5 21.1 %collective-permute-start.9 = (f32[384,384]{1,0:T(8,128)}, f32[384,384]{1,0:T(8,128)}, u32[]{:S(2)}, u32[]{:S(2)}) collective-permute-start(f32[384,384]{1,0:T(8,128)} %get-tuple-element.32.refs_7_), channel_id=1, source_target_pairs={{0,2},{1,3},{2,0},{3,1},{4,6},{5,7},{6,4},{7,5},{8,10},{9,11},{10,... | collective-permute-start | bytes 1769480 | tf_op jit(solution)/shard_map/ppermute | solution.py:156
  62.7 26.7 %collective-permute-start.7 = (bf16[384,1024]{1,0:T(8,128)(2,1)}, bf16[384,1024]{1,0:T(8,128)(2,1)}, u32[]{:S(2)}, u32[]{:S(2)}) collective-permute-start(bf16[384,1024]{1,0:T(8,128)(2,1)} %collective-permute-done.5.xb.refs_1_), channel_id=1, source_target_pairs={{0,255},{1,4},{2,253},{3,6},{4,1},{5,8},{6,3},{7,10},{8,5},{9,12},... | collective-permute-start | bytes 2359304 | tf_op jit(solution)/shard_map/ppermute | solution.py:153
  66.6 22.9 %collective-permute-start.6 = (bf16[384,1024]{1,0:T(8,128)(2,1)}, bf16[384,1024]{1,0:T(8,128)(2,1)}, u32[]{:S(2)}, u32[]{:S(2)}) collective-permute-start(bf16[384,1024]{1,0:T(8,128)(2,1)} %collective-permute-done.2.xa.refs_0_), channel_id=1, source_target_pairs={{0,255},{1,4},{2,253},{3,6},{4,1},{5,8},{6,3},{7,10},{8,5},{9,12},... | collective-permute-start | bytes 2359304 | tf_op jit(solution)/shard_map/ppermute | solution.py:153
  72.1 32.9 %collective-permute-start.11 = (f32[384,384]{1,0:T(8,128)}, f32[384,384]{1,0:T(8,128)}, u32[]{:S(2)}, u32[]{:S(2)}) collective-permute-start(f32[384,384]{1,0:T(8,128)} %get-tuple-element.28.refs_4_), channel_id=1, source_target_pairs={{0,2},{1,3},{2,0},{3,1},{4,6},{5,7},{6,4},{7,5},{8,10},{9,11},{10,... | collective-permute-start | bytes 1769480 | tf_op jit(solution)/shard_map/ppermute | solution.py:156
  94.8 10.2 %collective-permute-start.12 = (bf16[384,384]{1,0:T(8,128)(2,1)}, bf16[384,384]{1,0:T(8,128)(2,1)S(1)}, u32[]{:S(2)}, u32[]{:S(2)}) collective-permute-start(bf16[384,384]{1,0:T(8,128)(2,1)} %get-tuple-element.44.refs_6_), channel_id=1, source_target_pairs={{0,2},{1,3},{2,0},{3,1},{4,6},{5,7},{6,4},{7,5},{8,10},{9,11},{10,... | collective-permute-start | bytes 884744 | tf_op jit(solution)/shard_map/ppermute | solution.py:156
  102.9 10.1 %collective-permute-start.10 = (f32[2,64,8,384]{3,2,1,0:T(8,128)}, f32[2,64,8,384]{3,2,1,0:T(8,128)}, u32[]{:S(2)}, u32[]{:S(2)}) collective-permute-start(f32[2,64,8,384]{3,2,1,0:T(8,128)} %get-tuple-element.43), channel_id=1, source_target_pairs={{0,1},{1,0},{2,3},{3,2},{4,5},{5,4},{6,7},{7,6},{8,9},{9,8},{10,11... | collective-permute-start | bytes 4718600 | tf_op jit(solution)/shard_map/ppermute | solution.py:262
  105.0 0.7 copy-start.8
  112.9 3.8 %collective-permute-start.13 = (f32[2,64,8,384]{3,2,1,0:T(8,128)}, f32[2,64,8,384]{3,2,1,0:T(8,128)}, u32[]{:S(2)}, u32[]{:S(2)}) collective-permute-start(f32[2,64,8,384]{3,2,1,0:T(8,128)} %get-tuple-element.47), channel_id=1, source_target_pairs={{0,1},{1,0},{2,3},{3,2},{4,5},{5,4},{6,7},{7,6},{8,9},{9,8},{10,11... | collective-permute-start | bytes 4718600 | tf_op jit(solution)/shard_map/ppermute | solution.py:266
  112.9 3.7 %copy-start.7 = (f32[2,64,8,384]{3,2,1,0:T(8,128)S(1)}, f32[2,64,8,384]{3,2,1,0:T(8,128)}, u32[]{:S(2)}) copy-start(f32[2,64,8,384]{3,2,1,0:T(8,128)} %get-tuple-element.46) | copy-start | bytes 4718596
  115.2 12.2 %collective-permute-start.15 = (bf16[64,8,384]{2,1,0:T(8,128)(2,1)}, bf16[64,8,384]{2,1,0:T(8,128)(2,1)S(1)}, u32[]{:S(2)}, u32[]{:S(2)}) collective-permute-start(bf16[64,8,384]{2,1,0:T(8,128)(2,1)} %fusion.3), channel_id=1, source_target_pairs={{0,2},{1,3},{2,0},{3,1},{4,6},{5,7},{6,4},{7,5},{8,10},{9,11},{10,... | collective-permute-start | bytes 1179656 | tf_op jit(solution)/shard_map/ppermute | solution.py:264
  118.6 16.9 %collective-permute-start.14 = (bf16[64,8,384]{2,1,0:T(8,128)(2,1)}, bf16[64,8,384]{2,1,0:T(8,128)(2,1)}, u32[]{:S(2)}, u32[]{:S(2)}) collective-permute-start(bf16[64,8,384]{2,1,0:T(8,128)(2,1)} %fusion.2), channel_id=1, source_target_pairs={{0,2},{1,3},{2,0},{3,1},{4,6},{5,7},{6,4},{7,5},{8,10},{9,11},{10,... | collective-permute-start | bytes 1179656 | tf_op jit(solution)/shard_map/ppermute | solution.py:268
  119.5 16.0 %copy-start.6 = (f32[2,64,8,384]{3,2,1,0:T(8,128)S(1)}, f32[2,64,8,384]{3,2,1,0:T(8,128)}, u32[]{:S(2)}) copy-start(f32[2,64,8,384]{3,2,1,0:T(8,128)} %get-tuple-element.40) | copy-start | bytes 4718596

commit v9 on v8

--- a/solution.py
+++ b/solution.py
@@ -117,7 +117,7 @@
     xs = [refs[2 * k : 2 * k + 2] for k in range(n)]
     per = 2 if mixed else 1
     mixes, refs = refs[2 * n : (2 + per) * n], refs[(2 + per) * n :]
-    early, keep, send, w = refs
+    early, keep_far, keep_own, send_far, send_own, w = refs
 
     @pl.when(pl.program_id(0) == 0)
     def _():
@@ -129,9 +129,11 @@
     a, b = res[:, :, 0], res[:, :, 1]
     first = sc[1] == 0
     kept, sent = jnp.where(first, a, b), jnp.where(first, b, a)
-    for c in range(2):
-        keep[c] = kept[:, c]
-        send[c] = sent[:, c]
+    first = sc[2] == 0
+    keep_far[...] = jnp.where(first, kept[:, 1], kept[:, 0])
+    keep_own[...] = jnp.where(first, kept[:, 0], kept[:, 1])
+    send_far[...] = jnp.where(first, sent[:, 1], sent[:, 0])
+    send_own[...] = jnp.where(first, sent[:, 0], sent[:, 1])
 
 
 def body(
@@ -238,35 +240,34 @@
         n, mixed = len(xs), len(mixes) == 2 * len(xs)
         return pl.pallas_call(
             functools.partial(last_kernel, n=n, half=half, mixed=mixed),
-            out_shape=(sds((2, n_occ, 8, half), F32),) * 2,
+            out_shape=(sds((n_occ, 8, half), F32),) * 4,
             grid_spec=pltpu.PrefetchScalarGridSpec(
                 num_scalar_prefetch=1,
                 grid=(tiles,),
                 in_specs=x_specs * n + [whole] * len(mixes) + [row_spec],
-                out_specs=[pl.BlockSpec((2, groups, 8, half), lambda t, s: (0, t, 0, 0))] * 2,
+                out_specs=[pl.BlockSpec((groups, 8, half), lambda t, s: (t, 0, 0))] * 4,
                 scratch_shapes=[pltpu.VMEM((n * half, half), BF16)],
             ),
             cost_estimate=cost(n * n_aux * half * n_vir, 2 * n_aux * (n_vir + n * half)),
             name="last",
         )(sc, *(a for x in xs for a in x), *mixes, early)
 
-    def part(keep, got, c):
-        a = lax.dynamic_index_in_dim(keep, c, 0, keepdims=False)
-        return a + lax.dynamic_index_in_dim(got, c, 0, keepdims=False)
-
-    def low(keep, got, far):
-        return (part(keep, got, chip) + far.astype(F32)).astype(BF16)
-
-    keep0, send0 = last([x3, x4], [v3, v4], early[0])
+    def near(x):
+        return lax.ppermute(x, BOTH, swap(n_occ, 1))
+
+    def far(keep, got):
+        return lax.ppermute((keep + got).astype(BF16), BOTH, swap(n_occ, 2)).astype(F32)
+
+    keep0, own0, send0, mate0 = last([x3, x4], [v3, v4], early[0])
     early1, send0 = lax.optimization_barrier((early[1], send0))
-    got0 = lax.ppermute(send0, BOTH, swap(n_occ, 1))
-    away0 = part(keep0, got0, 1 - chip).astype(BF16)
-    far0 = lax.ppermute(away0, BOTH, swap(n_occ, 2))
-    keep1, send1 = last([x3, x4], [s3, q3, s4, q4], early1)
-    got1 = lax.ppermute(send1, BOTH, swap(n_occ, 1))
-    away1 = part(keep1, got1, 1 - chip).astype(BF16)
-    far1 = lax.ppermute(away1, BOTH, swap(n_occ, 2))
-    gamma_low = jnp.concatenate([low(keep0, got0, far1), low(keep1, got1, far0)], axis=2)
+    far0 = far(keep0, near(send0))
+    mate0 = near(mate0)
+    keep1, own1, send1, mate1 = last([x3, x4], [s3, q3, s4, q4], early1)
+    far1 = far(keep1, near(send1))
+    mate1 = near(mate1)
+    gamma_low = jnp.concatenate(
+        [(own0 + mate0 + far1).astype(BF16), (own1 + mate1 + far0).astype(BF16)], axis=2
+    )
     mine = lax.all_to_all(gamma_low, "occ", split_axis=0, concat_axis=0, tiled=True)
     mine = mine.reshape(2, n_occ // 2 * mine.shape[1], n_vir)
     out = jnp.einsum("zsd,zdw->zsw", mine, c_own, preferred_element_type=F32)

time: 178 us -> 181 us (1.017)
  waiting for transfers between devices: 46.2 us -> 50.9 us
  other arithmetic: 10.8 us -> 6.6 us
  blocking collectives: 37.4 us -> 39.7 us
    convert_element_type x4, other arithmetic: 7.1 us -> 2.93 us  [the longest x2 2.73 us: far(): (keep + got).astype(BF16)]
    all_to_all x1, blocking collectives: 37.4 us -> 39.7 us  [body(): lax.all_to_all(gamma_low, 'occ', split_axis=0, concat_axis=0, tiled=True)]
    ppermute x4 -> x6, starting transfers between devices: 4.21 us -> 6.13 us  [the longest x4 3.93 us: near(): return lax.ppermute(x, BOTH, swap(n_occ, 1))]
    ppermute x4 -> x6, waiting for transfers between devices: 14.7 us -> 16.4 us  [the longest x2 16.4 us: far(): lax.ppermute((keep + got).astype(BF16), BOTH, swap(n_occ, 2)).astype(F32)]
  transfers between devices with their start and end apart: 16 -> 18, of which waited for: 8 -> 6; matrix products, arithmetic and copies ran while one was open for 7% -> 5% of each run, Pallas kernels for 25% -> 25%
where the time goes in v9:
time: 181 us; the launch traced here: 180 us
  waiting for transfers between devices  50.9 us (28%)
  Pallas kernels  44.3 us (24%)
  blocking collectives  39.7 us (22%)
  starting transfers between devices  29.5 us (16%)
  local copies, waits for them, and re-layouts  6.65 us (4%)
  other arithmetic  6.6 us (4%)
  matrix products  2.33 us (1%)
    all_to_all x1, blocking collectives, body(): lax.all_to_all(gamma_low, 'occ', split_axis=0, concat_axis=0, tiled=True)  39.7 us
    ppermute x8, waiting for transfers between devices, ring(): return lax.ppermute(x, BOTH, moves(n_occ, rule))  25.9 us
    pallas_call x4, Pallas kernels, amp(): pl.pallas_call(functools.partial(amp_kernel, half=half, slot=slot), out_s...  21.8 us
    ppermute x8, starting transfers between devices, ring(): return lax.ppermute(x, BOTH, moves(n_occ, rule))  18.4 us
    ppermute x2, waiting for transfers between devices, far(): lax.ppermute((keep + got).astype(BF16), BOTH, swap(n_occ, 2)).astype(F32)  16.4 us
    pallas_call x2, Pallas kernels, last(): pl.pallas_call(functools.partial(last_kernel, n=n, half=half, mixed=mixed...  13.7 us
    pallas_call x1, Pallas kernels, gamma(): pl.pallas_call(functools.partial(gamma_kernel, n=n, half=half), out_shape...  8.86 us
    ppermute x4, waiting for transfers between devices, exchange(): return lax.ppermute(s, BOTH, swap(n_occ, 2))  8.56 us
  transfers between devices with their start and end apart: 18, of which 6 were waited for; matrix products, arithmetic and copies ran while one was open for 5% of the time, Pallas kernels for 25%

profile of v9, /device:TPU:56, one launch (start us, length us, event | category | flops | bytes accessed | tf_op | source)
XLA Modules:
  0.0 180.2 jit_solution(6947435255854431861)
XLA Ops:
  0.1 1.6 dynamic-slice_bitcast_fusion
  1.7 0.9 copy-done.2
  2.6 1.4 collective-permute-start
  3.9 2.7 %collective-permute-start.3 = (bf16[384,1024]{1,0:T(8,128)(2,1)S(1)}, bf16[384,1024]{1,0:T(8,128)(2,1)}, u32[]{:S(2)}, u32[]{:S(2)}) collective-permute-start(bf16[384,1024]{1,0:T(8,128)(2,1)S(1)} %get-tuple-element.57), channel_id=1, source_target_pairs={{0,5},{1,0},{2,7},{3,2},{4,9},{5,36},{6,11},{7,38},{8,13},{9,40},{... | collective-permute-start | bytes 2359304 | tf_op jit(solution)/shard_map/ppermute | solution.py:155
  6.9 7.2 %collective-permute-done = bf16[384,1024]{1,0:T(8,128)(2,1)} collective-permute-done((bf16[384,1024]{1,0:T(8,128)(2,1)S(1)}, bf16[384,1024]{1,0:T(8,128)(2,1)}, u32[]{:S(2)}, u32[]{:S(2)}) %collective-permute-start) | collective-permute-done | bytes 786464 | tf_op jit(solution)/shard_map/ppermute | solution.py:155
  14.1 4.1 %collective-permute-start.1 = (bf16[384,1024]{1,0:T(8,128)(2,1)}, bf16[384,1024]{1,0:T(8,128)(2,1)}, u32[]{:S(2)}, u32[]{:S(2)}) collective-permute-start(bf16[384,1024]{1,0:T(8,128)(2,1)} %collective-permute-done), channel_id=1, source_target_pairs={{0,29},{1,4},{2,31},{3,6},{4,1},{5,8},{6,3},{7,10},{8,5},{9,12},{1... | collective-permute-start | bytes 2359304 | tf_op jit(solution)/shard_map/ppermute | solution.py:155
  18.2 8.8 %collective-permute-done.3 = bf16[384,1024]{1,0:T(8,128)(2,1)} collective-permute-done((bf16[384,1024]{1,0:T(8,128)(2,1)S(1)}, bf16[384,1024]{1,0:T(8,128)(2,1)}, u32[]{:S(2)}, u32[]{:S(2)}) %collective-permute-start.3) | collective-permute-done | bytes 786464 | tf_op jit(solution)/shard_map/ppermute | solution.py:155
  27.0 5.6 %collective-permute-start.4 = (bf16[384,1024]{1,0:T(8,128)(2,1)}, bf16[384,1024]{1,0:T(8,128)(2,1)}, u32[]{:S(2)}, u32[]{:S(2)}) collective-permute-start(bf16[384,1024]{1,0:T(8,128)(2,1)} %collective-permute-done.3), channel_id=1, source_target_pairs={{0,29},{1,4},{2,31},{3,6},{4,1},{5,8},{6,3},{7,10},{8,5},{9,12},{1... | collective-permute-start | bytes 2359304 | tf_op jit(solution)/shard_map/ppermute | solution.py:155
  34.9 1.2 copy-done.1
  36.7 10.0 %collective-permute-done.4.xb.refs_3_ = bf16[384,1024]{1,0:T(8,128)(2,1)} collective-permute-done((bf16[384,1024]{1,0:T(8,128)(2,1)}, bf16[384,1024]{1,0:T(8,128)(2,1)}, u32[]{:S(2)}, u32[]{:S(2)}) %collective-permute-start.4) | collective-permute-done | bytes 786464 | tf_op jit(solution)/shard_map/ppermute | solution.py:155
  46.7 1.0 broadcast_select_fusion.xb.refs_1_
  47.6 1.0 broadcast_select_fusion.1.xa.refs_0_
  49.4 5.5 %amp.5 = (f32[384,384]{1,0:T(8,128)}, bf16[384,384]{1,0:T(8,128)(2,1)}) custom-call(s32[8]{0:T(128)} %stack.49.sc, bf16[768,2048]{1,0:T(8,128)(2,1)} %bitcast.20, bf16[384,1024]{1,0:T(8,128)(2,1)} %broadcast_select_fusion.1.xa.refs_0_, bf16[384,1024]{1,0:T(8,128)(2,1)} %broadcast_select_fusion.xb.refs_1_, f32[384,128]{1,0:T(8,128)} %broadcast_in_dim.41.evc, ...), custom_call_target="tpu_custom_call" | custom-call | flops 1207959552 | bytes 4718592 | tf_op jit(solution)/shard_map/amp/pallas_call | solution.py:171
  54.9 1.5 collective-permute-start.8
  56.4 5.4 %amp.6 = (f32[384,384]{1,0:T(8,128)}, bf16[384,384]{1,0:T(8,128)(2,1)}) custom-call(s32[8]{0:T(128)} %stack.49.sc, bf16[768,2048]{1,0:T(8,128)(2,1)} %bitcast.21, bf16[384,1024]{1,0:T(8,128)(2,1)} %collective-permute-done.1.xa.refs_2_, bf16[384,1024]{1,0:T(8,128)(2,1)} %collective-permute-done.4.xb.refs_3_, f32[384,128]{1,0:T(8,128)} %broadcast_in_dim.41.evc, ...), custom_call_target="tpu_custom_call" | custom-call | flops 1207959552 | bytes 4718592 | tf_op jit(solution)/shard_map/amp/pallas_call | solution.py:171
  62.4 4.4 %collective-permute-start.7 = (bf16[384,1024]{1,0:T(8,128)(2,1)}, bf16[384,1024]{1,0:T(8,128)(2,1)}, u32[]{:S(2)}, u32[]{:S(2)}) collective-permute-start(bf16[384,1024]{1,0:T(8,128)(2,1)} %collective-permute-done.5.xb.refs_1_), channel_id=1, source_target_pairs={{0,255},{1,4},{2,253},{3,6},{4,1},{5,8},{6,3},{7,10},{8,5},{9,12},... | collective-permute-start | bytes 2359304 | tf_op jit(solution)/shard_map/ppermute | solution.py:155
  66.9 5.5 %amp.4 = (f32[384,384]{1,0:T(8,128)}, bf16[384,384]{1,0:T(8,128)(2,1)}) custom-call(s32[8]{0:T(128)} %stack.49.sc, bf16[768,2048]{1,0:T(8,128)(2,1)} %bitcast.22, bf16[384,1024]{1,0:T(8,128)(2,1)} %collective-permute-done.2.xa.refs_0_, bf16[384,1024]{1,0:T(8,128)(2,1)} %collective-permute-done.5.xb.refs_1_, f32[384,128]{1,0:T(8,128)} %broadcast_in_dim.41.evc, ...), custom_call_target="tpu_custom_call" | custom-call | flops 1207959552 | bytes 4718592 | tf_op jit(solution)/shard_map/amp/pallas_call | solution.py:171
  72.3 1.5 collective-permute-start.11
  73.8 8.6 %collective-permute-done.9.refs_8_ = f32[384,384]{1,0:T(8,128)} collective-permute-done((f32[384,384]{1,0:T(8,128)}, f32[384,384]{1,0:T(8,128)}, u32[]{:S(2)}, u32[]{:S(2)}) %collective-permute-start.9) | collective-permute-done | bytes 589856 | tf_op jit(solution)/shard_map/ppermute | solution.py:158
  82.4 8.9 %gamma.1 = (f32[2048,384]{1,0:T(8,128)}, f32[2048,384]{1,0:T(8,128)}) custom-call(s32[8]{0:T(128)} %stack.49.sc, bf16[384,1024]{1,0:T(8,128)(2,1)} %broadcast_select_fusion.1.xa.refs_0_, bf16[384,1024]{1,0:T(8,128)(2,1)} %broadcast_select_fusion.xb.refs_1_, bf16[384,1024]{1,0:T(8,128)(2,1)} %collective-permute-done.1.xa.refs_2_, ...), custom_call_target="tpu_custom_call" | custom-call | flops 2415919104 | bytes 9437184 | tf_op jit(solution)/shard_map/gamma/pallas_call | solution.py:203
  91.3 5.4 %amp.7 = (bf16[384,384]{1,0:T(8,128)(2,1)}, bf16[384,384]{1,0:T(8,128)(2,1)}) custom-call(s32[8]{0:T(128)} %stack.49.sc, bf16[768,2048]{1,0:T(8,128)(2,1)} %bitcast.23, bf16[384,1024]{1,0:T(8,128)(2,1)} %collective-permute-done.6.xa.refs_2_, bf16[384,1024]{1,0:T(8,128)(2,1)} %collective-permute-done.7.xb.refs_3_, f32[384,128]{1,0:T(8,128)} %broadcast_in_dim.41.evc, ...), custom_call_target="tpu_custom_call" | custom-call | flops 1207959552 | bytes 4718592 | tf_op jit(solution)/shard_map/amp/pallas_call | solution.py:171
  96.6 1.5 collective-permute-start.12
  98.1 6.5 %last.2 = (f32[64,8,384]{2,1,0:T(8,128)}, f32[64,8,384]{2,1,0:T(8,128)}, f32[64,8,384]{2,1,0:T(8,128)}, f32[64,8,384]{2,1,0:T(8,128)}) custom-call(s32[8]{0:T(128)} %stack.49.sc, bf16[384,1024]{1,0:T(8,128)(2,1)} %collective-permute-done.2.xa.refs_0_, bf16[384,1024]{1,0:T(8,128)(2,1)} %collective-permute-done.5.xb.refs_1_, ...), custom_call_target="tpu_custom_call" | custom-call | flops 1207959552 | bytes 6291456 | tf_op jit(solution)/shard_map/last/pallas_call | solution.py:241
  104.6 3.2 %collective-permute-start.16 = (f32[64,8,384]{2,1,0:T(8,128)}, f32[64,8,384]{2,1,0:T(8,128)}, u32[]{:S(2)}, u32[]{:S(2)}) collective-permute-start(f32[64,8,384]{2,1,0:T(8,128)} %get-tuple-element.55), channel_id=1, source_target_pairs={{0,1},{1,0},{2,3},{3,2},{4,5},{5,4},{6,7},{7,6},{8,9},{9,8},{10,11... | collective-permute-start | bytes 2359304 | tf_op jit(solution)/shard_map/ppermute | solution.py:256
  108.6 7.2 %last.3 = (f32[64,8,384]{2,1,0:T(8,128)}, f32[64,8,384]{2,1,0:T(8,128)}, f32[64,8,384]{2,1,0:T(8,128)}, f32[64,8,384]{2,1,0:T(8,128)}) custom-call(s32[8]{0:T(128)} %stack.49.sc, bf16[384,1024]{1,0:T(8,128)(2,1)} %collective-permute-done.2.xa.refs_0_, bf16[384,1024]{1,0:T(8,128)(2,1)} %collective-permute-done.5.xb.refs_1_, ...), custom_call_target="tpu_custom_call" | custom-call | flops 1207959552 | bytes 6291456 | tf_op jit(solution)/shard_map/last/pallas_call | solution.py:241
  116.5 1.5 add_convert_fusion.1
  118.6 1.2 add_convert_fusion.3
  119.8 1.6 collective-permute-start.14
  121.4 8.7 %collective-permute-done.17 = bf16[64,8,384]{2,1,0:T(8,128)(2,1)S(1)} collective-permute-done((bf16[64,8,384]{2,1,0:T(8,128)(2,1)S(1)}, bf16[64,8,384]{2,1,0:T(8,128)(2,1)S(1)}, u32[]{:S(2)}, u32[]{:S(2)}) %collective-permute-start.17) | collective-permute-done | bytes 393248 | tf_op jit(solution)/shard_map/ppermute | solution.py:259
  130.2 7.8 %collective-permute-done.14 = bf16[64,8,384]{2,1,0:T(8,128)(2,1)S(1)} collective-permute-done((bf16[64,8,384]{2,1,0:T(8,128)(2,1)S(1)}, bf16[64,8,384]{2,1,0:T(8,128)(2,1)S(1)}, u32[]{:S(2)}, u32[]{:S(2)}) %collective-permute-start.14) | collective-permute-done | bytes 393248 | tf_op jit(solution)/shard_map/ppermute | solution.py:259
  138.1 39.7 %all_to_all.5 = bf16[64,8,768]{2,1,0:T(8,128)(2,1)S(1)} all-to-all(bf16[64,8,768]{2,1,0:T(8,128)(2,1)S(1)} %pad_maximum_fusion), channel_id=1, replica_groups=mesh['occ'=64,'off'=4] {'occ'}, dimensions={0} | all-to-all | bytes 1572864 | tf_op jit(solution)/shard_map/all_to_all | solution.py:271
  177.8 2.3 %fusion.1 = f32[2,256,1024]{2,1,0:T(8,128)} fusion(bf16[2,256,768]{2,1,0:T(8,128)(2,1)S(1)} %bitcast.25, bf16[2,768,1024]{2,1,0:T(8,128)(2,1)S(1)} %maximum_select_fusion), kind=kOutput, calls=%fused_computation.16 | convolution fusion | flops 805306368 | bytes 6029312 | tf_op jit(solution)/shard_map/zsd,zdw->zsw/dot_general | solution.py:273
  (56 shorter events, 7.0 us)
Async XLA Ops:
  0.0 6.6 %copy-start.10 = (f32[256]{0:T(256)S(1)}, f32[256]{0:T(256)}, u32[]{:S(2)}) copy-start(f32[256]{0:T(256)} %param.10) | copy-start | bytes 3076
  0.0 6.6 %copy-start.9 = (s32[768]{0:T(1024)S(1)}, s32[768]{0:T(1024)}, u32[]{:S(2)}) copy-start(s32[768]{0:T(1024)} %param.8) | copy-start | bytes 9220
  0.0 32.6 %copy-start.12 = (s32[64]{0:T(128)S(1)}, s32[64]{0:T(128)}, u32[]{:S(2)}) copy-start(s32[64]{0:T(128)} %param.7) | copy-start | bytes 772
  0.0 32.6 %copy-start.11 = (f32[256]{0:T(256)S(1)}, f32[256]{0:T(256)}, u32[]{:S(2)}) copy-start(f32[256]{0:T(256)} %param.9) | copy-start | bytes 3076
  0.0 34.6 %copy-start = (bf16[768,1024]{1,0:T(8,128)(2,1)S(1)}, bf16[768,1024]{1,0:T(8,128)(2,1)}, u32[]{:S(2)}) copy-start(bf16[768,1024]{1,0:T(8,128)(2,1)} %param.11) | copy-start | bytes 4718596
  1.7 0.9 copy-start.2
  1.7 12.4 %copy-start.4 = (bf16[384,1024]{1,0:T(8,128)(2,1)}, bf16[384,1024]{1,0:T(8,128)(2,1)S(1)}, u32[]{:S(2)}) copy-start(bf16[384,1024]{1,0:T(8,128)(2,1)S(1)} %get-tuple-element.57) | copy-start | bytes 2359300
  2.6 11.5 %collective-permute-start = (bf16[384,1024]{1,0:T(8,128)(2,1)S(1)}, bf16[384,1024]{1,0:T(8,128)(2,1)}, u32[]{:S(2)}, u32[]{:S(2)}) collective-permute-start(bf16[384,1024]{1,0:T(8,128)(2,1)S(1)} %get-tuple-element.58), channel_id=1, source_target_pairs={{0,5},{1,0},{2,7},{3,2},{4,9},{5,36},{6,11},{7,38},{8,13},{9,40},{... | collective-permute-start | bytes 2359304 | tf_op jit(solution)/shard_map/ppermute | solution.py:155
  3.9 23.1 %collective-permute-start.3 = (bf16[384,1024]{1,0:T(8,128)(2,1)S(1)}, bf16[384,1024]{1,0:T(8,128)(2,1)}, u32[]{:S(2)}, u32[]{:S(2)}) collective-permute-start(bf16[384,1024]{1,0:T(8,128)(2,1)S(1)} %get-tuple-element.57), channel_id=1, source_target_pairs={{0,5},{1,0},{2,7},{3,2},{4,9},{5,36},{6,11},{7,38},{8,13},{9,40},{... | collective-permute-start | bytes 2359304 | tf_op jit(solution)/shard_map/ppermute | solution.py:155
  14.1 22.5 %collective-permute-start.1 = (bf16[384,1024]{1,0:T(8,128)(2,1)}, bf16[384,1024]{1,0:T(8,128)(2,1)}, u32[]{:S(2)}, u32[]{:S(2)}) collective-permute-start(bf16[384,1024]{1,0:T(8,128)(2,1)} %collective-permute-done), channel_id=1, source_target_pairs={{0,29},{1,4},{2,31},{3,6},{4,1},{5,8},{6,3},{7,10},{8,5},{9,12},{1... | collective-permute-start | bytes 2359304 | tf_op jit(solution)/shard_map/ppermute | solution.py:155
  27.0 19.7 %collective-permute-start.4 = (bf16[384,1024]{1,0:T(8,128)(2,1)}, bf16[384,1024]{1,0:T(8,128)(2,1)}, u32[]{:S(2)}, u32[]{:S(2)}) collective-permute-start(bf16[384,1024]{1,0:T(8,128)(2,1)} %collective-permute-done.3), channel_id=1, source_target_pairs={{0,29},{1,4},{2,31},{3,6},{4,1},{5,8},{6,3},{7,10},{8,5},{9,12},{1... | collective-permute-start | bytes 2359304 | tf_op jit(solution)/shard_map/ppermute | solution.py:155
  34.6 1.4 copy-start.1
  36.0 10.6 %copy-start.5 = (bf16[384,1024]{1,0:T(8,128)(2,1)S(1)}, bf16[384,1024]{1,0:T(8,128)(2,1)}, u32[]{:S(2)}) copy-start(bf16[384,1024]{1,0:T(8,128)(2,1)} %copy-done.4) | copy-start | bytes 2359300
  36.0 11.6 %copy-start.3 = (bf16[384,1024]{1,0:T(8,128)(2,1)S(1)}, bf16[384,1024]{1,0:T(8,128)(2,1)}, u32[]{:S(2)}) copy-start(bf16[384,1024]{1,0:T(8,128)(2,1)} %copy-done.2) | copy-start | bytes 2359300
  36.6 30.2 %collective-permute-start.2 = (bf16[384,1024]{1,0:T(8,128)(2,1)}, bf16[384,1024]{1,0:T(8,128)(2,1)}, u32[]{:S(2)}, u32[]{:S(2)}) collective-permute-start(bf16[384,1024]{1,0:T(8,128)(2,1)} %collective-permute-done.1.xa.refs_2_), channel_id=1, source_target_pairs={{0,5},{1,254},{2,7},{3,252},{4,9},{5,0},{6,11},{7,2},{8,13},{9,4},... | collective-permute-start | bytes 2359304 | tf_op jit(solution)/shard_map/ppermute | solution.py:155
  46.6 15.7 %collective-permute-start.5 = (bf16[384,1024]{1,0:T(8,128)(2,1)}, bf16[384,1024]{1,0:T(8,128)(2,1)}, u32[]{:S(2)}, u32[]{:S(2)}) collective-permute-start(bf16[384,1024]{1,0:T(8,128)(2,1)} %collective-permute-done.4.xb.refs_3_), channel_id=1, source_target_pairs={{0,5},{1,254},{2,7},{3,252},{4,9},{5,0},{6,11},{7,2},{8,13},{9,4},... | collective-permute-start | bytes 2359304 | tf_op jit(solution)/shard_map/ppermute | solution.py:155
  54.9 18.9 %collective-permute-start.8 = (f32[384,384]{1,0:T(8,128)}, f32[384,384]{1,0:T(8,128)}, u32[]{:S(2)}, u32[]{:S(2)}) collective-permute-start(f32[384,384]{1,0:T(8,128)} %get-tuple-element.34.refs_4_), channel_id=1, source_target_pairs={{0,2},{1,3},{2,0},{3,1},{4,6},{5,7},{6,4},{7,5},{8,10},{9,11},{10,... | collective-permute-start | bytes 1769480 | tf_op jit(solution)/shard_map/ppermute | solution.py:158
  61.8 20.5 %collective-permute-start.9 = (f32[384,384]{1,0:T(8,128)}, f32[384,384]{1,0:T(8,128)}, u32[]{:S(2)}, u32[]{:S(2)}) collective-permute-start(f32[384,384]{1,0:T(8,128)} %get-tuple-element.36.refs_7_), channel_id=1, source_target_pairs={{0,2},{1,3},{2,0},{3,1},{4,6},{5,7},{6,4},{7,5},{8,10},{9,11},{10,... | collective-permute-start | bytes 1769480 | tf_op jit(solution)/shard_map/ppermute | solution.py:158
  62.4 28.9 %collective-permute-start.7 = (bf16[384,1024]{1,0:T(8,128)(2,1)}, bf16[384,1024]{1,0:T(8,128)(2,1)}, u32[]{:S(2)}, u32[]{:S(2)}) collective-permute-start(bf16[384,1024]{1,0:T(8,128)(2,1)} %collective-permute-done.5.xb.refs_1_), channel_id=1, source_target_pairs={{0,255},{1,4},{2,253},{3,6},{4,1},{5,8},{6,3},{7,10},{8,5},{9,12},... | collective-permute-start | bytes 2359304 | tf_op jit(solution)/shard_map/ppermute | solution.py:155
  66.8 24.5 %collective-permute-start.6 = (bf16[384,1024]{1,0:T(8,128)(2,1)}, bf16[384,1024]{1,0:T(8,128)(2,1)}, u32[]{:S(2)}, u32[]{:S(2)}) collective-permute-start(bf16[384,1024]{1,0:T(8,128)(2,1)} %collective-permute-done.2.xa.refs_0_), channel_id=1, source_target_pairs={{0,255},{1,4},{2,253},{3,6},{4,1},{5,8},{6,3},{7,10},{8,5},{9,12},... | collective-permute-start | bytes 2359304 | tf_op jit(solution)/shard_map/ppermute | solution.py:155
  72.3 35.5 %collective-permute-start.11 = (f32[384,384]{1,0:T(8,128)}, f32[384,384]{1,0:T(8,128)}, u32[]{:S(2)}, u32[]{:S(2)}) collective-permute-start(f32[384,384]{1,0:T(8,128)} %get-tuple-element.32.refs_4_), channel_id=1, source_target_pairs={{0,2},{1,3},{2,0},{3,1},{4,6},{5,7},{6,4},{7,5},{8,10},{9,11},{10,... | collective-permute-start | bytes 1769480 | tf_op jit(solution)/shard_map/ppermute | solution.py:158
  96.6 11.2 %collective-permute-start.12 = (bf16[384,384]{1,0:T(8,128)(2,1)}, bf16[384,384]{1,0:T(8,128)(2,1)S(1)}, u32[]{:S(2)}, u32[]{:S(2)}) collective-permute-start(bf16[384,384]{1,0:T(8,128)(2,1)} %get-tuple-element.46.refs_6_), channel_id=1, source_target_pairs={{0,2},{1,3},{2,0},{3,1},{4,6},{5,7},{6,4},{7,5},{8,10},{9,11},{10,... | collective-permute-start | bytes 884744 | tf_op jit(solution)/shard_map/ppermute | solution.py:158
  104.6 11.8 %collective-permute-start.16 = (f32[64,8,384]{2,1,0:T(8,128)}, f32[64,8,384]{2,1,0:T(8,128)}, u32[]{:S(2)}, u32[]{:S(2)}) collective-permute-start(f32[64,8,384]{2,1,0:T(8,128)} %get-tuple-element.55), channel_id=1, source_target_pairs={{0,1},{1,0},{2,3},{3,2},{4,5},{5,4},{6,7},{7,6},{8,9},{9,8},{10,11... | collective-permute-start | bytes 2359304 | tf_op jit(solution)/shard_map/ppermute | solution.py:256
  107.9 0.7 copy-start.8
  115.7 14.3 %copy-start.7 = (f32[64,8,384]{2,1,0:T(8,128)S(1)}, f32[64,8,384]{2,1,0:T(8,128)}, u32[]{:S(2)}) copy-start(f32[64,8,384]{2,1,0:T(8,128)} %get-tuple-element.52) | copy-start | bytes 2359300
  115.8 2.8 %collective-permute-start.13 = (f32[64,8,384]{2,1,0:T(8,128)}, f32[64,8,384]{2,1,0:T(8,128)S(1)}, u32[]{:S(2)}, u32[]{:S(2)}) collective-permute-start(f32[64,8,384]{2,1,0:T(8,128)} %get-tuple-element.51), channel_id=1, source_target_pairs={{0,1},{1,0},{2,3},{3,2},{4,5},{5,4},{6,7},{7,6},{8,9},{9,8},{10,11... | collective-permute-start | bytes 2359304 | tf_op jit(solution)/shard_map/ppermute | solution.py:256
  115.9 5.5 %collective-permute-start.15 = (f32[64,8,384]{2,1,0:T(8,128)}, f32[64,8,384]{2,1,0:T(8,128)S(1)}, u32[]{:S(2)}, u32[]{:S(2)}) collective-permute-start(f32[64,8,384]{2,1,0:T(8,128)} %get-tuple-element.53), channel_id=1, source_target_pairs={{0,1},{1,0},{2,3},{3,2},{4,5},{5,4},{6,7},{7,6},{8,9},{9,8},{10,11... | collective-permute-start | bytes 2359304 | tf_op jit(solution)/shard_map/ppermute | solution.py:256
  116.4 13.8 %collective-permute-start.10 = (f32[64,8,384]{2,1,0:T(8,128)}, f32[64,8,384]{2,1,0:T(8,128)S(1)}, u32[]{:S(2)}, u32[]{:S(2)}) collective-permute-start(f32[64,8,384]{2,1,0:T(8,128)} %get-tuple-element.45), channel_id=1, source_target_pairs={{0,1},{1,0},{2,3},{3,2},{4,5},{5,4},{6,7},{7,6},{8,9},{9,8},{10,11... | collective-permute-start | bytes 2359304 | tf_op jit(solution)/shard_map/ppermute | solution.py:256
  116.5 21.5 %copy-start.6 = (f32[64,8,384]{2,1,0:T(8,128)S(1)}, f32[64,8,384]{2,1,0:T(8,128)}, u32[]{:S(2)}) copy-start(f32[64,8,384]{2,1,0:T(8,128)} %get-tuple-element.44) | copy-start | bytes 2359300
  118.0 12.1 %collective-permute-start.17 = (bf16[64,8,384]{2,1,0:T(8,128)(2,1)S(1)}, bf16[64,8,384]{2,1,0:T(8,128)(2,1)S(1)}, u32[]{:S(2)}, u32[]{:S(2)}) collective-permute-start(bf16[64,8,384]{2,1,0:T(8,128)(2,1)S(1)} %add_convert_fusion.1), channel_id=1, source_target_pairs={{0,2},{1,3},{2,0},{3,1},{4,6},{5,7},{6,4},{7,5},{8,10},{9,11},{10,... | collective-permute-start | bytes 1179656 | tf_op jit(solution)/shard_map/ppermute | solution.py:259
  119.8 18.1 %collective-permute-start.14 = (bf16[64,8,384]{2,1,0:T(8,128)(2,1)S(1)}, bf16[64,8,384]{2,1,0:T(8,128)(2,1)S(1)}, u32[]{:S(2)}, u32[]{:S(2)}) collective-permute-start(bf16[64,8,384]{2,1,0:T(8,128)(2,1)S(1)} %add_convert_fusion.3), channel_id=1, source_target_pairs={{0,2},{1,3},{2,0},{3,1},{4,6},{5,7},{6,4},{7,5},{8,10},{9,11},{10,... | collective-permute-start | bytes 1179656 | tf_op jit(solution)/shard_map/ppermute | solution.py:259

commit v10 on v9

--- a/solution.py
+++ b/solution.py
@@ -42,6 +42,10 @@
     if core == 0:
         return i + 1, 1
     return (i + RING, 0) if i % RING else (i, 0)
+
+
+def round1_swapped(i, core):
+    return round1(i, 1 - core)
 
 
 def round2(i, core):
@@ -159,7 +163,7 @@
 
     tile = n_aux // 2
     x0 = [lax.dynamic_slice(own, (h * half, p * tile), (half, tile)) for p in range(2)]
-    x1 = [ring(x0[p], round1) for p in range(2)]
+    x1 = [ring(x0[p], rule) for p, rule in enumerate((round1, round1_swapped))]
     x2 = [ring(x1[p], round2) for p in range(2)]
 
     ev = lookup(vir_level, vir_table)
@@ -221,10 +225,10 @@
     c_flip = c_halves[::-1]
     c_both = [jnp.concatenate([c[0], c[1]], axis=0) for c in (c_halves, c_flip)]
     c_own = jnp.where(chip == 0, jnp.stack(c_both), jnp.stack(c_both[::-1]))
-    x2[0], c_own = lax.optimization_barrier((x2[0], c_own))
     x3 = [ring(x2[p], round3) for p in range(2)]
     s2, v2 = amp(x2, 1, F32)
     q2 = exchange(s2)
+    x3[1], c_own = lax.optimization_barrier((x3[1], c_own))
     x4 = [ring(x3[p], round4) for p in range(2)]
     s3, v3 = amp(x3, 2, F32)
     q3 = exchange(s3)

time: 181 us -> 181 us (level)
  other arithmetic: 6.6 us -> 10.6 us
  starting transfers between devices: 29.5 us -> 27.3 us
  local copies, waits for them, and re-layouts: 6.65 us -> 4.6 us
    ppermute x8, waiting for transfers between devices: 25.9 us -> 30 us  [ring(): return lax.ppermute(x, BOTH, moves(n_occ, rule))]
    ppermute x4, starting transfers between devices: 3.93 us -> 0.71 us  [near(): return lax.ppermute(x, BOTH, swap(n_occ, 1))]
    select_n x1, other arithmetic: 0.51 us -> 3.36 us  [body(): c_own = jnp.where(chip == 0, jnp.stack(c_both), jnp.stack(c_both[::-1]))]
    ppermute x4, waiting for transfers between devices: 8.56 us -> 6.04 us  [exchange(): return lax.ppermute(s, BOTH, swap(n_occ, 2))]
    unnamed x26 -> x16, local copies, waits for them, and re-layouts: 2.78 us -> 0.73 us
  transfers between devices with their start and end apart: 18 -> 18, of which waited for: 6 -> 7; matrix products, arithmetic and copies ran while one was open for 5% -> 7% of each run, Pallas kernels for 25% -> 25%
where the time goes in v10:
time: 181 us; the launch traced here: 180 us
  waiting for transfers between devices  52.5 us (29%)
  Pallas kernels  44.3 us (24%)
  blocking collectives  38.3 us (21%)
  starting transfers between devices  27.3 us (15%)
  other arithmetic  10.6 us (6%)
  local copies, waits for them, and re-layouts  4.6 us (3%)
  matrix products  2.33 us (1%)
    all_to_all x1, blocking collectives, body(): lax.all_to_all(gamma_low, 'occ', split_axis=0, concat_axis=0, tiled=True)  38.3 us
    ppermute x8, waiting for transfers between devices, ring(): return lax.ppermute(x, BOTH, moves(n_occ, rule))  30 us
    pallas_call x4, Pallas kernels, amp(): pl.pallas_call(functools.partial(amp_kernel, half=half, slot=slot), out_s...  21.7 us
    ppermute x8, starting transfers between devices, ring(): return lax.ppermute(x, BOTH, moves(n_occ, rule))  19.1 us
    ppermute x2, waiting for transfers between devices, far(): lax.ppermute((keep + got).astype(BF16), BOTH, swap(n_occ, 2)).astype(F32)  16.4 us
    pallas_call x2, Pallas kernels, last(): pl.pallas_call(functools.partial(last_kernel, n=n, half=half, mixed=mixed...  13.7 us
    pallas_call x1, Pallas kernels, gamma(): pl.pallas_call(functools.partial(gamma_kernel, n=n, half=half), out_shape...  8.85 us
    ppermute x4, waiting for transfers between devices, exchange(): return lax.ppermute(s, BOTH, swap(n_occ, 2))  6.04 us
  transfers between devices with their start and end apart: 18, of which 7 were waited for; matrix products, arithmetic and copies ran while one was open for 7% of the time, Pallas kernels for 25%

profile of v10, /device:TPU:56, one launch (start us, length us, event | category | flops | bytes accessed | tf_op | source)
XLA Modules:
  0.0 180.1 jit_solution(4330310723753127128)
XLA Ops:
  0.1 1.6 dynamic-slice_bitcast_fusion
  1.7 4.3 %collective-permute-start.3 = (bf16[384,1024]{1,0:T(8,128)(2,1)S(1)}, bf16[384,1024]{1,0:T(8,128)(2,1)}, u32[]{:S(2)}, u32[]{:S(2)}) collective-permute-start(bf16[384,1024]{1,0:T(8,128)(2,1)S(1)} %get-tuple-element.57), channel_id=1, source_target_pairs={{0,0},{1,5},{2,2},{3,7},{4,36},{5,9},{6,38},{7,11},{8,40},{9,13},{... | collective-permute-start | bytes 2359304 | tf_op jit(solution)/shard_map/ppermute | solution.py:159
  8.3 14.5 %collective-permute-done.3 = bf16[384,1024]{1,0:T(8,128)(2,1)} collective-permute-done((bf16[384,1024]{1,0:T(8,128)(2,1)S(1)}, bf16[384,1024]{1,0:T(8,128)(2,1)}, u32[]{:S(2)}, u32[]{:S(2)}) %collective-permute-start.3) | collective-permute-done | bytes 786464 | tf_op jit(solution)/shard_map/ppermute | solution.py:159
  22.8 1.7 collective-permute-start.4
  24.6 2.2 %collective-permute-start.1 = (bf16[384,1024]{1,0:T(8,128)(2,1)}, bf16[384,1024]{1,0:T(8,128)(2,1)}, u32[]{:S(2)}, u32[]{:S(2)}) collective-permute-start(bf16[384,1024]{1,0:T(8,128)(2,1)} %collective-permute-done), channel_id=1, source_target_pairs={{0,29},{1,4},{2,31},{3,6},{4,1},{5,8},{6,3},{7,10},{8,5},{9,12},{1... | collective-permute-start | bytes 2359304 | tf_op jit(solution)/shard_map/ppermute | solution.py:159
  27.6 1.3 maximum_bitcast_fusion
  28.9 1.0 broadcast_select_fusion.xb.refs_1_
  29.9 4.7 %collective-permute-done.4.xb.refs_3_ = bf16[384,1024]{1,0:T(8,128)(2,1)} collective-permute-done((bf16[384,1024]{1,0:T(8,128)(2,1)}, bf16[384,1024]{1,0:T(8,128)(2,1)}, u32[]{:S(2)}, u32[]{:S(2)}) %collective-permute-start.4) | collective-permute-done | bytes 786464 | tf_op jit(solution)/shard_map/ppermute | solution.py:159
  34.6 2.1 %collective-permute-start.5 = (bf16[384,1024]{1,0:T(8,128)(2,1)}, bf16[384,1024]{1,0:T(8,128)(2,1)}, u32[]{:S(2)}, u32[]{:S(2)}) collective-permute-start(bf16[384,1024]{1,0:T(8,128)(2,1)} %collective-permute-done.4.xb.refs_3_), channel_id=1, source_target_pairs={{0,5},{1,254},{2,7},{3,252},{4,9},{5,0},{6,11},{7,2},{8,13},{9,4},... | collective-permute-start | bytes 2359304 | tf_op jit(solution)/shard_map/ppermute | solution.py:159
  36.7 10.8 %collective-permute-done.1.xa.refs_2_ = bf16[384,1024]{1,0:T(8,128)(2,1)} collective-permute-done((bf16[384,1024]{1,0:T(8,128)(2,1)}, bf16[384,1024]{1,0:T(8,128)(2,1)}, u32[]{:S(2)}, u32[]{:S(2)}) %collective-permute-start.1) | collective-permute-done | bytes 786464 | tf_op jit(solution)/shard_map/ppermute | solution.py:159
  47.5 1.9 %collective-permute-start.2 = (bf16[384,1024]{1,0:T(8,128)(2,1)}, bf16[384,1024]{1,0:T(8,128)(2,1)}, u32[]{:S(2)}, u32[]{:S(2)}) collective-permute-start(bf16[384,1024]{1,0:T(8,128)(2,1)} %collective-permute-done.1.xa.refs_2_), channel_id=1, source_target_pairs={{0,5},{1,254},{2,7},{3,252},{4,9},{5,0},{6,11},{7,2},{8,13},{9,4},... | collective-permute-start | bytes 2359304 | tf_op jit(solution)/shard_map/ppermute | solution.py:159
  49.4 1.0 broadcast_select_fusion.1.xa.refs_0_
  51.2 5.4 %amp.5 = (f32[384,384]{1,0:T(8,128)}, bf16[384,384]{1,0:T(8,128)(2,1)}) custom-call(s32[8]{0:T(128)} %stack.49.sc, bf16[768,2048]{1,0:T(8,128)(2,1)} %bitcast.20, bf16[384,1024]{1,0:T(8,128)(2,1)} %broadcast_select_fusion.1.xa.refs_0_, bf16[384,1024]{1,0:T(8,128)(2,1)} %broadcast_select_fusion.xb.refs_1_, f32[384,128]{1,0:T(8,128)} %broadcast_in_dim.41.evc, ...), custom_call_target="tpu_custom_call" | custom-call | flops 1207959552 | bytes 4718592 | tf_op jit(solution)/shard_map/amp/pallas_call | solution.py:175
  56.6 1.8 %collective-permute-start.8 = (f32[384,384]{1,0:T(8,128)}, f32[384,384]{1,0:T(8,128)}, u32[]{:S(2)}, u32[]{:S(2)}) collective-permute-start(f32[384,384]{1,0:T(8,128)} %get-tuple-element.34.refs_4_), channel_id=1, source_target_pairs={{0,2},{1,3},{2,0},{3,1},{4,6},{5,7},{6,4},{7,5},{8,10},{9,11},{10,... | collective-permute-start | bytes 1769480 | tf_op jit(solution)/shard_map/ppermute | solution.py:162
  58.4 5.5 %amp.6 = (f32[384,384]{1,0:T(8,128)}, bf16[384,384]{1,0:T(8,128)(2,1)}) custom-call(s32[8]{0:T(128)} %stack.49.sc, bf16[768,2048]{1,0:T(8,128)(2,1)} %bitcast.21, bf16[384,1024]{1,0:T(8,128)(2,1)} %collective-permute-done.1.xa.refs_2_, bf16[384,1024]{1,0:T(8,128)(2,1)} %collective-permute-done.4.xb.refs_3_, f32[384,128]{1,0:T(8,128)} %broadcast_in_dim.41.evc, ...), custom_call_target="tpu_custom_call" | custom-call | flops 1207959552 | bytes 4718592 | tf_op jit(solution)/shard_map/amp/pallas_call | solution.py:175
  64.1 3.4 %maximum_select_fusion = bf16[2,768,1024]{2,1,0:T(8,128)(2,1)S(1)} fusion(bf16[1,768,1024]{2,1,0:T(8,128)(2,1)} %maximum_bitcast_fusion, bf16[1,768,1024]{2,1,0:T(8,128)(2,1)} %bitcast.24, pred[]{:T(512)S(6)} %eq.44), kind=kLoop, calls=%fused_computation | loop fusion | flops 4718592 | bytes 6291457 | tf_op jit(solution)/shard_map/jit(_where)/select_n | solution.py:227
  67.5 6.0 %collective-permute-start.7 = (bf16[384,1024]{1,0:T(8,128)(2,1)}, bf16[384,1024]{1,0:T(8,128)(2,1)}, u32[]{:S(2)}, u32[]{:S(2)}) collective-permute-start(bf16[384,1024]{1,0:T(8,128)(2,1)} %collective-permute-done.5.xb.refs_1_), channel_id=1, source_target_pairs={{0,255},{1,4},{2,253},{3,6},{4,1},{5,8},{6,3},{7,10},{8,5},{9,12},... | collective-permute-start | bytes 2359304 | tf_op jit(solution)/shard_map/ppermute | solution.py:159
  73.6 5.5 %amp.4 = (f32[384,384]{1,0:T(8,128)}, bf16[384,384]{1,0:T(8,128)(2,1)}) custom-call(s32[8]{0:T(128)} %stack.49.sc, bf16[768,2048]{1,0:T(8,128)(2,1)} %bitcast.22, bf16[384,1024]{1,0:T(8,128)(2,1)} %collective-permute-done.2.xa.refs_0_, bf16[384,1024]{1,0:T(8,128)(2,1)} %collective-permute-done.5.xb.refs_1_, f32[384,128]{1,0:T(8,128)} %broadcast_in_dim.41.evc, ...), custom_call_target="tpu_custom_call" | custom-call | flops 1207959552 | bytes 4718592 | tf_op jit(solution)/shard_map/amp/pallas_call | solution.py:175
  79.1 1.5 collective-permute-start.11
  80.6 5.1 %collective-permute-done.9.refs_8_ = f32[384,384]{1,0:T(8,128)} collective-permute-done((f32[384,384]{1,0:T(8,128)}, f32[384,384]{1,0:T(8,128)}, u32[]{:S(2)}, u32[]{:S(2)}) %collective-permute-start.9) | collective-permute-done | bytes 589856 | tf_op jit(solution)/shard_map/ppermute | solution.py:162
  85.7 8.8 %gamma.1 = (f32[2048,384]{1,0:T(8,128)}, f32[2048,384]{1,0:T(8,128)}) custom-call(s32[8]{0:T(128)} %stack.49.sc, bf16[384,1024]{1,0:T(8,128)(2,1)} %broadcast_select_fusion.1.xa.refs_0_, bf16[384,1024]{1,0:T(8,128)(2,1)} %broadcast_select_fusion.xb.refs_1_, bf16[384,1024]{1,0:T(8,128)(2,1)} %collective-permute-done.1.xa.refs_2_, ...), custom_call_target="tpu_custom_call" | custom-call | flops 2415919104 | bytes 9437184 | tf_op jit(solution)/shard_map/gamma/pallas_call | solution.py:207
  94.6 5.4 %amp.7 = (bf16[384,384]{1,0:T(8,128)(2,1)}, bf16[384,384]{1,0:T(8,128)(2,1)}) custom-call(s32[8]{0:T(128)} %stack.49.sc, bf16[768,2048]{1,0:T(8,128)(2,1)} %bitcast.23, bf16[384,1024]{1,0:T(8,128)(2,1)} %collective-permute-done.6.xa.refs_2_, bf16[384,1024]{1,0:T(8,128)(2,1)} %collective-permute-done.7.xb.refs_3_, f32[384,128]{1,0:T(8,128)} %broadcast_in_dim.41.evc, ...), custom_call_target="tpu_custom_call" | custom-call | flops 1207959552 | bytes 4718592 | tf_op jit(solution)/shard_map/amp/pallas_call | solution.py:175
  99.9 1.9 %collective-permute-start.12 = (bf16[384,384]{1,0:T(8,128)(2,1)}, bf16[384,384]{1,0:T(8,128)(2,1)S(1)}, u32[]{:S(2)}, u32[]{:S(2)}) collective-permute-start(bf16[384,384]{1,0:T(8,128)(2,1)} %get-tuple-element.46.refs_6_), channel_id=1, source_target_pairs={{0,2},{1,3},{2,0},{3,1},{4,6},{5,7},{6,4},{7,5},{8,10},{9,11},{10,... | collective-permute-start | bytes 884744 | tf_op jit(solution)/shard_map/ppermute | solution.py:162
  101.8 6.5 %last.2 = (f32[64,8,384]{2,1,0:T(8,128)}, f32[64,8,384]{2,1,0:T(8,128)}, f32[64,8,384]{2,1,0:T(8,128)}, f32[64,8,384]{2,1,0:T(8,128)}) custom-call(s32[8]{0:T(128)} %stack.49.sc, bf16[384,1024]{1,0:T(8,128)(2,1)} %collective-permute-done.2.xa.refs_0_, bf16[384,1024]{1,0:T(8,128)(2,1)} %collective-permute-done.5.xb.refs_1_, ...), custom_call_target="tpu_custom_call" | custom-call | flops 1207959552 | bytes 6291456 | tf_op jit(solution)/shard_map/last/pallas_call | solution.py:245
  110.0 7.2 %last.3 = (f32[64,8,384]{2,1,0:T(8,128)}, f32[64,8,384]{2,1,0:T(8,128)}, f32[64,8,384]{2,1,0:T(8,128)}, f32[64,8,384]{2,1,0:T(8,128)}) custom-call(s32[8]{0:T(128)} %stack.49.sc, bf16[384,1024]{1,0:T(8,128)(2,1)} %collective-permute-done.2.xa.refs_0_, bf16[384,1024]{1,0:T(8,128)(2,1)} %collective-permute-done.5.xb.refs_1_, ...), custom_call_target="tpu_custom_call" | custom-call | flops 1207959552 | bytes 6291456 | tf_op jit(solution)/shard_map/last/pallas_call | solution.py:245
  117.9 1.5 add_convert_fusion.1
  119.4 1.8 %collective-permute-start.17 = (bf16[64,8,384]{2,1,0:T(8,128)(2,1)S(1)}, bf16[64,8,384]{2,1,0:T(8,128)(2,1)S(1)}, u32[]{:S(2)}, u32[]{:S(2)}) collective-permute-start(bf16[64,8,384]{2,1,0:T(8,128)(2,1)S(1)} %add_convert_fusion.1), channel_id=1, source_target_pairs={{0,2},{1,3},{2,0},{3,1},{4,6},{5,7},{6,4},{7,5},{8,10},{9,11},{10,... | collective-permute-start | bytes 1179656 | tf_op jit(solution)/shard_map/ppermute | solution.py:263
  121.2 1.2 add_convert_fusion.3
  122.8 8.7 %collective-permute-done.17 = bf16[64,8,384]{2,1,0:T(8,128)(2,1)S(1)} collective-permute-done((bf16[64,8,384]{2,1,0:T(8,128)(2,1)S(1)}, bf16[64,8,384]{2,1,0:T(8,128)(2,1)S(1)}, u32[]{:S(2)}, u32[]{:S(2)}) %collective-permute-start.17) | collective-permute-done | bytes 393248 | tf_op jit(solution)/shard_map/ppermute | solution.py:263
  131.6 7.8 %collective-permute-done.14 = bf16[64,8,384]{2,1,0:T(8,128)(2,1)S(1)} collective-permute-done((bf16[64,8,384]{2,1,0:T(8,128)(2,1)S(1)}, bf16[64,8,384]{2,1,0:T(8,128)(2,1)S(1)}, u32[]{:S(2)}, u32[]{:S(2)}) %collective-permute-start.14) | collective-permute-done | bytes 393248 | tf_op jit(solution)/shard_map/ppermute | solution.py:263
  139.5 38.3 %all_to_all.5 = bf16[64,8,768]{2,1,0:T(8,128)(2,1)S(1)} all-to-all(bf16[64,8,768]{2,1,0:T(8,128)(2,1)S(1)} %pad_maximum_fusion), channel_id=1, replica_groups=mesh['occ'=64,'off'=4] {'occ'}, dimensions={0} | all-to-all | bytes 1572864 | tf_op jit(solution)/shard_map/all_to_all | solution.py:275
  177.8 2.3 %fusion.1 = f32[2,256,1024]{2,1,0:T(8,128)} fusion(bf16[2,256,768]{2,1,0:T(8,128)(2,1)S(1)} %bitcast.25, bf16[2,768,1024]{2,1,0:T(8,128)(2,1)S(1)} %maximum_select_fusion), kind=kOutput, calls=%fused_computation.16 | convolution fusion | flops 805306368 | bytes 6029312 | tf_op jit(solution)/shard_map/zsd,zdw->zsw/dot_general | solution.py:277
  (46 shorter events, 7.3 us)
Async XLA Ops:
  0.0 6.7 %copy-start.5 = (f32[256]{0:T(256)S(1)}, f32[256]{0:T(256)}, u32[]{:S(2)}) copy-start(f32[256]{0:T(256)} %param.10) | copy-start | bytes 3076
  0.0 6.7 %copy-start.4 = (s32[768]{0:T(1024)S(1)}, s32[768]{0:T(1024)}, u32[]{:S(2)}) copy-start(s32[768]{0:T(1024)} %param.8) | copy-start | bytes 9220
  0.0 26.8 %copy-start.6 = (f32[256]{0:T(256)S(1)}, f32[256]{0:T(256)}, u32[]{:S(2)}) copy-start(f32[256]{0:T(256)} %param.9) | copy-start | bytes 3076
  0.0 26.8 %copy-start.7 = (s32[64]{0:T(128)S(1)}, s32[64]{0:T(128)}, u32[]{:S(2)}) copy-start(s32[64]{0:T(128)} %param.7) | copy-start | bytes 772
  0.0 27.5 %copy-start = (bf16[768,1024]{1,0:T(8,128)(2,1)S(1)}, bf16[768,1024]{1,0:T(8,128)(2,1)}, u32[]{:S(2)}) copy-start(bf16[768,1024]{1,0:T(8,128)(2,1)} %param.11) | copy-start | bytes 4718596
  1.7 21.1 %collective-permute-start.3 = (bf16[384,1024]{1,0:T(8,128)(2,1)S(1)}, bf16[384,1024]{1,0:T(8,128)(2,1)}, u32[]{:S(2)}, u32[]{:S(2)}) collective-permute-start(bf16[384,1024]{1,0:T(8,128)(2,1)S(1)} %get-tuple-element.57), channel_id=1, source_target_pairs={{0,0},{1,5},{2,2},{3,7},{4,36},{5,9},{6,38},{7,11},{8,40},{9,13},{... | collective-permute-start | bytes 2359304 | tf_op jit(solution)/shard_map/ppermute | solution.py:159
  6.0 18.6 %collective-permute-start = (bf16[384,1024]{1,0:T(8,128)(2,1)S(1)}, bf16[384,1024]{1,0:T(8,128)(2,1)}, u32[]{:S(2)}, u32[]{:S(2)}) collective-permute-start(bf16[384,1024]{1,0:T(8,128)(2,1)S(1)} %get-tuple-element.58), channel_id=1, source_target_pairs={{0,5},{1,0},{2,7},{3,2},{4,9},{5,36},{6,11},{7,38},{8,13},{9,40},{... | collective-permute-start | bytes 2359304 | tf_op jit(solution)/shard_map/ppermute | solution.py:159
  22.8 11.7 %collective-permute-start.4 = (bf16[384,1024]{1,0:T(8,128)(2,1)}, bf16[384,1024]{1,0:T(8,128)(2,1)}, u32[]{:S(2)}, u32[]{:S(2)}) collective-permute-start(bf16[384,1024]{1,0:T(8,128)(2,1)} %collective-permute-done.3), channel_id=1, source_target_pairs={{0,29},{1,4},{2,31},{3,6},{4,1},{5,8},{6,3},{7,10},{8,5},{9,12},{1... | collective-permute-start | bytes 2359304 | tf_op jit(solution)/shard_map/ppermute | solution.py:159
  24.6 22.9 %collective-permute-start.1 = (bf16[384,1024]{1,0:T(8,128)(2,1)}, bf16[384,1024]{1,0:T(8,128)(2,1)}, u32[]{:S(2)}, u32[]{:S(2)}) collective-permute-start(bf16[384,1024]{1,0:T(8,128)(2,1)} %collective-permute-done), channel_id=1, source_target_pairs={{0,29},{1,4},{2,31},{3,6},{4,1},{5,8},{6,3},{7,10},{8,5},{9,12},{1... | collective-permute-start | bytes 2359304 | tf_op jit(solution)/shard_map/ppermute | solution.py:159
  34.6 32.9 %collective-permute-start.5 = (bf16[384,1024]{1,0:T(8,128)(2,1)}, bf16[384,1024]{1,0:T(8,128)(2,1)}, u32[]{:S(2)}, u32[]{:S(2)}) collective-permute-start(bf16[384,1024]{1,0:T(8,128)(2,1)} %collective-permute-done.4.xb.refs_3_), channel_id=1, source_target_pairs={{0,5},{1,254},{2,7},{3,252},{4,9},{5,0},{6,11},{7,2},{8,13},{9,4},... | collective-permute-start | bytes 2359304 | tf_op jit(solution)/shard_map/ppermute | solution.py:159
  47.5 26.0 %collective-permute-start.2 = (bf16[384,1024]{1,0:T(8,128)(2,1)}, bf16[384,1024]{1,0:T(8,128)(2,1)}, u32[]{:S(2)}, u32[]{:S(2)}) collective-permute-start(bf16[384,1024]{1,0:T(8,128)(2,1)} %collective-permute-done.1.xa.refs_2_), channel_id=1, source_target_pairs={{0,5},{1,254},{2,7},{3,252},{4,9},{5,0},{6,11},{7,2},{8,13},{9,4},... | collective-permute-start | bytes 2359304 | tf_op jit(solution)/shard_map/ppermute | solution.py:159
  56.6 24.0 %collective-permute-start.8 = (f32[384,384]{1,0:T(8,128)}, f32[384,384]{1,0:T(8,128)}, u32[]{:S(2)}, u32[]{:S(2)}) collective-permute-start(f32[384,384]{1,0:T(8,128)} %get-tuple-element.34.refs_4_), channel_id=1, source_target_pairs={{0,2},{1,3},{2,0},{3,1},{4,6},{5,7},{6,4},{7,5},{8,10},{9,11},{10,... | collective-permute-start | bytes 1769480 | tf_op jit(solution)/shard_map/ppermute | solution.py:162
  63.9 21.8 %collective-permute-start.9 = (f32[384,384]{1,0:T(8,128)}, f32[384,384]{1,0:T(8,128)}, u32[]{:S(2)}, u32[]{:S(2)}) collective-permute-start(f32[384,384]{1,0:T(8,128)} %get-tuple-element.36.refs_7_), channel_id=1, source_target_pairs={{0,2},{1,3},{2,0},{3,1},{4,6},{5,7},{6,4},{7,5},{8,10},{9,11},{10,... | collective-permute-start | bytes 1769480 | tf_op jit(solution)/shard_map/ppermute | solution.py:162
  67.5 27.1 %collective-permute-start.7 = (bf16[384,1024]{1,0:T(8,128)(2,1)}, bf16[384,1024]{1,0:T(8,128)(2,1)}, u32[]{:S(2)}, u32[]{:S(2)}) collective-permute-start(bf16[384,1024]{1,0:T(8,128)(2,1)} %collective-permute-done.5.xb.refs_1_), channel_id=1, source_target_pairs={{0,255},{1,4},{2,253},{3,6},{4,1},{5,8},{6,3},{7,10},{8,5},{9,12},... | collective-permute-start | bytes 2359304 | tf_op jit(solution)/shard_map/ppermute | solution.py:159
  73.5 21.1 %collective-permute-start.6 = (bf16[384,1024]{1,0:T(8,128)(2,1)}, bf16[384,1024]{1,0:T(8,128)(2,1)}, u32[]{:S(2)}, u32[]{:S(2)}) collective-permute-start(bf16[384,1024]{1,0:T(8,128)(2,1)} %collective-permute-done.2.xa.refs_0_), channel_id=1, source_target_pairs={{0,255},{1,4},{2,253},{3,6},{4,1},{5,8},{6,3},{7,10},{8,5},{9,12},... | collective-permute-start | bytes 2359304 | tf_op jit(solution)/shard_map/ppermute | solution.py:159
  79.1 29.3 %collective-permute-start.11 = (f32[384,384]{1,0:T(8,128)}, f32[384,384]{1,0:T(8,128)}, u32[]{:S(2)}, u32[]{:S(2)}) collective-permute-start(f32[384,384]{1,0:T(8,128)} %get-tuple-element.32.refs_4_), channel_id=1, source_target_pairs={{0,2},{1,3},{2,0},{3,1},{4,6},{5,7},{6,4},{7,5},{8,10},{9,11},{10,... | collective-permute-start | bytes 1769480 | tf_op jit(solution)/shard_map/ppermute | solution.py:162
  99.9 9.3 %collective-permute-start.12 = (bf16[384,384]{1,0:T(8,128)(2,1)}, bf16[384,384]{1,0:T(8,128)(2,1)S(1)}, u32[]{:S(2)}, u32[]{:S(2)}) collective-permute-start(bf16[384,384]{1,0:T(8,128)(2,1)} %get-tuple-element.46.refs_6_), channel_id=1, source_target_pairs={{0,2},{1,3},{2,0},{3,1},{4,6},{5,7},{6,4},{7,5},{8,10},{9,11},{10,... | collective-permute-start | bytes 884744 | tf_op jit(solution)/shard_map/ppermute | solution.py:162
  108.3 9.5 %collective-permute-start.16 = (f32[64,8,384]{2,1,0:T(8,128)}, f32[64,8,384]{2,1,0:T(8,128)}, u32[]{:S(2)}, u32[]{:S(2)}) collective-permute-start(f32[64,8,384]{2,1,0:T(8,128)} %get-tuple-element.55), channel_id=1, source_target_pairs={{0,1},{1,0},{2,3},{3,2},{4,5},{5,4},{6,7},{7,6},{8,9},{9,8},{10,11... | collective-permute-start | bytes 2359304 | tf_op jit(solution)/shard_map/ppermute | solution.py:260
  109.3 0.7 copy-start.3
  117.2 14.3 %copy-start.2 = (f32[64,8,384]{2,1,0:T(8,128)S(1)}, f32[64,8,384]{2,1,0:T(8,128)}, u32[]{:S(2)}) copy-start(f32[64,8,384]{2,1,0:T(8,128)} %get-tuple-element.52) | copy-start | bytes 2359300
  117.2 4.1 %collective-permute-start.13 = (f32[64,8,384]{2,1,0:T(8,128)}, f32[64,8,384]{2,1,0:T(8,128)S(1)}, u32[]{:S(2)}, u32[]{:S(2)}) collective-permute-start(f32[64,8,384]{2,1,0:T(8,128)} %get-tuple-element.51), channel_id=1, source_target_pairs={{0,1},{1,0},{2,3},{3,2},{4,5},{5,4},{6,7},{7,6},{8,9},{9,8},{10,11... | collective-permute-start | bytes 2359304 | tf_op jit(solution)/shard_map/ppermute | solution.py:260
  117.3 5.5 %collective-permute-start.15 = (f32[64,8,384]{2,1,0:T(8,128)}, f32[64,8,384]{2,1,0:T(8,128)S(1)}, u32[]{:S(2)}, u32[]{:S(2)}) collective-permute-start(f32[64,8,384]{2,1,0:T(8,128)} %get-tuple-element.53), channel_id=1, source_target_pairs={{0,1},{1,0},{2,3},{3,2},{4,5},{5,4},{6,7},{7,6},{8,9},{9,8},{10,11... | collective-permute-start | bytes 2359304 | tf_op jit(solution)/shard_map/ppermute | solution.py:260
  117.8 13.8 %collective-permute-start.10 = (f32[64,8,384]{2,1,0:T(8,128)}, f32[64,8,384]{2,1,0:T(8,128)S(1)}, u32[]{:S(2)}, u32[]{:S(2)}) collective-permute-start(f32[64,8,384]{2,1,0:T(8,128)} %get-tuple-element.45), channel_id=1, source_target_pairs={{0,1},{1,0},{2,3},{3,2},{4,5},{5,4},{6,7},{7,6},{8,9},{9,8},{10,11... | collective-permute-start | bytes 2359304 | tf_op jit(solution)/shard_map/ppermute | solution.py:260
  117.9 21.5 %copy-start.1 = (f32[64,8,384]{2,1,0:T(8,128)S(1)}, f32[64,8,384]{2,1,0:T(8,128)}, u32[]{:S(2)}) copy-start(f32[64,8,384]{2,1,0:T(8,128)} %get-tuple-element.44) | copy-start | bytes 2359300
  119.4 12.1 %collective-permute-start.17 = (bf16[64,8,384]{2,1,0:T(8,128)(2,1)S(1)}, bf16[64,8,384]{2,1,0:T(8,128)(2,1)S(1)}, u32[]{:S(2)}, u32[]{:S(2)}) collective-permute-start(bf16[64,8,384]{2,1,0:T(8,128)(2,1)S(1)} %add_convert_fusion.1), channel_id=1, source_target_pairs={{0,2},{1,3},{2,0},{3,1},{4,6},{5,7},{6,4},{7,5},{8,10},{9,11},{10,... | collective-permute-start | bytes 1179656 | tf_op jit(solution)/shard_map/ppermute | solution.py:263
  122.4 16.9 %collective-permute-start.14 = (bf16[64,8,384]{2,1,0:T(8,128)(2,1)S(1)}, bf16[64,8,384]{2,1,0:T(8,128)(2,1)S(1)}, u32[]{:S(2)}, u32[]{:S(2)}) collective-permute-start(bf16[64,8,384]{2,1,0:T(8,128)(2,1)S(1)} %add_convert_fusion.3), channel_id=1, source_target_pairs={{0,2},{1,3},{2,0},{3,1},{4,6},{5,7},{6,4},{7,5},{8,10},{9,11},{10,... | collective-permute-start | bytes 1179656 | tf_op jit(solution)/shard_map/ppermute | solution.py:263
